TPU v7x, 32 devices: a whole 2x2x4 slice. The times are simulated.
32 devices in a mesh: nodes: 32 (over z, y, x, core).
Axes of the slice: x: 2, y: 2, z: 4, core: 2. Of those that a mesh axis runs over, the one named last changes fastest.
Arguments:
- features: bfloat16 [131072, 602], P('nodes'), may hold values from -6 to 6
- labels: int32 [131072, 121], P('nodes'), may hold values 0 or 1
- labelled: int32 [131072], P('nodes'), may hold values 0 or 1
- label_count: int32 [1], replicated, may hold values from 65536 to 131072
- need_blocks: int32 [32, 32, 2], P('nodes'), may hold values from 0 to 31
- need_count: int32 [32, 32], P('nodes'), may hold values from 1 to 2
- target_block: int32 [32, 32, 2], P('nodes'), may hold values from 0 to 31
- adjacency: bfloat16 [2048, 128, 128], P('nodes'), may hold values from 0 to 0.14355469
- embed_weight: float32 [602, 512], replicated, may hold values from -0.25 to 0.25
- pair_weight: float32 [1, 2, 512, 512], replicated, may hold values from -0.25 to 0.25
- merge_weight: float32 [1, 1024, 512], replicated, may hold values from -0.1875 to 0.1875
- head_weight: float32 [512, 121], replicated, may hold values from -0.25 to 0.25
- embed_moment: float32 [602, 512], replicated, may hold values from -2.9802322e-07 to 2.9802322e-07
- pair_moment: float32 [1, 2, 512, 512], replicated, may hold values from -2.9802322e-07 to 2.9802322e-07
- merge_moment: float32 [1, 1024, 512], replicated, may hold values from -2.9802322e-07 to 2.9802322e-07
- head_moment: float32 [512, 121], replicated, may hold values from -8.34465e-07 to 8.34465e-07
- embed_variance: float32 [602, 512], replicated, may hold values from 2.8863303e-17 to 1.1785848e-16
- pair_variance: float32 [1, 2, 512, 512], replicated, may hold values from 2.8863303e-17 to 1.1785848e-16
- merge_variance: float32 [1, 1024, 512], replicated, may hold values from 2.8863303e-17 to 1.1785848e-16
- head_variance: float32 [512, 121], replicated, may hold values from 2.5444234e-16 to 1.0177694e-15
Outputs:
- loss_value: float32 [1], replicated
- embed_updated: float32 [602, 512], replicated
- pair_updated: float32 [1, 2, 512, 512], replicated
- merge_updated: float32 [1, 1024, 512], replicated
- head_updated: float32 [512, 121], replicated
- embed_momentum: float32 [602, 512], replicated
- pair_momentum: float32 [1, 2, 512, 512], replicated
- merge_momentum: float32 [1, 1024, 512], replicated
- head_momentum: float32 [512, 121], replicated
- embed_squares: float32 [602, 512], replicated
- pair_squares: float32 [1, 2, 512, 512], replicated
- merge_squares: float32 [1, 1024, 512], replicated
- head_squares: float32 [512, 121], replicated
Inputs may be any that keep to these rules, and one draw needn't show every extreme that they name: `need_blocks`: block indices within an owner's blocks. `need_count`: live slots per device pair. `target_block`: block indices within the taking device's blocks.
All inputs are finite; a program needn't handle non-finite values. No bound on the sum of `labels` or of `labelled` on one device may be relied on, other than what follows from the above.
Results may differ from a plain program's by a relative error of at most 0.008.
Values may be sent and summed in bfloat16 or wider, within the bound.
A program may use at most 448 MiB of HBM per device.

v0:
```python
import jax
import jax.numpy as jnp
from jax import lax
from jax.sharding import PartitionSpec as P

norm_eps = 1e-06
learn_rate = 0.03
beta_one = 0.9
beta_two = 0.999
adam_eps = 1e-08
decay_rate = 0.01
adam_step = 10.0


def to_half(value):
    return value.astype(jnp.bfloat16)


def mat_product(former, latter):
    return jnp.dot(former, latter, preferred_element_type=jnp.float32)


def left_product(former, latter):
    return lax.dot_general(
        former, latter, (((0,), (0,)), ((), ())), preferred_element_type=jnp.float32
    )


def right_product(former, latter):
    return lax.dot_general(
        former, latter, (((1,), (1,)), ((), ())), preferred_element_type=jnp.float32
    )


def adam_update(weight, grad, first, second):
    first_new = beta_one * first + (1.0 - beta_one) * grad
    second_new = beta_two * second + (1.0 - beta_two) * grad * grad
    first_hat = first_new / (1.0 - beta_one**adam_step)
    second_hat = second_new / (1.0 - beta_two**adam_step)
    weight_new = weight - learn_rate * (
        first_hat / (jnp.sqrt(second_hat) + adam_eps) + decay_rate * weight
    )
    return (weight_new, first_new, second_new)


def shards(
    features,
    labels,
    labelled,
    label_count,
    need_blocks,
    need_count,
    target_block,
    adjacency,
    embed_weight,
    pair_weight,
    merge_weight,
    head_weight,
    embed_moment,
    pair_moment,
    merge_moment,
    head_moment,
    embed_variance,
    pair_variance,
    merge_variance,
    head_variance,
):
    row_count = features.shape[0]
    hidden_width = embed_weight.shape[1]
    block_rows = adjacency.shape[1]
    slot_width = need_blocks.shape[2]
    device_count = lax.axis_size("nodes")
    block_count = row_count // block_rows
    layer_count = pair_weight.shape[0]
    slot_total = device_count * slot_width
    wanted = need_blocks[0]
    live_slots = lax.broadcasted_iota(jnp.int32, wanted.shape, 1) < need_count[0][:, None]
    live_weights = jnp.where(
        live_slots.reshape(-1)[:, None, None], adjacency, jnp.zeros_like(adjacency)
    )
    sinks = target_block[0].reshape(-1)
    asked_grid = lax.all_to_all(wanted, "nodes", split_axis=0, concat_axis=0, tiled=True)
    asked = asked_grid.reshape(-1)
    pair_half = to_half(pair_weight)
    merge_half = to_half(merge_weight)
    head_half = to_half(head_weight)
    hidden = mat_product(features, to_half(embed_weight))
    layer = 0
    hidden_half = to_half(hidden)
    outgoing = hidden_half.reshape(block_count, block_rows, hidden_width)[asked]
    outgoing = outgoing.reshape(device_count, slot_width, block_rows, hidden_width)
    arrived = lax.all_to_all(outgoing, "nodes", split_axis=0, concat_axis=0, tiled=True)
    received = arrived.reshape(slot_total, block_rows, hidden_width)
    products = jnp.einsum(
        "kab,kbh->kah", live_weights, received, preferred_element_type=jnp.float32
    )
    gathered = to_half(
        jax.ops.segment_sum(products, sinks, num_segments=block_count).reshape(
            row_count, hidden_width
        )
    )
    self_part = mat_product(hidden_half, pair_half[layer, 0])
    neigh_part = mat_product(gathered, pair_half[layer, 1])
    joined = to_half(jnp.concatenate([self_part, neigh_part], axis=1))
    linear = mat_product(joined, merge_half[layer])
    active = linear * jax.nn.sigmoid(linear)
    scale = lax.rsqrt(jnp.sum(active * active, axis=1, keepdims=True) + norm_eps)
    hidden = active * scale
    kept = (hidden_half, gathered, joined, linear, scale)
    kept_layers = [kept]
    layer_outputs = [hidden]
    final_half = to_half(hidden)
    logits = mat_product(final_half, head_half)
    truth = labels.astype(jnp.float32)
    row_mask = labelled.astype(jnp.float32)[:, None]
    denom = label_count[0].astype(jnp.float32) * logits.shape[1]
    per_entry = jnp.maximum(logits, 0.0) - logits * truth + jnp.log1p(jnp.exp(-jnp.abs(logits)))
    loss_part = jnp.sum(per_entry * row_mask) / denom
    grad_logits = to_half((jax.nn.sigmoid(logits) - truth) * row_mask / denom)
    head_grad = left_product(final_half, grad_logits)
    grad_hidden = right_product(grad_logits, head_half)
    pair_grads = [None] * layer_count
    merge_grads = [None] * layer_count
    for layer in reversed(range(layer_count)):
        grad_out = grad_hidden
        output = layer_outputs[layer]
        layer_kept = kept_layers[layer]
        layer_hidden_half, layer_gathered, layer_joined, layer_linear, layer_scale = layer_kept
        grad_active = layer_scale * (
            grad_out - output * jnp.sum(grad_out * output, axis=1, keepdims=True)
        )
        sig_value = jax.nn.sigmoid(layer_linear)
        grad_linear = to_half(grad_active * sig_value * (1.0 + layer_linear * (1.0 - sig_value)))
        grad_merge = left_product(layer_joined, grad_linear)
        grad_joined = to_half(right_product(grad_linear, merge_half[layer]))
        grad_self_out = grad_joined[:, :hidden_width]
        grad_neigh_out = grad_joined[:, hidden_width:]
        grad_self = left_product(layer_hidden_half, grad_self_out)
        grad_neigh = left_product(layer_gathered, grad_neigh_out)
        layer_grad_gathered = to_half(right_product(grad_neigh_out, pair_half[layer, 1]))
        grad_blocks = layer_grad_gathered.reshape(block_count, block_rows, hidden_width)[sinks]
        grad_received = to_half(
            jnp.einsum(
                "kab,kah->kbh", live_weights, grad_blocks, preferred_element_type=jnp.float32
            )
        )
        return_outgoing = grad_received.reshape(device_count, slot_width, block_rows, hidden_width)
        return_arrived = lax.all_to_all(
            return_outgoing, "nodes", split_axis=0, concat_axis=0, tiled=True
        )
        flat_grads = return_arrived.reshape(slot_total, block_rows * hidden_width).astype(
            jnp.float32
        )
        summed = jax.ops.segment_sum(flat_grads, asked, num_segments=block_count)
        layer_grad_hidden = right_product(grad_self_out, pair_half[layer, 0]) + summed.reshape(
            row_count, hidden_width
        )
        grad_hidden, pair_grads[layer], merge_grads[layer] = (
            layer_grad_hidden,
            jnp.stack([grad_self, grad_neigh]),
            grad_merge,
        )
    pair_grad = jnp.stack(pair_grads)
    merge_grad = jnp.stack(merge_grads)
    embed_grad = left_product(features, to_half(grad_hidden))
    loss_total, embed_grad, pair_grad, merge_grad, head_grad = lax.psum(
        (loss_part, embed_grad, pair_grad, merge_grad, head_grad), "nodes"
    )
    embed_next = adam_update(embed_weight, embed_grad, embed_moment, embed_variance)
    pair_next = adam_update(pair_weight, pair_grad, pair_moment, pair_variance)
    merge_next = adam_update(merge_weight, merge_grad, merge_moment, merge_variance)
    head_next = adam_update(head_weight, head_grad, head_moment, head_variance)
    return (
        loss_total.reshape(1),
        embed_next[0],
        pair_next[0],
        merge_next[0],
        head_next[0],
        embed_next[1],
        pair_next[1],
        merge_next[1],
        head_next[1],
        embed_next[2],
        pair_next[2],
        merge_next[2],
        head_next[2],
    )


def solution(mesh):
    return jax.shard_map(
        shards,
        mesh=mesh,
        in_specs=(
            P("nodes", None),
            P("nodes", None),
            P("nodes"),
            P(),
            P("nodes", None, None),
            P("nodes", None),
            P("nodes", None, None),
            P("nodes", None, None),
            P(),
            P(),
            P(),
            P(),
            P(),
            P(),
            P(),
            P(),
            P(),
            P(),
            P(),
            P(),
        ),
        out_specs=(P(), P(), P(), P(), P(), P(), P(), P(), P(), P(), P(), P(), P()),
        check_vma=False,
    )
```

profile of v0, /device:TPU:0, one launch (start us, length us, event | category | flops | bytes accessed | tf_op | source)
XLA Modules:
  0.0 892.4 jit_solution(14402231583675379104)
XLA Ops:
  8.5 7.3 all-to-all-start
  15.8 8.3 convolution_convert_fusion.5
  25.5 7.8 gather_fusion
  33.3 6.2 all-to-all-start.1
  40.9 6.7 convolution_convert_fusion.4
  47.6 177.9 %all-to-all-done.1 = bf16[32,2,128,512]{3,2,1,0:T(8,128)(2,1)} async-done(((bf16[32,2,128,512]{3,2,1,0:T(8,128)(2,1)}), bf16[32,2,128,512]{3,2,1,0:T(8,128)(2,1)}, u32[]{:S(2)}, u32[]{:S(2)}) %all-to-all-start.1) | async-done | bytes 8388640 | tf_op jit(solution)/shard_map/all_to_all | solution.py:92
  225.5 11.5 %fusion.23 = f32[64,128,512]{2,1,0:T(8,128)} fusion(bf16[64,128,512]{2,1,0:T(8,128)(2,1)} %bitcast.6, bf16[64,128,128]{2,1,0:T(8,128)(2,1)S(1)} %copy-done, pred[64]{0:T(512)(128)(4,1)S(1)} %lt.40), kind=kOutput, calls=%fused_computation.50 | convolution fusion | flops 1074790400 | bytes 27263040 | tf_op jit(solution)/shard_map/kab,kbh->kah/dot_general | solution.py:94
  241.4 36.7 %scatter_fusion = f32[32,128,512]{2,1,0:T(8,128)} fusion(f32[32,128,512]{2,1,0:T(8,128)} %broadcast_in_dim.22, s32[64]{0:T(128)S(1)} %reshape.170, f32[64,128,512]{2,1,0:T(8,128)} %fusion.23), kind=kCustom, calls=%fused_computation.2 | custom fusion | flops 4194304 | bytes 50331904 | tf_op jit(solution)/shard_map/scatter-add | solution.py:98
  288.5 8.3 multiply_reduce_fusion.1
  308.7 4.8 convolution_convert_fusion
  313.6 4.5 convolution_convert_fusion.2
  318.1 7.7 gather_fusion.1
  325.8 9.1 %convolution_convert_fusion.1 = bf16[64,128,512]{2,1,0:T(8,128)(2,1)} fusion(bf16[64,128,512]{2,1,0:T(8,128)(2,1)} %gather_fusion.1, bf16[64,128,128]{2,1,0:T(8,128)(2,1)S(1)} %copy-done, pred[64]{0:T(512)(128)(4,1)S(1)} %lt.40), kind=kOutput, calls=%fused_computation.13 | convolution fusion | flops 1078984704 | bytes 18874432 | tf_op jit(solution)/shard_map/kab,kah->kbh/dot_general | solution.py:143
  339.0 5.9 fusion.14
  345.0 4.7 fusion.17
  351.2 8.5 fusion.11
  359.7 5.2 fusion.12
  364.9 159.9 %all-to-all-done.2 = bf16[32,2,128,512]{3,2,1,0:T(8,128)(2,1)} async-done(((bf16[32,2,128,512]{3,2,1,0:T(8,128)(2,1)}), bf16[32,2,128,512]{3,2,1,0:T(8,128)(2,1)}, u32[]{:S(2)}, u32[]{:S(2)}) %all-to-all-start.2) | async-done | bytes 8388640 | tf_op jit(solution)/shard_map/all_to_all | solution.py:148
  524.9 14.4 %copy.48 = f32[8,8,128,512]{3,1,2,0:T(8,128)} copy(bf16[8,8,128,512]{3,2,1,0:T(8,128)(2,1)} %bitcast.41) | data formatting | bytes 25165824
  543.0 154.6 %scatter_fusion.1 = f32[32,65536]{1,0:T(8,128)} fusion(f32[32,65536]{1,0:T(8,128)} %broadcast_in_dim.25, s32[64]{0:T(128)S(1)} %reshape.178, f32[64,65536]{1,0:T(8,128)} %bitcast.59), kind=kCustom, calls=%fused_computation.3 | custom fusion | flops 4194304 | bytes 50331904 | tf_op jit(solution)/shard_map/scatter-add | solution.py:154
  697.6 7.8 reshape.150
  705.4 12.0 %convolution_bitcast_fusion = f32[602,512]{1,0:T(8,128)} fusion(bf16[4096,602]{0,1:T(8,128)(2,1)} %param.20, f32[4096,512]{1,0:T(8,128)} %reshape.150, bf16[4096,1024]{1,0:T(8,128)(2,1)} %copy-done.29, bf16[1,2,512,512]{3,2,1,0:T(8,128)(2,1)S(1)} %convert_element_type.62), kind=kOutput, calls=%fused_computation.42 | convolution fusion | flops 4676648960 | bytes 19320832 | tf_op jit(solution)/shard_map/dot_general | solution.py:24
  718.3 39.3 %psum.35 = f32[1]{0:T(128)} all-reduce(f32[1]{0:T(128)} %bitcast.11), channel_id=1, replica_groups=mesh['nodes'=32] {'nodes'}, use_global_device_ids=true, to_apply=%region_3.4 | all-reduce | flops 1 | bytes 8 | tf_op jit(solution)/shard_map/psum | solution.py:166
  757.6 110.5 %all-reduce.3.cloned.1.call-done = (f32[602,512]{1,0:T(8,128)}, f32[1,2,512,512]{3,2,1,0:T(8,128)}, f32[1,1024,512]{2,1,0:T(8,128)}, f32[512,121]{1,0:T(8,128)}) async-done(((f32[602,512]{1,0:T(8,128)}, f32[1,2,512,512]{3,2,1,0:T(8,128)}, f32[1,1024,512]{2,1,0:T(8,128)}, f32[512,121]{1,0:T(8,128)}), (f32[602,512]{1,0:T(8,128)}, f32[1,2,512,512]{3,2,1,0:T(8,128)}, f32[1,1024,512]{2,1,0:T(8,128)}, ...) | async-done | bytes 5675024 | tf_op jit(solution)/shard_map/psum | solution.py:166
  (104 shorter events, 56.3 us)
Async XLA Ops:
  8.5 15.6 %all-to-all-start = ((s32[32,1,2]{2,1,0:T(1,128)}), s32[32,1,2]{2,1,0:T(1,128)S(1)}, u32[]{:S(2)}, u32[]{:S(2)}) async-start(s32[32,1,2]{2,1,0:T(1,128)} %copy.44), calls=%async_computation | async-start | bytes 32768 | tf_op jit(solution)/shard_map/all_to_all | solution.py:82
  24.2 9.1 %copy-start.22 = (s32[32,1,2]{2,1,0:T(1,128)}, s32[32,1,2]{2,1,0:T(1,128)S(1)}, u32[]{:S(2)}) copy-start(s32[32,1,2]{2,1,0:T(1,128)S(1)} %all-to-all-done) | copy-start | bytes 772
  33.3 6.2 copy-start.25
  33.3 7.2 copy-start.26
  33.3 7.4 copy-start.24
  33.3 7.4 copy-start.2
  33.3 192.2 %all-to-all-start.1 = ((bf16[32,2,128,512]{3,2,1,0:T(8,128)(2,1)}), bf16[32,2,128,512]{3,2,1,0:T(8,128)(2,1)}, u32[]{:S(2)}, u32[]{:S(2)}) async-start(bf16[32,2,128,512]{3,2,1,0:T(8,128)(2,1)} %bitcast.60), calls=%async_computation.1 | async-start | bytes 16777216 | tf_op jit(solution)/shard_map/all_to_all | solution.py:92
  40.9 184.7 %copy-start = (bf16[64,128,128]{2,1,0:T(8,128)(2,1)S(1)}, bf16[64,128,128]{2,1,0:T(8,128)(2,1)}, u32[]{:S(2)}) copy-start(bf16[64,128,128]{2,1,0:T(8,128)(2,1)} %param.27) | copy-start | bytes 6291460
  288.5 8.4 copy-start.18
  288.5 8.4 copy-start.27
  296.9 7.6 copy-start.1
  334.9 190.0 %all-to-all-start.2 = ((bf16[32,2,128,512]{3,2,1,0:T(8,128)(2,1)}), bf16[32,2,128,512]{3,2,1,0:T(8,128)(2,1)}, u32[]{:S(2)}, u32[]{:S(2)}) async-start(bf16[32,2,128,512]{3,2,1,0:T(8,128)(2,1)} %bitcast.61), calls=%async_computation.2 | async-start | bytes 16777216 | tf_op jit(solution)/shard_map/all_to_all | solution.py:148
  338.7 529.4 %all-reduce.3.cloned.1.call-start = ((), (), s32[]{:S(2)}) async-start(), calls=%async_computation.3 | async-start | bytes 11403264 | tf_op jit(solution)/shard_map/psum | solution.py:166
  339.0 6.0 copy-start.5
  345.0 6.2 copy-start.7
  345.0 6.2 copy-start.31
  349.7 10.0 %slice-start = ((s8[8388608]{0:T(1024)(128)(4,1)}), s8[4194304]{0:T(1024)(128)(4,1)S(1)}, s32[]{:S(2)}) async-start(s8[8388608]{0:T(1024)(128)(4,1)} %bitcast.64), calls=%async_computation.4 | async-start | bytes 8388608
  351.2 8.5 slice-start.1
  351.2 8.5 copy-start.28
  717.4 150.7 %copy-start.19 = (f32[512,121]{1,0:T(8,128)S(1)}, f32[512,121]{1,0:T(8,128)}, u32[]{:S(2)}) copy-start(f32[512,121]{1,0:T(8,128)} %param.31) | copy-start | bytes 743428
  717.4 150.7 %copy-start.20 = (f32[512,121]{1,0:T(8,128)S(1)}, f32[512,121]{1,0:T(8,128)}, u32[]{:S(2)}) copy-start(f32[512,121]{1,0:T(8,128)} %param.35) | copy-start | bytes 743428
  717.4 150.7 %copy-start.21 = (f32[512,121]{1,0:T(8,128)S(1)}, f32[512,121]{1,0:T(8,128)}, u32[]{:S(2)}) copy-start(f32[512,121]{1,0:T(8,128)} %param.39) | copy-start | bytes 743428
  717.4 152.6 %copy-start.16 = (f32[602,512]{1,0:T(8,128)S(1)}, f32[602,512]{1,0:T(8,128)}, u32[]{:S(2)}) copy-start(f32[602,512]{1,0:T(8,128)} %param.28) | copy-start | bytes 3698692
  717.4 152.6 %copy-start.17 = (f32[602,512]{1,0:T(8,128)S(1)}, f32[602,512]{1,0:T(8,128)}, u32[]{:S(2)}) copy-start(f32[602,512]{1,0:T(8,128)} %param.32) | copy-start | bytes 3698692
  (15 other events, 65.0 us)
Sparse Core Ops, SparseCore 0:
  717.6 150.4 all-reduce.2
where the time goes:
time: 898 us; the launch traced here: 892 us
  waiting for transfers between devices  448 us (50%)
  other arithmetic  216 us (24%)
  matrix products  102 us (11%)
  local copies, waits for them, and re-layouts  53.2 us (6%)
  blocking collectives  39.3 us (4%)
  starting transfers between devices  17.5 us (2%)
  between operations  16.4 us (2%)
    all_to_all x1, waiting for transfers between devices, shards(): lax.all_to_all(outgoing, 'nodes', split_axis=0, concat_axis=0, tiled=True)  178 us
    all_to_all x1, waiting for transfers between devices, shards(): lax.all_to_all(return_outgoing, 'nodes', split_axis=0, concat_axis=0, til...  160 us
    scatter-add x1, other arithmetic, shards(): summed = jax.ops.segment_sum(flat_grads, asked, num_segments=block_count)  155 us
    psum x1, waiting for transfers between devices, shards(): lax.psum((loss_part, embed_grad, pair_grad, merge_grad, head_grad), 'nodes')  110 us
    psum x1, blocking collectives, shards(): lax.psum((loss_part, embed_grad, pair_grad, merge_grad, head_grad), 'nodes')  39.3 us
    scatter-add x1, other arithmetic, shards(): jax.ops.segment_sum(products, sinks, num_segments=block_count)  36.7 us
    dot_general x5, matrix products, left_product(): lax.dot_general(former, latter, (((0,), (0,)), ((), ())), preferred_eleme...  36.3 us
    dot_general x5, matrix products, mat_product(): return jnp.dot(former, latter, preferred_element_type=jnp.float32)  32.1 us
  transfers between devices with their start and end apart: 4, of which 3 were waited for; matrix products, arithmetic and copies ran while one was open for 5% of the time, Pallas kernels for 0%

commit v1 on v0

v1 whole, which is shorter than its diff:
```python
import functools

import jax
import jax.numpy as jnp
from jax import lax
from jax.experimental import pallas as pl
from jax.experimental.pallas import tpu as pltpu
from jax.sharding import PartitionSpec as P

norm_eps = 1e-06
learn_rate = 0.03
beta_one = 0.9
beta_two = 0.999
adam_eps = 1e-08
decay_rate = 0.01
adam_step = 10.0

PLANES = 4
KINDS = 4
CHUNKS = 8
MESH = pl.DeviceIdType.MESH


def to_half(value):
    return value.astype(jnp.bfloat16)


def mat_product(former, latter):
    return jnp.dot(former, latter, preferred_element_type=jnp.float32)


def left_product(former, latter):
    return lax.dot_general(
        former, latter, (((0,), (0,)), ((), ())), preferred_element_type=jnp.float32
    )


def right_product(former, latter):
    return lax.dot_general(
        former, latter, (((1,), (1,)), ((), ())), preferred_element_type=jnp.float32
    )


def adam_update(weight, grad, first, second):
    first_new = beta_one * first + (1.0 - beta_one) * grad
    second_new = beta_two * second + (1.0 - beta_two) * grad * grad
    first_hat = first_new / (1.0 - beta_one**adam_step)
    second_hat = second_new / (1.0 - beta_two**adam_step)
    weight_new = weight - learn_rate * (
        first_hat / (jnp.sqrt(second_hat) + adam_eps) + decay_rate * weight
    )
    return (weight_new, first_new, second_new)


def place(me, plane_size):
    z = me // plane_size
    spot = me % plane_size
    inner = (z % 2 + z // 2) % 2
    near = z + 1 - 2 * (z % 2)
    far_in = 2 - z // 2
    far_out = 3 * (1 - z // 2)
    return z, spot, inner, near, far_in, far_out


def exchange_kernel(n, slots, far_cap, near_cap, ring, *refs):
    far_list, near_list, pass_list, serve = refs[:4]
    table = refs[4]
    out = refs[5]
    rest = list(refs[6:])
    far_stage = [rest.pop(0) for _ in range(CHUNKS)]
    near_stage = [rest.pop(0) for _ in range(CHUNKS)]
    near_got = [rest.pop(0) for _ in range(CHUNKS)]
    far_got = [[rest.pop(0) for _ in range(CHUNKS)] for _ in range(2)]
    pass_stage = [[rest.pop(0) for _ in range(CHUNKS)] for _ in range(2)]
    serve_stage = [rest.pop(0) for _ in range(ring)]
    far_sent, near_sent, near_recv, far_recv, pass_sent, serve_sent, serve_recv = rest

    size = n // PLANES
    rows = table.shape[1] // CHUNKS
    me = lax.axis_index("nodes")
    z, spot, inner, near, far_in, far_out = place(me, size)
    near_dev = near * size + spot
    relay_dev = far_in * size + spot
    outer_dev = far_out * size + spot
    is_inner = inner == 1

    barrier = pltpu.get_barrier_semaphore()

    def greet(step, carry):
        pl.semaphore_signal(
            barrier,
            inc=1,
            device_id=(z * size + lax.rem(spot + step, size),),
            device_id_type=MESH,
        )
        return carry

    lax.fori_loop(1, size, greet, 0)
    pl.semaphore_signal(barrier, inc=1, device_id=(near_dev,), device_id_type=MESH)

    @pl.when(is_inner)
    def _():
        pl.semaphore_signal(barrier, inc=1, device_id=(relay_dev,), device_id_type=MESH)
        pl.semaphore_signal(barrier, inc=1, device_id=(outer_dev,), device_id_type=MESH)

    pl.semaphore_wait(barrier, size + 1)

    def far_copy(step, lane):
        return pltpu.make_async_remote_copy(
            src_ref=far_stage[step],
            dst_ref=far_got[lane][step],
            send_sem=far_sent.at[step],
            recv_sem=far_recv.at[lane, step],
            device_id=(relay_dev,),
            device_id_type=MESH,
        )

    def near_copy(step):
        return pltpu.make_async_remote_copy(
            src_ref=near_stage[step],
            dst_ref=near_got[step],
            send_sem=near_sent.at[step],
            recv_sem=near_recv.at[step],
            device_id=(near_dev,),
            device_id_type=MESH,
        )

    def pass_copy(step, lane):
        return pltpu.make_async_remote_copy(
            src_ref=pass_stage[lane][step],
            dst_ref=far_got[lane][step].at[pl.ds(0, near_cap)],
            send_sem=pass_sent.at[lane, step],
            recv_sem=far_recv.at[lane, step],
            device_id=(near_dev,),
            device_id_type=MESH,
        )

    for step in range(CHUNKS):
        window = pl.ds(step * rows, rows)

        def fill_far(at, carry):
            far_stage[step][at] = table[far_list[at], window, :]
            return carry

        lax.fori_loop(0, far_cap, fill_far, 0)

        @pl.when(is_inner)
        def _():
            far_copy(step, 0).start()

        @pl.when(inner == 0)
        def _():
            far_copy(step, 1).start()

        def fill_near(at, carry):
            near_stage[step][at] = table[near_list[at], window, :]
            return carry

        lax.fori_loop(0, near_cap, fill_near, 0)
        near_copy(step).start()

    def serve_copy(step, peer):
        return pltpu.make_async_remote_copy(
            src_ref=serve_stage[step % ring].at[peer],
            dst_ref=out.at[step, spot],
            send_sem=serve_sent.at[step % ring],
            recv_sem=serve_recv.at[step],
            device_id=(z * size + peer,),
            device_id_type=MESH,
        )

    def serve_drain(step):
        held = serve_stage[step % ring].at[pl.ds(0, size - 1)]
        pltpu.make_async_copy(held, held, serve_sent.at[step % ring]).wait()

    for step in range(CHUNKS):
        window = pl.ds(step * rows, rows)

        @pl.when(is_inner)
        def _():
            for lane in range(2):
                pltpu.make_async_copy(
                    far_got[lane][step], far_got[lane][step], far_recv.at[lane, step]
                ).wait()

                def fill_pass(at, carry):
                    pass_stage[lane][step][at] = far_got[lane][step][pass_list[lane, at]]
                    return carry

                lax.fori_loop(0, near_cap, fill_pass, 0)
                pass_copy(step, lane).start()

        @pl.when(inner == 0)
        def _():
            for lane in range(2):
                part = far_got[lane][step].at[pl.ds(0, near_cap)]
                pltpu.make_async_copy(part, part, far_recv.at[lane, step]).wait()

        pltpu.make_async_copy(near_got[step], near_got[step], near_recv.at[step]).wait()
        if step >= ring:
            serve_drain(step - ring)

        def fill_serve(peer, carry):
            stage = serve_stage[step % ring]
            for slot in range(slots):
                stage[peer, 0, slot] = table[serve[peer, 0, slot], window, :]
                stage[peer, 1, slot] = near_got[step][serve[peer, 1, slot]]
                stage[peer, 2, slot] = far_got[0][step][serve[peer, 2, slot]]
                stage[peer, 3, slot] = far_got[1][step][serve[peer, 3, slot]]
            return carry

        lax.fori_loop(0, size, fill_serve, 0)
        pltpu.make_async_copy(
            serve_stage[step % ring].at[spot], out.at[step, spot], serve_recv.at[step]
        ).start()

        def send(hop, carry):
            serve_copy(step, lax.rem(spot + hop, size)).start()
            return carry

        lax.fori_loop(1, size, send, 0)

    for step in range(CHUNKS):
        pltpu.make_async_copy(out.at[step], out.at[step], serve_recv.at[step]).wait()
    for step in range(max(0, CHUNKS - ring), CHUNKS):
        serve_drain(step)
    for step in range(CHUNKS):
        pltpu.make_async_copy(far_stage[step], far_stage[step], far_sent.at[step]).wait()
        pltpu.make_async_copy(near_stage[step], near_stage[step], near_sent.at[step]).wait()

    @pl.when(is_inner)
    def _():
        for step in range(CHUNKS):
            for lane in range(2):
                held = pass_stage[lane][step]
                pltpu.make_async_copy(held, held, pass_sent.at[lane, step]).wait()


def exchange(n, slots, far_cap, near_cap, collective, lists, table):
    size = n // PLANES
    blocks, depth, width = table.shape
    rows = depth // CHUNKS
    kind = table.dtype
    ring = CHUNKS if size <= 8 else 2

    def rows_of(*lead):
        return pltpu.VMEM(lead + (rows, width), kind)

    scratch = (
        [rows_of(far_cap) for _ in range(CHUNKS)]
        + [rows_of(near_cap) for _ in range(2 * CHUNKS)]
        + [rows_of(far_cap) for _ in range(2 * CHUNKS)]
        + [rows_of(near_cap) for _ in range(2 * CHUNKS)]
        + [rows_of(size, KINDS, slots) for _ in range(ring)]
        + [
            pltpu.SemaphoreType.DMA((CHUNKS,)),
            pltpu.SemaphoreType.DMA((CHUNKS,)),
            pltpu.SemaphoreType.DMA((CHUNKS,)),
            pltpu.SemaphoreType.DMA((2, CHUNKS)),
            pltpu.SemaphoreType.DMA((2, CHUNKS)),
            pltpu.SemaphoreType.DMA((ring,)),
            pltpu.SemaphoreType.DMA((CHUNKS,)),
        ]
    )
    far_list, near_list, pass_list, serve = lists
    smem = pl.BlockSpec(memory_space=pltpu.SMEM)
    return pl.pallas_call(
        functools.partial(exchange_kernel, n, slots, far_cap, near_cap, ring),
        out_shape=jax.ShapeDtypeStruct((CHUNKS, size, KINDS, slots, rows, width), kind),
        in_specs=[smem, smem, smem, smem, pl.BlockSpec(memory_space=pltpu.VMEM)],
        out_specs=pl.BlockSpec(memory_space=pl.ANY),
        scratch_shapes=scratch,
        compiler_params=pltpu.CompilerParams(
            collective_id=collective, has_side_effects=True, vmem_limit_bytes=60 * 2**20
        ),
        name="exchange",
    )(far_list[:far_cap], near_list[:near_cap], pass_list[:, :near_cap], serve, table)


def gather_sum_kernel(flip, slots, order, sinks, weights, got, out, total):
    at = pl.program_id(0)

    @pl.when(at == 0)
    def _():
        total[...] = jnp.zeros_like(total)

    blocks, depth, width = total.shape
    for kind in range(KINDS):
        for slot in range(slots):
            sink = sinks[at, kind, slot]

            @pl.when(sink < blocks)
            def _():
                edge = weights[order[kind], 0, slot]
                rows = got[:, 0, kind, slot].reshape(depth, width)
                dims = (((0,), (0,)), ((), ())) if flip else (((1,), (0,)), ((), ()))
                total[sink] += lax.dot_general(
                    edge, rows, dims, preferred_element_type=jnp.float32
                )

    @pl.when(at == pl.num_programs(0) - 1)
    def _():
        out[...] = total[...].astype(out.dtype)


def gather_sum(flip, kind, order, sinks, weights, got, blocks):
    size, _, slots = sinks.shape
    chunks, _, _, _, rows, width = got.shape
    depth = chunks * rows
    edges = weights.reshape(PLANES, size, slots, depth, depth)
    return pl.pallas_call(
        functools.partial(gather_sum_kernel, flip, slots),
        out_shape=jax.ShapeDtypeStruct((blocks, depth, width), kind),
        grid_spec=pltpu.PrefetchScalarGridSpec(
            num_scalar_prefetch=2,
            grid=(size,),
            in_specs=[
                pl.BlockSpec(
                    (PLANES, 1, slots, depth, depth), lambda at, order, sinks: (0, at, 0, 0, 0)
                ),
                pl.BlockSpec(
                    (chunks, 1, KINDS, slots, rows, width),
                    lambda at, order, sinks: (0, at, 0, 0, 0, 0),
                ),
            ],
            out_specs=pl.BlockSpec((blocks, depth, width), lambda at, order, sinks: (0, 0, 0)),
            scratch_shapes=[pltpu.VMEM((blocks, depth, width), jnp.float32)],
        ),
        compiler_params=pltpu.CompilerParams(vmem_limit_bytes=40 * 2**20),
        name="gather_sum",
    )(order, sinks, edges, got)


def pick(values, hot, axis):
    shape = [1] * values.ndim
    shape[axis] = values.shape[axis]
    return jnp.sum(jnp.where(hot.reshape(shape), values, 0), axis=axis)


def by_kind(values, order, axis):
    planes = jnp.arange(PLANES, dtype=jnp.int32)
    return jnp.stack([pick(values, planes == order[kind], axis) for kind in range(KINDS)], axis)


def index_tables(n, blocks, taken, me):
    size = n // PLANES
    ways, slots = taken.shape[0], taken.shape[3]
    z, spot, inner, near, far_in, far_out = place(me, size)
    planes = jnp.arange(PLANES, dtype=jnp.int32)
    block_ids = jnp.arange(blocks, dtype=jnp.int32)
    split = taken.reshape(ways, PLANES, size, PLANES, size, slots)
    every = jnp.any(
        split[..., None] == block_ids, axis=(2, 5)
    )
    every_far = every.reshape(ways, 2, 2, PLANES, size, blocks).any(axis=2)
    own_plane = (planes[:, None] == planes[None, :])[None, :, :, None]
    own_half = (jnp.arange(2)[:, None] == planes[None, :] // 2)[None, :, :, None]
    near_need = jnp.max(
        jnp.where(own_plane, 0, jnp.sum(every.astype(jnp.int32), axis=-1)), axis=(1, 2, 3)
    )
    far_need = jnp.max(
        jnp.where(own_half, 0, jnp.sum(every_far.astype(jnp.int32), axis=-1)), axis=(1, 2, 3)
    )

    order = jnp.stack([z, near, far_in, far_out])
    mine = lax.dynamic_index_in_dim(split, spot, 4, keepdims=False)
    mine = by_kind(mine, order, 3)
    hit = jnp.any(
        mine[..., None] == block_ids, axis=(2, 4)
    )
    hit_half = hit.reshape(ways, 2, 2, KINDS, blocks).any(axis=2)
    below = (block_ids[:, None] > block_ids[None, :]).astype(jnp.int32)

    def ranks(present):
        return jnp.sum(present[..., None, :].astype(jnp.int32) * below, axis=-1)

    rank = ranks(hit)
    rank_half = ranks(hit_half)
    half = z // 2
    outer_plane = 3 * half
    here = planes == z
    pos_here = pick(rank, here, 1)
    hit_outer = jnp.any(hit & (planes == outer_plane).reshape(1, PLANES, 1, 1), axis=1)
    pos_outer = pick(rank, planes == outer_plane, 1)
    hit_near = jnp.any(hit & (planes == near).reshape(1, PLANES, 1, 1), axis=1)
    pos_near = pick(rank, planes == near, 1)
    halves = jnp.arange(2)
    pos_half = pick(rank_half, halves == half, 1)
    hit_far = jnp.any(hit_half & (halves == 1 - half).reshape(1, 2, 1, 1), axis=1)
    pos_far = pick(rank_half, halves == 1 - half, 1)

    def compact(present, pos, value):
        spots = block_ids[:, None]
        return jnp.sum(
            jnp.where(present[..., None, :] & (pos[..., None, :] == spots), value[..., None, :], 0),
            axis=-1,
        )

    ids = jnp.broadcast_to(block_ids, (ways, blocks))
    far_list = compact(hit_far[:, 0], pos_far[:, 0], ids)
    near_list = compact(hit_near[:, 0], pos_near[:, 0], ids)
    pass_list = compact(hit_outer[:, 2:], pos_outer[:, 2:], pos_half[:, 2:])
    kinds = jnp.arange(KINDS)[None, :, None]
    spot_map = jnp.where(
        kinds == 0, block_ids, jnp.where((kinds >= 2) & (inner == 1), pos_half, pos_here)
    )
    wanted = pick(mine, here, 1)
    serve = jnp.sum(
        jnp.where(wanted[..., None] == block_ids, spot_map[:, None, :, None, :], 0), axis=-1
    )
    return order, far_list, near_list, pass_list, serve, near_need, far_need


def my_slots(n, table, order):
    size = n // PLANES
    return by_kind(table.reshape(PLANES, size, -1), order, 0).transpose(1, 0, 2)


def shards(
    features,
    labels,
    labelled,
    label_count,
    need_blocks,
    need_count,
    target_block,
    adjacency,
    embed_weight,
    pair_weight,
    merge_weight,
    head_weight,
    embed_moment,
    pair_moment,
    merge_moment,
    head_moment,
    embed_variance,
    pair_variance,
    merge_variance,
    head_variance,
):
    row_count = features.shape[0]
    hidden_width = embed_weight.shape[1]
    block_rows = adjacency.shape[1]
    slots = need_blocks.shape[2]
    n = lax.axis_size("nodes")
    size = n // PLANES
    block_count = row_count // block_rows
    me = lax.axis_index("nodes")

    alive = lax.broadcasted_iota(jnp.int32, need_blocks.shape[1:], 1) < need_count[0][:, None]
    wanted = jnp.where(alive, need_blocks[0], block_count)
    sunk = jnp.where(alive, target_block[0], block_count)
    tables = lax.all_gather(jnp.stack([wanted, sunk]), "nodes", axis=0, tiled=False)
    taken = jnp.stack([tables[:, 0], tables[:, 1].transpose(1, 0, 2)])
    order, far_list, near_list, pass_list, serve, near_need, far_need = index_tables(
        n, block_count, taken, me
    )
    near_full = min(block_count, size * slots)
    rungs = [(min(23, block_count), min(15, near_full)), (block_count, near_full)]
    if near_full > 16:
        rungs = rungs[1:]

    def swap(way, table):
        lists = (far_list[way], near_list[way], pass_list[way], serve[way])

        def at(rung):
            far_cap, near_cap = rungs[rung]
            return lambda *held: exchange(
                n, slots, far_cap, near_cap, 1 + way * len(rungs) + rung, held[:4], held[4]
            )

        if len(rungs) == 1:
            return at(0)(*lists, table)
        fits = (far_need[way] <= rungs[0][0]) & (near_need[way] <= rungs[0][1])
        return lax.cond(fits, at(0), at(1), *lists, table)

    pair_half = to_half(pair_weight)
    merge_half = to_half(merge_weight)
    head_half = to_half(head_weight)
    hidden_half = to_half(mat_product(features, to_half(embed_weight)))
    got = swap(0, hidden_half.reshape(block_count, block_rows, hidden_width))
    gathered = gather_sum(
        False, jnp.bfloat16, order, my_slots(n, sunk, order), adjacency, got, block_count
    ).reshape(row_count, hidden_width)
    adjacency_later, gathered = lax.optimization_barrier((adjacency, gathered))
    edges_back = lax.all_to_all(adjacency_later, "nodes", split_axis=0, concat_axis=0, tiled=True)

    self_part = mat_product(hidden_half, pair_half[0, 0])
    neigh_part = mat_product(gathered, pair_half[0, 1])
    joined = to_half(jnp.concatenate([self_part, neigh_part], axis=1))
    linear = mat_product(joined, merge_half[0])
    active = linear * jax.nn.sigmoid(linear)
    scale = lax.rsqrt(jnp.sum(active * active, axis=1, keepdims=True) + norm_eps)
    output = active * scale
    final_half = to_half(output)
    logits = mat_product(final_half, head_half)
    truth = labels.astype(jnp.float32)
    row_mask = labelled.astype(jnp.float32)[:, None]
    denom = label_count[0].astype(jnp.float32) * logits.shape[1]
    per_entry = jnp.maximum(logits, 0.0) - logits * truth + jnp.log1p(jnp.exp(-jnp.abs(logits)))
    loss_part = jnp.sum(per_entry * row_mask) / denom
    grad_logits = to_half((jax.nn.sigmoid(logits) - truth) * row_mask / denom)
    head_grad = left_product(final_half, grad_logits)
    grad_out = right_product(grad_logits, head_half)
    grad_active = scale * (grad_out - output * jnp.sum(grad_out * output, axis=1, keepdims=True))
    sig_value = jax.nn.sigmoid(linear)
    grad_linear = to_half(grad_active * sig_value * (1.0 + linear * (1.0 - sig_value)))
    merge_grad = left_product(joined, grad_linear)
    grad_joined = to_half(right_product(grad_linear, merge_half[0]))
    grad_self_out = grad_joined[:, :hidden_width]
    grad_neigh_out = grad_joined[:, hidden_width:]
    grad_self = left_product(hidden_half, grad_self_out)
    grad_neigh = left_product(gathered, grad_neigh_out)
    grad_gathered = to_half(right_product(grad_neigh_out, pair_half[0, 1]))
    pair_grad = jnp.stack([grad_self, grad_neigh])[None]
    merge_grad = merge_grad[None]
    spread = jnp.zeros((head_grad.shape[0], 128 - head_grad.shape[1]), jnp.float32)
    spread = spread.at[0, 0].set(loss_part)
    head_wide = jnp.concatenate([head_grad, spread], axis=1)
    pair_grad, merge_grad, head_wide = lax.psum((pair_grad, merge_grad, head_wide), "nodes")
    labels_width = head_grad.shape[1]
    head_grad = head_wide[:, :labels_width]
    loss_total = head_wide[0, labels_width]

    back = swap(1, grad_gathered.reshape(block_count, block_rows, hidden_width))
    summed = gather_sum(
        True,
        jnp.float32,
        order,
        my_slots(n, taken[0][:, me], order),
        edges_back,
        back,
        block_count,
    ).reshape(row_count, hidden_width)
    grad_hidden = right_product(grad_self_out, pair_half[0, 0]) + summed
    embed_grad = lax.psum(left_product(features, to_half(grad_hidden)), "nodes")
    pair_next = adam_update(pair_weight, pair_grad, pair_moment, pair_variance)
    merge_next = adam_update(merge_weight, merge_grad, merge_moment, merge_variance)
    head_next = adam_update(head_weight, head_grad, head_moment, head_variance)
    embed_next = adam_update(embed_weight, embed_grad, embed_moment, embed_variance)
    return (
        loss_total.reshape(1),
        embed_next[0],
        pair_next[0],
        merge_next[0],
        head_next[0],
        embed_next[1],
        pair_next[1],
        merge_next[1],
        head_next[1],
        embed_next[2],
        pair_next[2],
        merge_next[2],
        head_next[2],
    )


def solution(mesh):
    split = ("nodes",)
    return jax.shard_map(
        shards,
        mesh=mesh,
        in_specs=(
            P("nodes", None),
            P("nodes", None),
            P("nodes"),
            P(),
            P("nodes", None, None),
            P("nodes", None),
            P("nodes", None, None),
            P("nodes", None, None),
        )
        + (P(),) * 12,
        out_specs=(P(),) * 13,
        check_vma=False,
    )
```

time: 898 us -> 708 us (0.79)
  Pallas kernels: 0 us -> 361 us
  waiting for transfers between devices: 448 us -> 152 us
  other arithmetic: 216 us -> 29.2 us
  matrix products: 102 us -> 63.9 us
  local copies, waits for them, and re-layouts: 53.2 us -> 21.8 us
    pallas_call x0 -> x4, Pallas kernels: none -> 361 us  [the longest x2 332 us: exchange(): pl.pallas_call(functools.partial(exchange_kernel, n, slots, far_cap, near...]
    all_to_all x3 -> x1, waiting for transfers between devices: 338 us -> 0.01 us  [shards(): lax.all_to_all(adjacency_later, 'nodes', split_axis=0, concat_axis=0, til...]
    scatter-add x2 -> x0, other arithmetic: 191 us -> none  [the longest x1 155 us: shards(): summed = jax.ops.segment_sum(flat_grads, asked, num_segments=block_count)]
    all_gather x0 -> x1, blocking collectives: none -> 43.4 us  [shards(): lax.all_gather(jnp.stack([wanted, sunk]), 'nodes', axis=0, tiled=False)]
    psum x1, waiting for transfers between devices: 110 us -> 152 us  [shards(): lax.psum((pair_grad, merge_grad, head_wide), 'nodes')]
    psum x1 -> x0, blocking collectives: 39.3 us -> none  [shards(): lax.psum((loss_part, embed_grad, pair_grad, merge_grad, head_grad), 'nodes')]
    dot_general x2 -> x0, matrix products: 20.6 us -> none  [the longest x1 11.5 us: shards(): jnp.einsum('kab,kbh->kah', live_weights, received, preferred_element_type...]
    gather x2 -> x0, local copies, waits for them, and re-layouts: 15.5 us -> none  [the longest x1 7.77 us: shards(): outgoing = hidden_half.reshape(block_count, block_rows, hidden_width)[asked]]
  transfers between devices with their start and end apart: 4 -> 2, of which waited for: 3 -> 1; matrix products, arithmetic and copies ran while one was open for 5% -> 8% of each run, Pallas kernels for 0% -> 24%
where the time goes in v1:
time: 708 us; the launch traced here: 700 us
  Pallas kernels  361 us (51%)
  waiting for transfers between devices  152 us (21%)
  matrix products  63.9 us (9%)
  blocking collectives  43.4 us (6%)
  other arithmetic  29.2 us (4%)
  local copies, waits for them, and re-layouts  21.8 us (3%)
  between operations  19.1 us (3%)
  starting transfers between devices  9.75 us (1%)
    pallas_call x2, Pallas kernels, exchange(): pl.pallas_call(functools.partial(exchange_kernel, n, slots, far_cap, near...  332 us
    psum x1, waiting for transfers between devices, shards(): lax.psum((pair_grad, merge_grad, head_wide), 'nodes')  152 us
    all_gather x1, blocking collectives, shards(): lax.all_gather(jnp.stack([wanted, sunk]), 'nodes', axis=0, tiled=False)  43.4 us
    pallas_call x2, Pallas kernels, gather_sum(): pl.pallas_call(functools.partial(gather_sum_kernel, flip, slots), out_sha...  28.2 us
    dot_general x5, matrix products, mat_product(): return jnp.dot(former, latter, preferred_element_type=jnp.float32)  25.6 us
    dot_general x5, matrix products, left_product(): lax.dot_general(former, latter, (((0,), (0,)), ((), ())), preferred_eleme...  21.1 us
    dot_general x4, matrix products, right_product(): lax.dot_general(former, latter, (((1,), (1,)), ((), ())), preferred_eleme...  17.3 us
    unnamed x75, local copies, waits for them, and re-layouts  15 us
  transfers between devices with their start and end apart: 2, of which 1 were waited for; matrix products, arithmetic and copies ran while one was open for 8% of the time, Pallas kernels for 24%

profile of v1, /device:TPU:0, one launch (start us, length us, event | category | flops | bytes accessed | tf_op | source)
XLA Modules:
  0.0 700.2 jit_solution(8630613233128445649)
XLA Ops:
  8.9 43.4 %all-gather = s32[64,32,2]{1,2,0:T(2,128)S(1)} all-gather(s32[2,32,2]{1,2,0:T(2,128)S(1)} %pad_add_fusion.1), channel_id=2, replica_groups=mesh['nodes'=32] {'nodes'}, dimensions={0}, use_global_device_ids=true | all-gather | bytes 16896 | tf_op jit(solution)/shard_map/all_gather | solution.py:453
  56.5 7.6 %convolution_convert_fusion.4 = bf16[4096,512]{1,0:T(8,128)(2,1)} fusion(bf16[4096,602]{0,1:T(8,128)(2,1)} %param.26, f32[602,512]{1,0:T(8,128)S(1)} %copy-done.16), kind=kOutput, calls=%fused_computation.13 | convolution fusion | flops 2527376384 | bytes 10358784 | tf_op jit(solution)/shard_map/dot_general | solution.py:29
  71.2 163.5 %conditional.2 = (bf16[8,8,4,2,16,512]{5,4,3,2,1,0:T(8,128)(2,1)}) conditional(s32[]{:T(128)} %bitcast.17, (s32[32]{0:T(128)S(1)}, s32[2,32]{1,0:T(2,128)S(1)}, s32[32]{0:T(128)S(1)}, s32[8,4,2]{0,1,2:T(4,128)S(1)}, bf16[32,128,512]{2,1,0:T(8,128)(2,1)}) %tuple.116, (s32[32]{0:T(128)S(1)}, s32[32]{0:T(128)S(1)}, s32[2,32]{1,0:T(2,128)S(1)}, ...), branch_computations={%region_31.32_spmd, %region_32.33_spmd} | conditional | bytes 520 | solution.py:475
  71.9 162.7 %exchange.5 = bf16[8,8,4,2,16,512]{5,4,3,2,1,0:T(8,128)(2,1)} custom-call(s32[23]{0:T(128)S(1)} %bitcast.177, s32[15]{0:T(128)S(1)} %bitcast.179, s32[2,15]{1,0:T(2,128)S(1)} %bitcast.173, s32[8,4,2]{2,1,0:T(4,128)} %copy.207.refs_3_, bf16[32,128,512]{2,1,0:T(8,128)(2,1)} %get-tuple-element.67.refs_4_), custom_call_target="tpu_custom_call" | custom-call | tf_op jit(solution)/shard_map/cond/branch_1_fun/exchange/pallas_call | solution.py:267
  234.7 12.9 %gather_sum.2 = bf16[32,128,512]{2,1,0:T(8,128)(2,1)S(1)} custom-call(s32[4]{0:T(128)S(1)} %get-tuple-element.360.order, s32[8,4,2]{2,1,0:T(4,128)S(1)} %add_bitcast_fusion.1.sinks, bf16[4,8,2,128,128]{4,3,2,1,0:T(8,128)(2,1)} %bitcast.10.weights, bf16[8,8,4,2,16,512]{5,4,3,2,1,0:T(8,128)(2,1)} %get-tuple-element.373.got), custom_call_target="tpu_custom_call" | custom-call | tf_op jit(solution)/shard_map/gather_sum/pallas_call | solution.py:311
  249.6 9.5 %all-to-all-start = ((bf16[64,128,128]{2,1,0:T(8,128)(2,1)}), bf16[64,128,128]{2,1,0:T(8,128)(2,1)S(1)}, u32[]{:S(2)}, u32[]{:S(2)}) async-start(bf16[64,128,128]{2,1,0:T(8,128)(2,1)} %param.33), calls=%async_computation | async-start | bytes 4194304 | tf_op jit(solution)/shard_map/all_to_all | solution.py:486
  261.7 4.7 convolution_convert_fusion.3
  269.6 6.1 multiply_reduce_fusion.1
  275.8 4.7 multiply_reduce_fusion.2
  283.6 3.3 multiply_reduce_fusion
  286.9 4.4 multiply_convert_fusion
  291.3 4.8 convolution_convert_fusion
  296.2 4.5 convolution_convert_fusion.1
  303.0 170.6 %conditional.3 = (bf16[8,8,4,2,16,512]{5,4,3,2,1,0:T(8,128)(2,1)}) conditional(s32[]{:T(128)} %bitcast.44, (s32[32]{0:T(128)S(1)}, s32[2,32]{1,0:T(2,128)S(1)}, s32[32]{0:T(128)S(1)}, s32[8,4,2]{0,1,2:T(4,128)S(1)}, bf16[32,128,512]{2,1,0:T(8,128)(2,1)}) %tuple.118, (s32[32]{0:T(128)S(1)}, s32[32]{0:T(128)S(1)}, s32[2,32]{1,0:T(2,128)S(1)}, ...), branch_computations={%region_41.42_spmd, %region_42.43_spmd} | conditional | bytes 520 | solution.py:475
  303.7 169.7 %exchange.7 = bf16[8,8,4,2,16,512]{5,4,3,2,1,0:T(8,128)(2,1)} custom-call(s32[23]{0:T(128)S(1)} %bitcast.174, s32[15]{0:T(128)S(1)} %bitcast.176, s32[2,15]{1,0:T(2,128)S(1)} %bitcast.171, s32[8,4,2]{2,1,0:T(4,128)} %copy.214.refs_3_, bf16[32,128,512]{2,1,0:T(8,128)(2,1)} %get-tuple-element.77.refs_4_), custom_call_target="tpu_custom_call" | custom-call | tf_op jit(solution)/shard_map/cond/branch_1_fun/exchange/pallas_call | solution.py:267
  474.4 5.9 fusion.16
  487.2 5.8 fusion.13
  493.0 15.2 %gather_sum.3 = f32[32,128,512]{2,1,0:T(8,128)S(1)} custom-call(s32[4]{0:T(128)S(1)} %get-tuple-element.360.order, s32[8,4,2]{2,1,0:T(4,128)S(1)} %add_bitcast_fusion.2.sinks, bf16[4,8,2,128,128]{4,3,2,1,0:T(8,128)(2,1)S(1)} %bitcast.150, bf16[8,8,4,2,16,512]{5,4,3,2,1,0:T(8,128)(2,1)} %get-tuple-element.374.got), custom_call_target="tpu_custom_call" | custom-call | tf_op jit(solution)/shard_map/gather_sum/pallas_call | solution.py:311
  508.3 4.6 fusion
  513.0 3.8 convolution_bitcast_fusion
  518.2 152.1 %all-reduce.4.cloned.1.call-done = (f32[512,128]{0,1:T(8,128)}, f32[602,512]{1,0:T(8,128)}, f32[1,2,512,512]{3,2,1,0:T(8,128)}, f32[1,1024,512]{2,1,0:T(8,128)}) async-done(((f32[512,128]{0,1:T(8,128)}, f32[602,512]{1,0:T(8,128)}, f32[1,2,512,512]{3,2,1,0:T(8,128)}, f32[1,1024,512]{2,1,0:T(8,128)}), (f32[512,128]{0,1:T(8,128)}, f32[602,512]{1,0:T(8,128)}, f32[1,2,512,512]{3,2,1,0:T(8,128)}, ...) | async-done | bytes 5689360 | tf_op jit(solution)/shard_map/psum | solution.py:520
  677.8 4.4 multiply_subtract_fusion.2
  683.4 4.0 multiply_subtract_fusion.1
  689.0 3.9 multiply_subtract_fusion
  (165 shorter events, 42.7 us)
Async XLA Ops:
  7.2 49.3 %copy-start.16 = (f32[602,512]{1,0:T(8,128)S(1)}, f32[602,512]{1,0:T(8,128)}, u32[]{:S(2)}) copy-start(f32[602,512]{1,0:T(8,128)} %param.34) | copy-start | bytes 3698692
  56.4 8.2 %copy-start.24 = (s32[1,32]{1,0:T(1,128)S(1)}, s32[1,32]{1,0:T(1,128)}, u32[]{:S(2)}) copy-start(s32[1,32]{1,0:T(1,128)} %param.31) | copy-start | bytes 388
  249.6 10.4 %copy-start.23 = (s32[4096]{0:T(1024)S(1)}, s32[4096]{0:T(1024)}, u32[]{:S(2)}) copy-start(s32[4096]{0:T(1024)} %param.28) | copy-start | bytes 49156
  249.6 243.4 %all-to-all-start = ((bf16[64,128,128]{2,1,0:T(8,128)(2,1)}), bf16[64,128,128]{2,1,0:T(8,128)(2,1)S(1)}, u32[]{:S(2)}, u32[]{:S(2)}) async-start(bf16[64,128,128]{2,1,0:T(8,128)(2,1)} %param.33), calls=%async_computation | async-start | bytes 4194304 | tf_op jit(solution)/shard_map/all_to_all | solution.py:486
  259.1 411.2 %all-reduce.4.cloned.1.call-start = ((), (), s32[]{:S(2)}) async-start(), calls=%async_computation.1 | async-start | bytes 11403264 | tf_op jit(solution)/shard_map/psum | solution.py:520
  261.7 4.7 copy-start.1
  269.6 6.2 copy-start.28
  269.6 6.2 copy-start.19
  269.6 6.2 copy-start.25
  291.3 4.9 copy-start.6
  296.2 4.5 copy-start.4
  474.4 6.0 copy-start.2
  474.4 7.1 %copy-start.5 = (bf16[4096,1024]{1,0:T(8,128)(2,1)S(1)}, bf16[4096,1024]{1,0:T(8,128)(2,1)}, u32[]{:S(2)}) copy-start(bf16[4096,1024]{1,0:T(8,128)(2,1)} %copy-done.4) | copy-start | bytes 25165828
  493.0 19.9 %slice-start = ((s8[4980736]{0:T(1024)(128)(4,1)}), s8[4194304]{0:T(1024)(128)(4,1)S(1)}, s32[]{:S(2)}) async-start(s8[4980736]{0:T(1024)(128)(4,1)} %bitcast.195), calls=%async_computation.2 | async-start | bytes 8388608
  508.3 4.7 slice-start.1
  518.0 159.8 %copy-start.17 = (f32[602,512]{1,0:T(8,128)S(1)}, f32[602,512]{1,0:T(8,128)}, u32[]{:S(2)}) copy-start(f32[602,512]{1,0:T(8,128)} %param.34) | copy-start | bytes 3698692
  518.0 159.8 %copy-start.18 = (f32[602,512]{1,0:T(8,128)S(1)}, f32[602,512]{1,0:T(8,128)}, u32[]{:S(2)}) copy-start(f32[602,512]{1,0:T(8,128)} %param.38) | copy-start | bytes 3698692
  677.8 4.4 copy-start.3
  677.8 4.4 copy-start.8
  677.8 4.4 copy-start.9
  677.8 5.5 copy-start.15
  683.4 4.0 copy-start.12
  683.4 5.1 copy-start.13
  683.4 5.7 copy-start.14
  (10 other events, 25.9 us)
Sparse Core Ops, SparseCore 0:
  516.9 153.3 all-reduce.3

commit v2 on v0

v2 whole, which is shorter than its diff:
```python
import functools

import jax
import jax.numpy as jnp
from jax import lax
from jax.experimental import pallas as pl
from jax.experimental.pallas import tpu as pltpu
from jax.sharding import PartitionSpec as P

norm_eps = 1e-06
learn_rate = 0.03
beta_one = 0.9
beta_two = 0.999
adam_eps = 1e-08
decay_rate = 0.01
adam_step = 10.0

PLANES = 4
KINDS = 4
CHUNKS = 8
PARTS = 2
AHEAD = 3
LEAD = 1
UNROLL = False
LANES = 128
MESH = pl.DeviceIdType.MESH


def to_half(value):
    return value.astype(jnp.bfloat16)


def mat_product(former, latter):
    return jnp.dot(former, latter, preferred_element_type=jnp.float32)


def left_product(former, latter):
    return lax.dot_general(
        former, latter, (((0,), (0,)), ((), ())), preferred_element_type=jnp.float32
    )


def right_product(former, latter):
    return lax.dot_general(
        former, latter, (((1,), (1,)), ((), ())), preferred_element_type=jnp.float32
    )


def adam_update(weight, grad, first, second):
    first_new = beta_one * first + (1.0 - beta_one) * grad
    second_new = beta_two * second + (1.0 - beta_two) * grad * grad
    first_hat = first_new / (1.0 - beta_one**adam_step)
    second_hat = second_new / (1.0 - beta_two**adam_step)
    weight_new = weight - learn_rate * (
        first_hat / (jnp.sqrt(second_hat) + adam_eps) + decay_rate * weight
    )
    return (weight_new, first_new, second_new)


def place(me, plane_size):
    z = me // plane_size
    spot = me % plane_size
    inner = (z % 2 + z // 2) % 2
    near = z + 1 - 2 * (z % 2)
    far_in = 2 - z // 2
    far_out = 3 * (1 - z // 2)
    return z, spot, inner, near, far_in, far_out


class Summer:
    STEPS = 7

    def __init__(self, n, shape):
        self.n, (self.rows, self.width) = n, shape
        self.size = n // PLANES
        self.chips = self.size // 2
        self.half = self.width // 2
        self.cuts = min(self.half // LANES, self.chips)
        self.cut = self.half // self.cuts
        self.bands = self.chips // self.cuts
        self.band = self.rows // self.bands
        self.shard = self.band // PLANES

    @staticmethod
    def padded(n, rows, width):
        summer = Summer(n, (rows, width))
        unit = summer.bands * PLANES * 8
        return -(-rows // unit) * unit

    def scratch(self):
        f32 = jnp.float32
        return [
            pltpu.VMEM((self.rows, self.half), f32),
            pltpu.VMEM((self.chips - 1, self.band, self.cut), f32),
            pltpu.VMEM((PLANES - 1, self.shard, self.cut), f32),
            pltpu.SemaphoreType.DMA((6,)),
            pltpu.SemaphoreType.DMA((6,)),
        ]

    def bind(self, part, total, refs):
        self.part, self.total = part, total
        self.from_core, self.from_chip, self.from_plane, self.sent, self.got = refs
        me = lax.axis_index("nodes")
        self.z, spot = me // self.size, me % self.size
        self.chip, self.core = spot // 2, spot % 2
        self.mine = pl.ds(pl.multiple_of(self.core * self.half, LANES), self.half)
        self.other = pl.ds(pl.multiple_of((1 - self.core) * self.half, LANES), self.half)

    def device(self, z, chip, core):
        return z * self.size + chip * 2 + core

    def plane_peers(self):
        found = [self.device(self.z, self.chip, 1 - self.core)]
        for hop in range(1, self.chips):
            found.append(self.device(self.z, lax.rem(self.chip + hop, self.chips), self.core))
        return found

    def column_peers(self):
        return [
            self.device(lax.rem(self.z + hop, PLANES), self.chip, self.core)
            for hop in range(1, PLANES)
        ]

    def patch(self, chip):
        row = pl.multiple_of((chip // self.cuts) * self.band, 8)
        col = self.core * self.half + (chip % self.cuts) * self.cut
        return row, pl.ds(pl.multiple_of(col, LANES), self.cut)

    def copy(self, hop, src, dst, device):
        return pltpu.make_async_remote_copy(
            src_ref=src,
            dst_ref=dst,
            send_sem=self.sent.at[hop],
            recv_sem=self.got.at[hop],
            device_id=(device,),
            device_id_type=MESH,
        )

    @staticmethod
    def settle(sem, held):
        pltpu.make_async_copy(held, held, sem).wait()

    def step(self, at):
        part, total = self.part, self.total
        across = self.device(self.z, self.chip, 1 - self.core)
        row, cols = self.patch(self.chip)
        band = pl.ds(row, self.band)
        rows = pl.ds(pl.multiple_of(row + self.z * self.shard, 8), self.shard)
        if at == 0:
            self.copy(0, part.at[:, self.other], self.from_core, across).start()
        elif at == 1:
            self.settle(self.got.at[0], self.from_core)
            part[:, self.mine] += self.from_core[...]
            for hop in range(1, self.chips):
                chip = lax.rem(self.chip + hop, self.chips)
                there, cut = self.patch(chip)
                src = part.at[pl.ds(there, self.band), cut]
                dst = self.from_chip.at[hop - 1]
                self.copy(1, src, dst, self.device(self.z, chip, self.core)).start()
        elif at == 2:
            self.settle(self.got.at[1], self.from_chip)
            held = part[band, cols]
            for hop in range(1, self.chips):
                held = held + self.from_chip[hop - 1]
            part[band, cols] = held
            for hop in range(1, PLANES):
                z = lax.rem(self.z + hop, PLANES)
                there = pl.multiple_of(row + z * self.shard, 8)
                src = part.at[pl.ds(there, self.shard), cols]
                dst = self.from_plane.at[hop - 1]
                self.copy(2, src, dst, self.device(z, self.chip, self.core)).start()
        elif at == 3:
            self.settle(self.got.at[2], self.from_plane)
            held = part[rows, cols]
            for hop in range(1, PLANES):
                held = held + self.from_plane[hop - 1]
            total[rows, cols] = held
            for hop in range(1, PLANES):
                z = lax.rem(self.z + hop, PLANES)
                held = total.at[rows, cols]
                self.copy(3, held, held, self.device(z, self.chip, self.core)).start()
        elif at == 4:
            self.settle(self.got.at[3], self.from_plane)
            for hop in range(1, self.chips):
                chip = lax.rem(self.chip + hop, self.chips)
                held = total.at[band, cols]
                self.copy(4, held, held, self.device(self.z, chip, self.core)).start()
        elif at == 5:
            self.settle(self.got.at[4], self.from_chip)
            held = total.at[:, self.mine]
            self.copy(5, held, held, across).start()
        else:
            self.settle(self.got.at[5], self.from_core)
            self.settle(self.sent.at[0], self.from_core)
            self.settle(self.sent.at[1], self.from_chip)
            self.settle(self.sent.at[2], self.from_plane)
            self.settle(self.sent.at[3], self.from_plane)
            self.settle(self.sent.at[4], self.from_chip)
            self.settle(self.sent.at[5], self.from_core)


def finish_kernel(n, tile, rows, grads, total, part, *refs):
    summer = Summer(n, part.shape)
    summer.bind(part, total, refs)
    barrier = pltpu.get_barrier_semaphore()
    peers = summer.plane_peers() + summer.column_peers()
    for peer in peers:
        pl.semaphore_signal(barrier, inc=1, device_id=(peer,), device_id_type=MESH)
    count, depth = rows.shape

    def multiply(cols):
        part[:, cols] = jnp.zeros((part.shape[0], summer.half), jnp.float32)

        def add(at, carry):
            window = pl.ds(pl.multiple_of(at * tile, tile), tile)
            part[:count, cols] += mat_product(rows[:, window], grads[window, cols])
            return carry

        lax.fori_loop(0, depth // tile, add, 0)

    multiply(summer.other)
    pl.semaphore_wait(barrier, len(peers))
    summer.step(0)
    multiply(summer.mine)
    for at in range(1, Summer.STEPS):
        summer.step(at)


def finish(n, rows, grads, collective):
    shape = (Summer.padded(n, rows.shape[0], grads.shape[1]), grads.shape[1])
    vmem = pl.BlockSpec(memory_space=pltpu.VMEM)
    return pl.pallas_call(
        functools.partial(finish_kernel, n, 1024),
        out_shape=jax.ShapeDtypeStruct(shape, jnp.float32),
        in_specs=[vmem, vmem],
        out_specs=vmem,
        scratch_shapes=[pltpu.VMEM(shape, jnp.float32)] + Summer(n, shape).scratch(),
        compiler_params=pltpu.CompilerParams(
            collective_id=collective, has_side_effects=True, vmem_limit_bytes=40 * 2**20
        ),
        name="finish",
    )(rows, grads)


class Exchange:
    def __init__(self, n, slots, far_cap, near_cap, shape, kind):
        self.n, self.slots = n, slots
        self.far_cap, self.near_cap = far_cap, near_cap
        self.size = n // PLANES
        self.blocks, self.depth, self.width = shape
        self.kind = kind
        self.rows = self.depth // CHUNKS
        self.cols = self.width // PARTS
        self.steps = CHUNKS * PARTS
        self.ring = self.steps if self.size <= 8 else 2

    def out_shape(self):
        return jax.ShapeDtypeStruct(
            (CHUNKS, self.size, KINDS, self.slots, self.rows, self.width), self.kind
        )

    def scratch(self):
        def piece(*lead):
            return pltpu.VMEM(lead + (self.rows, self.cols), self.kind)

        steps, ring = self.steps, self.ring
        dma = pltpu.SemaphoreType.DMA
        return (
            [piece(self.far_cap) for _ in range(steps)]
            + [piece(self.near_cap) for _ in range(2 * steps)]
            + [piece(self.far_cap) for _ in range(2 * steps)]
            + [piece(self.near_cap) for _ in range(2 * steps)]
            + [piece(self.size, 2, self.slots) for _ in range(2 * ring)]
            + [dma((steps,)), dma((steps,)), dma((steps,)), dma((2, steps)), dma((2, steps))]
            + [dma((2, ring)), dma((CHUNKS,))]
        )

    def bind(self, plan, table, out, refs):
        self.plan, self.table, self.out = plan, table, out
        rest = list(refs)
        steps = self.steps

        def take(count):
            found = rest[:count]
            del rest[:count]
            return found

        self.far_stage = take(steps)
        self.near_stage = take(steps)
        self.near_got = take(steps)
        self.far_got = [take(steps), take(steps)]
        self.pass_stage = [take(steps), take(steps)]
        self.serve_stage = [take(self.ring), take(self.ring)]
        (
            self.far_sent,
            self.near_sent,
            self.near_recv,
            self.far_recv,
            self.pass_sent,
            self.serve_sent,
            self.serve_recv,
        ) = rest
        me = lax.axis_index("nodes")
        self.z, self.spot, self.inner, near, far_in, far_out = place(me, self.size)
        self.near_dev = near * self.size + self.spot
        self.relay_dev = far_in * self.size + self.spot
        self.outer_dev = far_out * self.size + self.spot

    def greet(self, column=False):
        barrier = pltpu.get_barrier_semaphore()

        def hello(device):
            pl.semaphore_signal(barrier, inc=1, device_id=(device,), device_id_type=MESH)

        def in_plane(step, carry):
            hello(self.z * self.size + lax.rem(self.spot + step, self.size))
            return carry

        lax.fori_loop(1, self.size, in_plane, 0)
        if column:
            for hop in range(1, PLANES):
                hello(lax.rem(self.z + hop, PLANES) * self.size + self.spot)
            pl.semaphore_wait(barrier, self.size - 1 + PLANES - 1)
            return
        hello(self.near_dev)

        @pl.when(self.inner == 1)
        def _():
            hello(self.relay_dev)
            hello(self.outer_dev)

        pl.semaphore_wait(barrier, self.size + 1)

    def window(self, step):
        return pl.ds((step // PARTS) * self.rows, self.rows), pl.ds(
            (step % PARTS) * self.cols, self.cols
        )

    def remote(self, src, dst, sent, got, device):
        return pltpu.make_async_remote_copy(
            src_ref=src,
            dst_ref=dst,
            send_sem=sent,
            recv_sem=got,
            device_id=(device,),
            device_id_type=MESH,
        )

    @staticmethod
    def settle(sem, held):
        pltpu.make_async_copy(held, held, sem).wait()

    def launch(self, step):
        rows, cols = self.window(step)
        plan, table = self.plan, self.table
        far_stage, near_stage = self.far_stage[step], self.near_stage[step]

        def fill_far(at, carry):
            far_stage[at] = table[plan[ROW_FAR, at], rows, cols]
            return carry

        def fill_near(at, carry):
            near_stage[at] = table[plan[ROW_NEAR, at], rows, cols]
            return carry

        lax.fori_loop(0, self.far_cap, fill_far, 0, unroll=UNROLL)
        for lane in range(2):

            @pl.when(self.inner == 1 - lane)
            def _():
                self.remote(
                    far_stage,
                    self.far_got[lane][step],
                    self.far_sent.at[step],
                    self.far_recv.at[lane, step],
                    self.relay_dev,
                ).start()

        lax.fori_loop(0, self.near_cap, fill_near, 0, unroll=UNROLL)
        self.remote(
            near_stage,
            self.near_got[step],
            self.near_sent.at[step],
            self.near_recv.at[step],
            self.near_dev,
        ).start()

    def relay(self, step):
        plan = self.plan

        @pl.when(self.inner == 1)
        def _():
            for lane in range(2):
                got, stage = self.far_got[lane][step], self.pass_stage[lane][step]
                self.settle(self.far_recv.at[lane, step], got)

                def fill(at, carry):
                    stage[at] = got[plan[ROW_PASS + lane, at]]
                    return carry

                lax.fori_loop(0, self.near_cap, fill, 0, unroll=UNROLL)
                self.remote(
                    stage,
                    got.at[pl.ds(0, self.near_cap)],
                    self.pass_sent.at[lane, step],
                    self.far_recv.at[lane, step],
                    self.near_dev,
                ).start()

        @pl.when(self.inner == 0)
        def _():
            for lane in range(2):
                got = self.far_got[lane][step].at[pl.ds(0, self.near_cap)]
                self.settle(self.far_recv.at[lane, step], got)

    def serve(self, step, pair):
        rows, cols = self.window(step)
        plan, table, slots, size = self.plan, self.table, self.slots, self.size
        chunk, slot_at = step // PARTS, step % self.ring
        if pair == 0:
            self.settle(self.near_recv.at[step], self.near_got[step])
        if step >= self.ring:
            self.drain(step - self.ring, pair)
        stage = self.serve_stage[pair][slot_at]

        def fill(peer, carry):
            taker = self.z * size + peer
            for slot in range(slots):
                first = plan[ROW_SERVE + 2 * pair * slots + slot, taker]
                second = plan[ROW_SERVE + (2 * pair + 1) * slots + slot, taker]
                if pair == 0:
                    stage[peer, 0, slot] = table[first, rows, cols]
                    stage[peer, 1, slot] = self.near_got[step][second]
                else:
                    stage[peer, 0, slot] = self.far_got[0][step][first]
                    stage[peer, 1, slot] = self.far_got[1][step][second]
            return carry

        lax.fori_loop(0, size, fill, 0)
        there = self.out.at[chunk, self.spot, pl.ds(2 * pair, 2), :, :, cols]
        pltpu.make_async_copy(stage.at[self.spot], there, self.serve_recv.at[chunk]).start()

        def send(hop, carry):
            peer = lax.rem(self.spot + hop, size)
            self.remote(
                stage.at[peer],
                there,
                self.serve_sent.at[pair, slot_at],
                self.serve_recv.at[chunk],
                self.z * size + peer,
            ).start()
            return carry

        lax.fori_loop(1, size, send, 0)

    def drain(self, step, pair):
        slot_at = step % self.ring
        held = self.serve_stage[pair][slot_at].at[pl.ds(0, self.size - 1)]
        self.settle(self.serve_sent.at[pair, slot_at], held)

    def run(self, side=None):
        steps = self.steps
        for step in range(min(AHEAD, steps)):
            self.launch(step)
        for step in range(min(LEAD, steps)):
            self.serve(step, 0)
        for step in range(steps):
            if step + AHEAD < steps:
                self.launch(step + AHEAD)
            self.relay(step)
            self.serve(step, 1)
            if step + LEAD < steps:
                self.serve(step + LEAD, 0)
            if side is not None:
                side(step)
        for chunk in range(CHUNKS):
            self.settle(self.serve_recv.at[chunk], self.out.at[chunk])
        for step in range(max(0, steps - self.ring), steps):
            self.drain(step, 0)
            self.drain(step, 1)
        for step in range(steps):
            self.settle(self.far_sent.at[step], self.far_stage[step])
            self.settle(self.near_sent.at[step], self.near_stage[step])

        @pl.when(self.inner == 1)
        def _():
            for step in range(steps):
                for lane in range(2):
                    self.settle(self.pass_sent.at[lane, step], self.pass_stage[lane][step])


def exchange_kernel(moves, plan, table, out, *refs):
    moves.bind(plan, table, out, refs)
    moves.greet()
    moves.run()


def exchange_sum_kernel(moves, summer, plan, table, part, out, total, held, sem, *refs):
    moves.bind(plan, table, out, refs[5:])
    summer.bind(held, total, refs[:5])
    fetch = pltpu.make_async_copy(part, held, sem)
    fetch.start()
    moves.greet(column=True)

    def side(step):
        if step == 0:
            fetch.wait()
        at = step // PARTS
        if step % PARTS == 0 and at < Summer.STEPS:
            summer.step(at)

    moves.run(side)


def exchange(n, slots, far_cap, near_cap, collective, plan, table, part=None):
    moves = Exchange(n, slots, far_cap, near_cap, table.shape, table.dtype)
    hbm = pl.BlockSpec(memory_space=pl.ANY)
    vmem = pl.BlockSpec(memory_space=pltpu.VMEM)
    in_specs = [pl.BlockSpec(memory_space=pltpu.SMEM), vmem]
    params = pltpu.CompilerParams(
        collective_id=collective, has_side_effects=True, vmem_limit_bytes=60 * 2**20
    )
    if part is None:
        return pl.pallas_call(
            functools.partial(exchange_kernel, moves),
            out_shape=moves.out_shape(),
            in_specs=in_specs,
            out_specs=hbm,
            scratch_shapes=moves.scratch(),
            compiler_params=params,
            name="exchange",
        )(plan, table)
    summer = Summer(n, part.shape)
    return pl.pallas_call(
        functools.partial(exchange_sum_kernel, moves, summer),
        out_shape=(moves.out_shape(), jax.ShapeDtypeStruct(part.shape, jnp.float32)),
        in_specs=in_specs + [hbm],
        out_specs=(hbm, vmem),
        scratch_shapes=[pltpu.VMEM(part.shape, jnp.float32), pltpu.SemaphoreType.DMA]
        + summer.scratch()
        + moves.scratch(),
        compiler_params=params,
        name="exchange_sum",
    )(plan, table, part)


def gather_sum_kernel(flip, slots, first_row, sinks, weights, got, *refs):
    out, total = refs[-2:]
    at = pl.program_id(0)
    size = pl.num_programs(0)
    z, _, _, near, far_in, far_out = place(lax.axis_index("nodes"), size)

    @pl.when(at == 0)
    def _():
        total[...] = jnp.zeros_like(total)

    blocks, depth, width = total.shape
    if flip:
        own, mixer = refs[:2]
        span = own.shape[0] // depth
        base = right_product(own[...], mixer[...]).reshape(span, depth, width)
        total[pl.ds(at * span, span)] += base
    for kind, owner_z in enumerate((z, near, far_in, far_out)):
        for slot in range(slots):
            sink = sinks[first_row + slot, owner_z * size + at]

            @pl.when(sink < blocks)
            def _():
                edge = weights[owner_z, 0, slot]
                rows = got[:, 0, kind, slot].reshape(depth, width)
                dims = (((0,), (0,)), ((), ())) if flip else (((1,), (0,)), ((), ()))
                total[sink] += lax.dot_general(
                    edge, rows, dims, preferred_element_type=jnp.float32
                )

    @pl.when(at == pl.num_programs(0) - 1)
    def _():
        out[...] = total[...].astype(out.dtype)


def gather_sum(flip, first_row, sinks, weights, got, blocks, *base):
    chunks, size, _, slots, rows, width = got.shape
    depth = chunks * rows
    edges = weights.reshape(PLANES, size, slots, depth, depth)
    tile = blocks * depth // size
    base_specs = [
        pl.BlockSpec((tile, width), lambda at, sinks: (at, 0)),
        pl.BlockSpec((width, width), lambda at, sinks: (0, 0)),
    ]
    return pl.pallas_call(
        functools.partial(gather_sum_kernel, flip, slots, first_row),
        out_shape=jax.ShapeDtypeStruct((blocks, depth, width), jnp.bfloat16),
        grid_spec=pltpu.PrefetchScalarGridSpec(
            num_scalar_prefetch=1,
            grid=(size,),
            in_specs=[
                pl.BlockSpec(
                    (PLANES, 1, slots, depth, depth), lambda at, sinks: (0, at, 0, 0, 0)
                ),
                pl.BlockSpec(
                    (chunks, 1, KINDS, slots, rows, width),
                    lambda at, sinks: (0, at, 0, 0, 0, 0),
                ),
            ]
            + base_specs[: len(base)],
            out_specs=pl.BlockSpec((blocks, depth, width), lambda at, sinks: (0, 0, 0)),
            scratch_shapes=[pltpu.VMEM((blocks, depth, width), jnp.float32)],
        ),
        compiler_params=pltpu.CompilerParams(vmem_limit_bytes=40 * 2**20),
        name="gather_sum",
    )(sinks, edges, got, *base)


ROW_FAR, ROW_NEAR, ROW_PASS, ROW_SERVE = 0, 1, 2, 4


def plan_rows(slots):
    wishes = ROW_SERVE + KINDS * slots
    return wishes, wishes + slots, -(-(wishes + slots + 1) // 8) * 8


def column(values, lane):
    lanes = lax.broadcasted_iota(jnp.int32, values.shape, 1)
    return jnp.sum(jnp.where(lanes == lane, values, 0.0), axis=1, keepdims=True)


def lay_plan(n, slots, blocks, rungs, way, wishes_of, plan, present):
    size = n // PLANES
    me = lax.axis_index("nodes")
    z, spot, inner, near, far_in, far_out = place(me, size)
    half = z // 2
    row_wish, row_rung, _ = plan_rows(slots)

    taker = lax.broadcasted_iota(jnp.int32, (LANES, LANES), 0)
    group = lax.broadcasted_iota(jnp.int32, (LANES, LANES), 1)
    plane_of = taker // size
    member = (taker < n) & ((plane_of == group) | (plane_of // 2 + PLANES == group))
    member = jnp.where(member, 1.0, 0.0).astype(jnp.bfloat16)
    hits = jnp.zeros((n * blocks, LANES), jnp.float32)
    for slot in range(slots):
        wish = wishes_of[slot][...]
        ids = lax.broadcasted_iota(jnp.int32, (n, blocks, LANES), 1)
        hot = jnp.where(wish[:, None, :] == ids, 1.0, 0.0).astype(jnp.bfloat16)
        hits = hits + mat_product(hot.reshape(n * blocks, LANES), member)
    here = jnp.where(hits > 0.0, 1.0, 0.0)
    present[...] = here
    counts = jnp.sum(here.reshape(n, blocks, LANES), axis=1)
    owner_plane = lax.broadcasted_iota(jnp.int32, (n, LANES), 0) // size
    lane = lax.broadcasted_iota(jnp.int32, (n, LANES), 1)
    is_near = (lane < PLANES) & (lane != owner_plane)
    is_far = (lane >= PLANES) & (lane < PLANES + 2) & (lane - PLANES != owner_plane // 2)
    near_most = jnp.max(jnp.where(is_near, counts, 0.0), axis=(0, 1), keepdims=True)
    far_most = jnp.max(jnp.where(is_far, counts, 0.0), axis=(0, 1), keepdims=True)
    rung = jnp.zeros((1, 1), jnp.float32)
    for far_cap, near_cap in rungs[:-1]:
        over = (far_most > float(far_cap)) | (near_most > float(near_cap))
        rung = rung + jnp.where(over, 1.0, 0.0)

    def put(row, values):
        plan[way, pl.ds(row, 1), :] = values.astype(jnp.int32)

    put(row_rung, jnp.broadcast_to(rung, (1, LANES)))
    block_id = lax.broadcasted_iota(jnp.int32, (blocks, LANES), 0)
    block_lane = lax.broadcasted_iota(jnp.int32, (blocks, LANES), 1)
    ids = block_id.astype(jnp.float32)
    below = lax.broadcasted_iota(jnp.int32, (blocks, blocks), 0) > lax.broadcasted_iota(
        jnp.int32, (blocks, blocks), 1
    )
    below = jnp.where(below, 1.0, 0.0).astype(jnp.bfloat16)

    def listed(chosen, pos, values):
        at = (chosen > 0.0) & (pos.astype(jnp.int32) == block_lane)
        return jnp.sum(jnp.where(at, values, 0.0), axis=0, keepdims=True)

    for kind, owner_z in enumerate((z, near, far_in, far_out)):
        owner = owner_z * size + spot
        mine = present[pl.ds(pl.multiple_of(owner * blocks, 8), blocks), :]
        rank = mat_product(below, mine.astype(jnp.bfloat16))
        if kind == 0:
            where_held = ids
            far = PLANES + 1 - half
            put(ROW_FAR, listed(column(mine, far), column(rank, far), ids))
            put(ROW_NEAR, listed(column(mine, near), column(rank, near), ids))
        elif kind == 1:
            where_held = column(rank, z)
        else:
            where_held = column(rank, z + inner * (PLANES + half - z))
            edge = 3 * half
            put(
                ROW_PASS + kind - 2,
                listed(column(mine, edge), column(rank, edge), column(rank, PLANES + half)),
            )
        for slot in range(slots):
            wish = wishes_of[slot][pl.ds(owner, 1), :]
            held = jnp.where(wish == block_id, where_held, 0.0)
            put(ROW_SERVE + kind * slots + slot, jnp.sum(held, axis=0, keepdims=True))
            if kind == 0:
                put(row_wish + slot, wish)


def prelude_kernel(n, slots, blocks, rungs, tile, *refs):
    mine, rows, weight, hidden, plan, taken = refs[:6]
    wishes = refs[6 : 6 + 2 * slots]
    present, send_sem, recv_sem = refs[6 + 2 * slots :]
    me = lax.axis_index("nodes")
    barrier = pltpu.get_barrier_semaphore()

    def greet(step, carry):
        pl.semaphore_signal(
            barrier, inc=1, device_id=(lax.rem(me + step, n),), device_id_type=MESH
        )
        return carry

    lax.fori_loop(1, n, greet, 0)
    taken[me] = mine[...]
    pl.semaphore_wait(barrier, n - 1)

    def send(step, carry):
        pltpu.make_async_remote_copy(
            src_ref=mine,
            dst_ref=taken.at[me],
            send_sem=send_sem,
            recv_sem=recv_sem,
            device_id=(lax.rem(me + step, n),),
            device_id_type=MESH,
        ).start()
        return carry

    lax.fori_loop(1, n, send, 0)
    half_weight = to_half(weight[...])

    def project(at, carry):
        window = pl.ds(pl.multiple_of(at * tile, tile), tile)
        hidden[window, :] = to_half(left_product(rows[:, window], half_weight))
        return carry

    lax.fori_loop(0, rows.shape[1] // tile, project, 0)
    others = taken.at[pl.ds(0, n - 1)]
    pltpu.make_async_copy(others, others, recv_sem).wait()
    pltpu.make_async_copy(others, others, send_sem).wait()

    every = taken[...].reshape(n, 2 * slots * LANES)
    unit = lax.broadcasted_iota(jnp.int32, (n, LANES), 0) == lax.broadcasted_iota(
        jnp.int32, (n, LANES), 1
    )
    unit = jnp.where(unit, 1.0, 0.0).astype(jnp.bfloat16)
    for slot in range(slots):
        part = every[:, slot * LANES : (slot + 1) * LANES]
        turned = left_product(part.astype(jnp.float32).astype(jnp.bfloat16), unit)
        wishes[slot][...] = turned[:n].astype(jnp.int32)
        wishes[slots + slot][...] = every[:, (slots + slot) * LANES : (slots + slot + 1) * LANES]
    for way in range(2):
        lay_plan(
            n,
            slots,
            blocks,
            rungs,
            way,
            wishes[way * slots : (way + 1) * slots],
            plan,
            present,
        )


def prelude(n, slots, blocks, rungs, mine, rows, weight):
    count, width = rows.shape[1], weight.shape[1]
    vmem = pl.BlockSpec(memory_space=pltpu.VMEM)
    plan_shape = (2, plan_rows(slots)[2], LANES)
    return pl.pallas_call(
        functools.partial(prelude_kernel, n, slots, blocks, rungs, 512),
        out_shape=(
            jax.ShapeDtypeStruct((count, width), jnp.bfloat16),
            jax.ShapeDtypeStruct(plan_shape, jnp.int32),
        ),
        in_specs=[vmem, vmem, vmem],
        out_specs=(vmem, vmem),
        scratch_shapes=[pltpu.VMEM((n,) + mine.shape, jnp.int32)]
        + [pltpu.VMEM((n, LANES), jnp.int32) for _ in range(2 * slots)]
        + [
            pltpu.VMEM((n * blocks, LANES), jnp.float32),
            pltpu.SemaphoreType.DMA,
            pltpu.SemaphoreType.DMA,
        ],
        compiler_params=pltpu.CompilerParams(
            collective_id=0, has_side_effects=True, vmem_limit_bytes=40 * 2**20
        ),
        name="prelude",
    )(mine, rows, weight)


def shards(
    features,
    labels,
    labelled,
    label_count,
    need_blocks,
    need_count,
    target_block,
    adjacency,
    embed_weight,
    pair_weight,
    merge_weight,
    head_weight,
    embed_moment,
    pair_moment,
    merge_moment,
    head_moment,
    embed_variance,
    pair_variance,
    merge_variance,
    head_variance,
):
    row_count = features.shape[0]
    hidden_width = embed_weight.shape[1]
    block_rows = adjacency.shape[1]
    slots = need_blocks.shape[2]
    n = lax.axis_size("nodes")
    size = n // PLANES
    block_count = row_count // block_rows
    alive = lax.broadcasted_iota(jnp.int32, need_blocks.shape[1:], 1) < need_count[0][:, None]
    raw = jnp.stack([need_blocks[0], target_block[0]])
    raw = jnp.where(alive, raw, block_count).transpose(0, 2, 1).reshape(2 * slots, n)
    raw = jnp.pad(raw, ((0, 0), (0, LANES - n)), constant_values=block_count)
    near_full = min(block_count, size * slots)
    rungs = [(min(23, block_count), min(15, near_full)), (block_count, near_full)]
    if near_full > 16:
        rungs = rungs[1:]
    hidden_half, plan = prelude(
        n, slots, block_count, rungs, raw.reshape(1, 2 * slots * LANES), features.T, embed_weight
    )
    row_wish, row_rung, _ = plan_rows(slots)

    def swap(way, *held):
        def at(rung):
            far_cap, near_cap = rungs[rung]
            return lambda *held: exchange(
                n, slots, far_cap, near_cap, 2 + way * len(rungs) + rung, *held
            )

        if len(rungs) == 1:
            return at(0)(plan[way], *held)
        branches = [at(rung) for rung in range(len(rungs))]
        return lax.switch(plan[way, row_rung, 0], branches, plan[way], *held)

    pair_half = to_half(pair_weight)
    merge_half = to_half(merge_weight)
    head_half = to_half(head_weight)
    got = swap(0, hidden_half.reshape(block_count, block_rows, hidden_width))
    gathered = gather_sum(
        False, slots, raw, adjacency, got, block_count
    ).reshape(row_count, hidden_width)
    adjacency_later, gathered = lax.optimization_barrier((adjacency, gathered))
    edges_back = lax.all_to_all(adjacency_later, "nodes", split_axis=0, concat_axis=0, tiled=True)

    self_part = mat_product(hidden_half, pair_half[0, 0])
    neigh_part = mat_product(gathered, pair_half[0, 1])
    joined = to_half(jnp.concatenate([self_part, neigh_part], axis=1))
    linear = mat_product(joined, merge_half[0])
    active = linear * jax.nn.sigmoid(linear)
    scale = lax.rsqrt(jnp.sum(active * active, axis=1, keepdims=True) + norm_eps)
    output = active * scale
    final_half = to_half(output)
    logits = mat_product(final_half, head_half)
    truth = labels.astype(jnp.float32)
    row_mask = labelled.astype(jnp.float32)[:, None]
    denom = label_count[0].astype(jnp.float32) * logits.shape[1]
    per_entry = jnp.maximum(logits, 0.0) - logits * truth + jnp.log1p(jnp.exp(-jnp.abs(logits)))
    loss_part = jnp.sum(per_entry * row_mask) / denom
    grad_logits = to_half((jax.nn.sigmoid(logits) - truth) * row_mask / denom)
    head_grad = left_product(final_half, grad_logits)
    grad_out = right_product(grad_logits, head_half)
    grad_active = scale * (grad_out - output * jnp.sum(grad_out * output, axis=1, keepdims=True))
    sig_value = jax.nn.sigmoid(linear)
    grad_linear = to_half(grad_active * sig_value * (1.0 + linear * (1.0 - sig_value)))
    merge_grad = left_product(joined, grad_linear)
    grad_joined = to_half(right_product(grad_linear, merge_half[0]))
    grad_self_out = grad_joined[:, :hidden_width]
    grad_neigh_out = grad_joined[:, hidden_width:]
    grad_self = left_product(hidden_half, grad_self_out)
    grad_neigh = left_product(gathered, grad_neigh_out)
    grad_gathered = to_half(right_product(grad_neigh_out, pair_half[0, 1]))
    label_width = head_grad.shape[1]
    spread = jnp.zeros((hidden_width, LANES - label_width), jnp.float32)
    spread = spread.at[0, 0].set(loss_part)
    head_wide = jnp.concatenate([head_grad, spread], axis=1).reshape(-1, hidden_width)
    part = jnp.concatenate([grad_self, grad_neigh, merge_grad, head_wide], axis=0)
    part_rows = Summer.padded(n, part.shape[0], hidden_width)
    part = jnp.pad(part, ((0, part_rows - part.shape[0]), (0, 0)))
    back, total = swap(1, grad_gathered.reshape(block_count, block_rows, hidden_width), part)
    pair_grad = total[: 2 * hidden_width].reshape(pair_weight.shape)
    merge_grad = total[2 * hidden_width : 4 * hidden_width].reshape(merge_weight.shape)
    head_wide = total[4 * hidden_width : 4 * hidden_width + head_wide.shape[0]]
    head_wide = head_wide.reshape(hidden_width, LANES)
    head_grad = head_wide[:, :label_width]
    loss_total = head_wide[0, label_width]

    grad_hidden = gather_sum(
        True, row_wish, plan[0], edges_back, back, block_count, grad_joined, pair_half[0, 0]
    ).reshape(row_count, hidden_width)
    embed_grad = finish(n, features.T, grad_hidden, 1)[: features.shape[1]]
    pair_next = adam_update(pair_weight, pair_grad, pair_moment, pair_variance)
    merge_next = adam_update(merge_weight, merge_grad, merge_moment, merge_variance)
    head_next = adam_update(head_weight, head_grad, head_moment, head_variance)
    embed_next = adam_update(embed_weight, embed_grad, embed_moment, embed_variance)
    return (
        loss_total.reshape(1),
        embed_next[0],
        pair_next[0],
        merge_next[0],
        head_next[0],
        embed_next[1],
        pair_next[1],
        merge_next[1],
        head_next[1],
        embed_next[2],
        pair_next[2],
        merge_next[2],
        head_next[2],
    )


def solution(mesh):
    split = ("nodes",)
    return jax.shard_map(
        shards,
        mesh=mesh,
        in_specs=(
            P("nodes", None),
            P("nodes", None),
            P("nodes"),
            P(),
            P("nodes", None, None),
            P("nodes", None),
            P("nodes", None, None),
            P("nodes", None, None),
        )
        + (P(),) * 12,
        out_specs=(P(),) * 13,
        check_vma=False,
    )
```

time: 898 us -> 541 us (0.60)
  waiting for transfers between devices: 448 us -> 0.01 us
  Pallas kernels: 0 us -> 419 us
  other arithmetic: 216 us -> 25.7 us
  blocking collectives: 39.3 us -> 0 us
  local copies, waits for them, and re-layouts: 53.2 us -> 15.1 us
  matrix products: 102 us -> 65.5 us
  starting transfers between devices: 17.5 us -> 4.59 us
  between operations: 16.4 us -> 3.82 us
    pallas_call x0 -> x6, Pallas kernels: none -> 419 us  [the longest x1 192 us: exchange(): pl.pallas_call(functools.partial(exchange_sum_kernel, moves, summer), out...]
    all_to_all x3 -> x1, waiting for transfers between devices: 338 us -> 0.01 us  [shards(): lax.all_to_all(adjacency_later, 'nodes', split_axis=0, concat_axis=0, til...]
    scatter-add x2 -> x0, other arithmetic: 191 us -> none  [the longest x1 155 us: shards(): summed = jax.ops.segment_sum(flat_grads, asked, num_segments=block_count)]
    psum x1 -> x0, waiting for transfers between devices: 110 us -> none  [shards(): lax.psum((loss_part, embed_grad, pair_grad, merge_grad, head_grad), 'nodes')]
    psum x1 -> x0, blocking collectives: 39.3 us -> none  [shards(): lax.psum((loss_part, embed_grad, pair_grad, merge_grad, head_grad), 'nodes')]
    dot_general x2 -> x0, matrix products: 20.6 us -> none  [the longest x1 11.5 us: shards(): jnp.einsum('kab,kbh->kah', live_weights, received, preferred_element_type...]
    gather x2 -> x0, local copies, waits for them, and re-layouts: 15.5 us -> none  [the longest x1 7.77 us: shards(): outgoing = hidden_half.reshape(block_count, block_rows, hidden_width)[asked]]
    unnamed x72 -> x54, local copies, waits for them, and re-layouts: 19.4 us -> 5.78 us
  transfers between devices with their start and end apart: 4 -> 1, of which waited for: 3 -> 0; matrix products, arithmetic and copies ran while one was open for 5% -> 18% of each run, Pallas kernels for 0% -> 36%
where the time goes in v2:
time: 541 us; the launch traced here: 535 us
  Pallas kernels  419 us (77%)
  matrix products  65.5 us (12%)
  other arithmetic  25.7 us (5%)
  local copies, waits for them, and re-layouts  15.1 us (3%)
    pallas_call x1, Pallas kernels, exchange(): pl.pallas_call(functools.partial(exchange_sum_kernel, moves, summer), out...  192 us
    pallas_call x1, Pallas kernels, exchange(): pl.pallas_call(functools.partial(exchange_kernel, moves), out_shape=moves...  149 us
    pallas_call x1, Pallas kernels, finish(): pl.pallas_call(functools.partial(finish_kernel, n, 1024), out_shape=jax.S...  33.1 us
    pallas_call x2, Pallas kernels, gather_sum(): pl.pallas_call(functools.partial(gather_sum_kernel, flip, slots, first_ro...  30.3 us
    dot_general x4, matrix products, left_product(): lax.dot_general(former, latter, (((0,), (0,)), ((), ())), preferred_eleme...  25.1 us
    dot_general x4, matrix products, mat_product(): return jnp.dot(former, latter, preferred_element_type=jnp.float32)  21.7 us
    dot_general x3, matrix products, right_product(): lax.dot_general(former, latter, (((1,), (1,)), ((), ())), preferred_eleme...  18.6 us
    sub x4, other arithmetic, adam_update(): weight - learn_rate * (first_hat / (jnp.sqrt(second_hat) + adam_eps) + de...  16.4 us
  transfers between devices with their start and end apart: 1, of which 0 were waited for; matrix products, arithmetic and copies ran while one was open for 18% of the time, Pallas kernels for 36%

profile of v2, /device:TPU:0, one launch (start us, length us, event | category | flops | bytes accessed | tf_op | source)
XLA Modules:
  0.0 534.6 jit_solution(6899786115631311449)
XLA Ops:
  5.7 14.7 %prelude.1 = (bf16[4096,512]{1,0:T(8,128)(2,1)}, s32[2,16,128]{2,1,0:T(8,128)S(1)}) custom-call(s32[1,512]{1,0:T(1,128)S(1)} %bitcast.60, bf16[602,4096]{1,0:T(8,128)(2,1)S(1)} %bitcast.53, f32[602,512]{1,0:T(8,128)S(1)} %copy-done.1), custom_call_target="tpu_custom_call" | custom-call | tf_op jit(solution)/shard_map/prelude/pallas_call | solution.py:769
  22.2 149.3 %conditional.2 = (bf16[8,8,4,2,16,512]{5,4,3,2,1,0:T(8,128)(2,1)}) conditional(s32[]{:T(128)} %bitcast.8, (s32[16,128]{1,0:T(8,128)}, bf16[32,128,512]{2,1,0:T(8,128)(2,1)}) %tuple.73, (s32[16,128]{1,0:T(8,128)}, bf16[32,128,512]{2,1,0:T(8,128)(2,1)}) %tuple.74), branch_computations={%region_0.1_spmd, %region_1.2_spmd} | conditional | bytes 8 | solution.py:843
  22.3 149.3 %exchange.2 = bf16[8,8,4,2,16,512]{5,4,3,2,1,0:T(8,128)(2,1)} custom-call(s32[16,128]{1,0:T(8,128)} %get-tuple-element.102.plan, bf16[32,128,512]{2,1,0:T(8,128)(2,1)} %get-tuple-element.103.table), custom_call_target="tpu_custom_call" | custom-call | tf_op jit(solution)/shard_map/cond/branch_0_fun/exchange/pallas_call | solution.py:524
  171.5 12.5 %gather_sum.2 = bf16[32,128,512]{2,1,0:T(8,128)(2,1)S(1)} custom-call(s32[4,128]{1,0:T(4,128)S(1)} %pad.10.sinks, bf16[4,8,2,128,128]{4,3,2,1,0:T(8,128)(2,1)} %bitcast.7.weights, bf16[8,8,4,2,16,512]{5,4,3,2,1,0:T(8,128)(2,1)} %get-tuple-element.179.got), custom_call_target="tpu_custom_call" | custom-call | tf_op jit(solution)/shard_map/gather_sum/pallas_call | solution.py:590
  186.0 4.6 all-to-all-start
  190.8 5.0 convolution_convert_fusion.3
  195.8 4.3 convolution_convert_fusion.2
  200.1 8.1 %multiply_reduce_fusion.1 = (f32[4096]{0:T(1024)S(1)}, f32[4096,512]{0,1:T(8,128)S(1)}) fusion(f32[1,1024,512]{2,1,0:T(8,128)S(1)} %copy-done.9, bf16[4096,512]{0,1:T(8,128)(2,1)} %convolution_convert_fusion.2, bf16[4096,512]{0,1:T(8,128)(2,1)S(1)} %convolution_convert_fusion.3), kind=kOutput, calls=%fused_computation.5 | convolution fusion | flops 4324847616 | bytes 18890752 | tf_op jit(solution)/shard_map/dot_general | solution.py:34
  208.9 4.3 multiply_reduce_fusion.2
  213.3 3.3 multiply_reduce_fusion
  216.6 4.3 multiply_convert_fusion
  220.9 8.7 %convolution_convert_fusion.refs_0_ = bf16[4096,1024]{1,0:T(8,128)(2,1)} fusion(bf16[4096,512]{0,1:T(8,128)(2,1)S(1)} %multiply_convert_fusion, f32[1,1024,512]{2,1,0:T(8,128)} %param.36), kind=kOutput, calls=%fused_computation.8 | convolution fusion | flops 4299685888 | bytes 14680064 | tf_op jit(solution)/shard_map/dot_general | solution.py:44
  229.6 9.3 %fusion.1 = f32[1024,512]{1,0:T(8,128)} fusion(bf16[4096,512]{0,1:T(8,128)(2,1)S(1)} %multiply_convert_fusion, bf16[4096,512]{0,1:T(8,128)(2,1)} %convolution_convert_fusion.2, bf16[4096,512]{0,1:T(8,128)(2,1)} %copy-done.23), kind=kOutput, calls=%fused_computation.13 | convolution fusion | flops 4311744512 | bytes 14680064 | tf_op jit(solution)/shard_map/dot_general | solution.py:38
  238.9 6.5 %fusion.11 = f32[512,121]{0,1:T(8,128)} fusion(f32[4096]{0:T(1024)S(1)} %add_rsqrt_fusion, s32[4096,121]{1,0:T(8,128)} %param.27, f32[4096,121]{1,0:T(8,128)} %copy-done.24, f32[]{:T(128)} %bitcast.14, f32[4096]{0:T(1024)S(1)} %convert_element_type.40, f32[4096,512]{0,1:T(8,128)S(1)} %get-tuple-element.170), kind=kOutput, calls=%fused_computation.33 | convolution fusion | flops 524058624 | bytes 12634116 | tf_op jit(solution)/shard_map/dot_general | solution.py:38
  245.4 3.4 fusion.5
  252.9 5.9 %fusion.3 = f32[512,512]{1,0:T(8,128)S(1)} fusion(bf16[4096,512]{1,0:T(8,128)(2,1)} %get-tuple-element.136, bf16[4096,1024]{1,0:T(8,128)(2,1)} %convolution_convert_fusion.refs_0_), kind=kOutput, calls=%fused_computation.16 | convolution fusion | flops 2147483648 | bytes 9437184 | tf_op jit(solution)/shard_map/dot_general | solution.py:38
  261.5 6.6 %convolution_convert_fusion.1 = bf16[4096,512]{1,0:T(8,128)(2,1)} fusion(bf16[4096,1024]{1,0:T(8,128)(2,1)} %convolution_convert_fusion.refs_0_, bf16[1,2,512,512]{3,2,1,0:T(8,128)(2,1)S(1)} %convert_element_type.35), kind=kOutput, calls=%fused_computation.10 | convolution fusion | flops 2149580800 | bytes 8912896 | tf_op jit(solution)/shard_map/dot_general | solution.py:44
  268.1 193.1 %conditional.3 = ((bf16[8,8,4,2,16,512]{5,4,3,2,1,0:T(8,128)(2,1)}, f32[2176,512]{1,0:T(8,128)})) conditional(s32[]{:T(128)} %bitcast.5, (s32[2,16,128]{2,1,0:T(8,128)S(1)}, bf16[4096,512]{1,0:T(8,128)(2,1)}, f32[2176,512]{1,0:T(8,128)}) %tuple.75, (s32[2,16,128]{2,1,0:T(8,128)S(1)}, bf16[4096,512]{1,0:T(8,128)(2,1)}, ...), branch_computations={%region_5.6_spmd.clone, %region_6.7_spmd.clone} | conditional | bytes 16392 | solution.py:843
  268.7 192.1 %exchange_sum.8 = (bf16[8,8,4,2,16,512]{5,4,3,2,1,0:T(8,128)(2,1)}, f32[2176,512]{1,0:T(8,128)}) custom-call(s32[16,128]{1,0:T(8,128)} %slice_bitcast_fusion.plan, bf16[32,128,512]{2,1,0:T(8,128)(2,1)} %bitcast.23.table, f32[2176,512]{1,0:T(8,128)} %get-tuple-element.143.part), custom_call_target="tpu_custom_call" | custom-call | tf_op jit(solution)/shard_map/cond/branch_0_fun/exchange_sum/pallas_call | solution.py:534
  461.2 3.1 slice.108
  469.1 6.3 %multiply_subtract_fusion.1 = (f32[1,2,512,512]{3,2,1,0:T(8,128)}, f32[1,2,512,512]{3,2,1,0:T(8,128)}, f32[1,2,512,512]{3,2,1,0:T(8,128)}) fusion(f32[1,2,512,512]{3,2,1,0:T(8,128)S(1)} %copy-done.5, f32[1,2,512,512]{3,2,1,0:T(8,128)S(1)} %bitcast.63, f32[1,2,512,512]{3,2,1,0:T(8,128)} %param.39, f32[1,2,512,512]{3,2,1,0:T(8,128)} %param.43), kind=kLoop, calls=%fused_computation.28 | loop fusion | flops 7864320 | bytes 14680064 | tf_op jit(solution)/shard_map/sub | solution.py:54
  475.4 5.5 %multiply_subtract_fusion = (f32[1,1024,512]{2,1,0:T(8,128)}, f32[1,1024,512]{2,1,0:T(8,128)}, f32[1,1024,512]{2,1,0:T(8,128)}) fusion(f32[1,1024,512]{2,1,0:T(8,128)S(1)} %copy-done.10, f32[2176,512]{1,0:T(8,128)} %get-tuple-element.138, f32[1,1024,512]{2,1,0:T(8,128)S(1)} %copy-done.11, f32[1,1024,512]{2,1,0:T(8,128)S(1)} %copy-done.12), kind=kLoop, calls=%fused_computation.27 | loop fusion | flops 7864320 | bytes 14680064 | tf_op jit(solution)/shard_map/sub | solution.py:54
  480.9 17.9 %gather_sum.3 = bf16[32,128,512]{2,1,0:T(8,128)(2,1)S(1)} custom-call(s32[16,128]{1,0:T(8,128)} %slice_bitcast_fusion.6.sinks, bf16[4,8,2,128,128]{4,3,2,1,0:T(8,128)(2,1)} %bitcast.17.weights, bf16[8,8,4,2,16,512]{5,4,3,2,1,0:T(8,128)(2,1)} %get-tuple-element.140.got, bf16[4096,1024]{1,0:T(8,128)(2,1)} %convolution_convert_fusion.refs_0_, ...), custom_call_target="tpu_custom_call" | custom-call | tf_op jit(solution)/shard_map/gather_sum/pallas_call | solution.py:590
  498.8 33.1 %finish.1 = f32[640,512]{1,0:T(8,128)S(1)} custom-call(bf16[602,4096]{1,0:T(8,128)(2,1)S(1)} %bitcast.56, bf16[4096,512]{1,0:T(8,128)(2,1)S(1)} %bitcast.57), custom_call_target="tpu_custom_call" | custom-call | tf_op jit(solution)/shard_map/finish/pallas_call | solution.py:232
  (75 shorter events, 21.7 us)
Async XLA Ops:
  186.0 4.6 copy-start.5
  186.0 294.9 %all-to-all-start = ((bf16[64,128,128]{2,1,0:T(8,128)(2,1)}), bf16[64,128,128]{2,1,0:T(8,128)(2,1)}, u32[]{:S(2)}, u32[]{:S(2)}) async-start(bf16[64,128,128]{2,1,0:T(8,128)(2,1)} %param.33), calls=%async_computation | async-start | bytes 4194304 | tf_op jit(solution)/shard_map/all_to_all | solution.py:853
  190.8 70.7 %copy-start.8 = (bf16[1,2,512,512]{3,2,1,0:T(8,128)(2,1)}, bf16[1,2,512,512]{3,2,1,0:T(8,128)(2,1)S(1)}, u32[]{:S(2)}) copy-start(bf16[1,2,512,512]{3,2,1,0:T(8,128)(2,1)S(1)} %convert_element_type.35) | copy-start | bytes 3145732
  190.8 5.0 copy-start.4
  195.8 4.3 copy-start.23
  195.8 4.3 copy-start.9
  200.1 8.1 %copy-start.21 = (s32[4096]{0:T(1024)S(1)}, s32[4096]{0:T(1024)}, u32[]{:S(2)}) copy-start(s32[4096]{0:T(1024)} %param.28) | copy-start | bytes 49156
  200.1 8.8 %copy-start.17 = (f32[512,121]{1,0:T(8,128)S(1)}, f32[512,121]{1,0:T(8,128)}, u32[]{:S(2)}) copy-start(f32[512,121]{1,0:T(8,128)} %param.37) | copy-start | bytes 743428
  200.1 8.8 %copy-start.22 = (s32[4096,121]{1,0:T(8,128)S(1)}, s32[4096,121]{1,0:T(8,128)}, u32[]{:S(2)}) copy-start(s32[4096,121]{1,0:T(8,128)} %param.27) | copy-start | bytes 5947396
  213.3 3.3 copy-start.24
  238.9 6.5 %copy-start.7 = (bf16[4096,1024]{1,0:T(8,128)(2,1)S(1)}, bf16[4096,1024]{1,0:T(8,128)(2,1)}, u32[]{:S(2)}) copy-start(bf16[4096,1024]{1,0:T(8,128)(2,1)} %convolution_convert_fusion.refs_0_) | copy-start | bytes 25165828
  252.9 6.0 %copy-start.13 = (f32[1024,512]{1,0:T(8,128)S(1)}, f32[1024,512]{1,0:T(8,128)}, u32[]{:S(2)}) copy-start(f32[1024,512]{1,0:T(8,128)} %fusion.1) | copy-start | bytes 6291460
  252.9 6.0 %copy-start.16 = (f32[512,512]{1,0:T(8,128)S(1)}, f32[512,512]{1,0:T(8,128)}, u32[]{:S(2)}) copy-start(f32[512,512]{1,0:T(8,128)} %fusion.5) | copy-start | bytes 3145732
  261.5 6.6 %copy-start.20 = (s32[2,16,128]{2,1,0:T(8,128)S(1)}, s32[2,16,128]{2,1,0:T(8,128)}, u32[]{:S(2)}) copy-start(s32[2,16,128]{2,1,0:T(8,128)} %copy-done.19) | copy-start | bytes 49156
  464.3 2.8 copy-start.18
  465.3 3.7 copy-start.6
  469.1 6.3 %copy-start.10 = (f32[1,1024,512]{2,1,0:T(8,128)S(1)}, f32[1,1024,512]{2,1,0:T(8,128)}, u32[]{:S(2)}) copy-start(f32[1,1024,512]{2,1,0:T(8,128)} %param.36) | copy-start | bytes 6291460
  469.1 6.3 %copy-start.11 = (f32[1,1024,512]{2,1,0:T(8,128)S(1)}, f32[1,1024,512]{2,1,0:T(8,128)}, u32[]{:S(2)}) copy-start(f32[1,1024,512]{2,1,0:T(8,128)} %param.40) | copy-start | bytes 6291460
  469.1 6.3 %copy-start.12 = (f32[1,1024,512]{2,1,0:T(8,128)S(1)}, f32[1,1024,512]{2,1,0:T(8,128)}, u32[]{:S(2)}) copy-start(f32[1,1024,512]{2,1,0:T(8,128)} %param.44) | copy-start | bytes 6291460
  475.4 23.4 %slice-start = ((s8[4980736]{0:T(1024)(128)(4,1)}), s8[786432]{0:T(1024)(128)(4,1)S(1)}, s32[]{:S(2)}) async-start(s8[4980736]{0:T(1024)(128)(4,1)} %bitcast.54), calls=%async_computation.1 | async-start | bytes 1572864
  480.9 17.9 %slice-start.1 = ((s8[4980736]{0:T(1024)(128)(4,1)}), s8[4194304]{0:T(1024)(128)(4,1)S(1)}, s32[]{:S(2)}) async-start(s8[4980736]{0:T(1024)(128)(4,1)} %bitcast.54), calls=%async_computation.2 | async-start | bytes 8388608
  498.8 33.1 %copy-start.2 = (f32[602,512]{1,0:T(8,128)S(1)}, f32[602,512]{1,0:T(8,128)}, u32[]{:S(2)}) copy-start(f32[602,512]{1,0:T(8,128)} %refs_2_.1) | copy-start | bytes 3698692
  498.8 33.1 %copy-start.14 = (f32[602,512]{1,0:T(8,128)S(1)}, f32[602,512]{1,0:T(8,128)}, u32[]{:S(2)}) copy-start(f32[602,512]{1,0:T(8,128)} %param.38) | copy-start | bytes 3698692
  498.8 33.1 %copy-start.15 = (f32[602,512]{1,0:T(8,128)S(1)}, f32[602,512]{1,0:T(8,128)}, u32[]{:S(2)}) copy-start(f32[602,512]{1,0:T(8,128)} %param.42) | copy-start | bytes 3698692
  (4 other events, 6.3 us)

commit v3 on v2

--- a/solution.py
+++ b/solution.py
@@ -18,11 +18,16 @@
 PLANES = 4
 KINDS = 4
 CHUNKS = 8
-PARTS = 2
+PARTS = 4
 AHEAD = 3
-LEAD = 1
+NEAR_AHEAD = 3
+LEAD = 2
 UNROLL = False
 LANES = 128
+VMEM_MOST = 60 * 2**20
+TILE = 1024
+PIECES = 2
+SUM_AT = (0, 2, 9, 13, 17, 20, 24, 30, 32)
 MESH = pl.DeviceIdType.MESH
 
 
@@ -49,8 +54,8 @@
 def adam_update(weight, grad, first, second):
     first_new = beta_one * first + (1.0 - beta_one) * grad
     second_new = beta_two * second + (1.0 - beta_two) * grad * grad
-    first_hat = first_new / (1.0 - beta_one**adam_step)
-    second_hat = second_new / (1.0 - beta_two**adam_step)
+    first_hat = first_new * (1.0 / (1.0 - beta_one**adam_step))
+    second_hat = second_new * (1.0 / (1.0 - beta_two**adam_step))
     weight_new = weight - learn_rate * (
         first_hat / (jnp.sqrt(second_hat) + adam_eps) + decay_rate * weight
     )
@@ -68,10 +73,11 @@
 
 
 class Summer:
-    STEPS = 7
-
-    def __init__(self, n, shape):
+    STEPS = 9
+
+    def __init__(self, n, shape, split_row=None, direct=False):
         self.n, (self.rows, self.width) = n, shape
+        self.split_row, self.direct = split_row, direct
         self.size = n // PLANES
         self.chips = self.size // 2
         self.half = self.width // 2
@@ -84,7 +90,7 @@
     @staticmethod
     def padded(n, rows, width):
         summer = Summer(n, (rows, width))
-        unit = summer.bands * PLANES * 8
+        unit = summer.bands * PLANES * 16
         return -(-rows // unit) * unit
 
     def scratch(self):
@@ -92,34 +98,38 @@
         return [
             pltpu.VMEM((self.rows, self.half), f32),
             pltpu.VMEM((self.chips - 1, self.band, self.cut), f32),
-            pltpu.VMEM((PLANES - 1, self.shard, self.cut), f32),
-            pltpu.SemaphoreType.DMA((6,)),
-            pltpu.SemaphoreType.DMA((6,)),
+            pltpu.VMEM(((1 if self.direct else 2) * self.shard, self.cut), f32),
+            pltpu.VMEM(((PLANES - 1 if self.direct else 1) * self.shard, self.cut), f32),
+            pltpu.SemaphoreType.DMA((8,)),
+            pltpu.SemaphoreType.DMA((8,)),
         ]
 
     def bind(self, part, total, refs):
         self.part, self.total = part, total
-        self.from_core, self.from_chip, self.from_plane, self.sent, self.got = refs
+        self.from_core, self.from_chip, self.from_pair, self.from_far, self.sent, self.got = refs
         me = lax.axis_index("nodes")
         self.z, spot = me // self.size, me % self.size
         self.chip, self.core = spot // 2, spot % 2
+        self.low, self.high = self.z % 2, self.z // 2
         self.mine = pl.ds(pl.multiple_of(self.core * self.half, LANES), self.half)
         self.other = pl.ds(pl.multiple_of((1 - self.core) * self.half, LANES), self.half)
+        self.across = self.device(self.z, self.chip, 1 - self.core)
+        self.pair = self.device(self.high * 2 + 1 - self.low, self.chip, self.core)
+        self.far = self.device((1 - self.high) * 2 + self.low, self.chip, self.core)
 
     def device(self, z, chip, core):
         return z * self.size + chip * 2 + core
 
-    def plane_peers(self):
-        found = [self.device(self.z, self.chip, 1 - self.core)]
+    def column(self, hop):
+        return self.device(lax.rem(self.z + hop, PLANES), self.chip, self.core)
+
+    def peers(self):
+        found = [self.across, self.pair, self.far]
+        if self.direct:
+            found = [self.across] + [self.column(hop) for hop in range(1, PLANES)]
         for hop in range(1, self.chips):
             found.append(self.device(self.z, lax.rem(self.chip + hop, self.chips), self.core))
         return found
-
-    def column_peers(self):
-        return [
-            self.device(lax.rem(self.z + hop, PLANES), self.chip, self.core)
-            for hop in range(1, PLANES)
-        ]
 
     def patch(self, chip):
         row = pl.multiple_of((chip // self.cuts) * self.band, 8)
@@ -127,83 +137,148 @@
         return row, pl.ds(pl.multiple_of(col, LANES), self.cut)
 
     def copy(self, hop, src, dst, device):
-        return pltpu.make_async_remote_copy(
+        pltpu.make_async_remote_copy(
             src_ref=src,
             dst_ref=dst,
             send_sem=self.sent.at[hop],
             recv_sem=self.got.at[hop],
             device_id=(device,),
             device_id_type=MESH,
-        )
+        ).start()
 
     @staticmethod
     def settle(sem, held):
         pltpu.make_async_copy(held, held, sem).wait()
 
+    def split(self, values, first_row):
+        high = values.astype(self.total.dtype).astype(jnp.float32)
+        middle = (values - high).astype(self.total.dtype).astype(jnp.float32)
+        at = lax.broadcasted_iota(jnp.int32, values.shape, 0) + first_row - self.split_row
+        rest = jnp.where(at == 1, values - high, values - high - middle)
+        return jnp.where((at == 1) | (at == 2), rest, values)
+
+    def column_step(self, at, band, cols, plane_shard, amount):
+        part, total, shard = self.part, self.total, self.shard
+        if at == 2:
+            self.settle(self.got.at[1], self.from_chip)
+            held = part[band, cols]
+            for hop in range(1, self.chips):
+                held = held + self.from_chip[hop - 1]
+            part[band, cols] = held
+            for hop in range(1, PLANES):
+                src = part.at[plane_shard(lax.rem(self.z + hop, PLANES)), cols]
+                dst = self.from_far.at[pl.ds((hop - 1) * shard, shard)]
+                self.copy(3, src, dst, self.column(hop))
+        elif at == 3:
+            self.settle(self.got.at[3], self.from_far)
+            held = part[plane_shard(self.z), cols]
+            for hop in range(1, PLANES):
+                held = held + self.from_far[pl.ds((hop - 1) * shard, shard), :]
+            if self.split_row is not None:
+                held = self.split(held, self.patch(self.chip)[0] + self.z * shard)
+            total[plane_shard(self.z), cols] = held.astype(total.dtype)
+            held = total.at[plane_shard(self.z), cols]
+            for hop in range(1, PLANES):
+                self.copy(4, held, held, self.column(hop))
+
     def step(self, at):
-        part, total = self.part, self.total
-        across = self.device(self.z, self.chip, 1 - self.core)
+        part, total, shard = self.part, self.total, self.shard
         row, cols = self.patch(self.chip)
         band = pl.ds(row, self.band)
-        rows = pl.ds(pl.multiple_of(row + self.z * self.shard, 8), self.shard)
-        if at == 0:
-            self.copy(0, part.at[:, self.other], self.from_core, across).start()
+
+        def pairs(low):
+            return pl.ds(pl.multiple_of(row + low * 2 * shard, 16), 2 * shard)
+
+        def shards(high):
+            return pl.ds(pl.multiple_of(row + (self.low * 2 + high) * shard, 16), shard)
+
+        def amount(*shape):
+            return total.at[pl.ds(0, shape[0]), pl.ds(0, shape[1])]
+
+        short = self.band * total.dtype.itemsize // part.dtype.itemsize
+        every_chip = self.from_chip.at[:, pl.ds(0, short)]
+
+        def chips(hop):
+            chip = lax.rem(self.chip + hop, self.chips)
+            return chip, self.device(self.z, chip, self.core)
+
+        def plane_shard(z):
+            return pl.ds(pl.multiple_of(row + z * shard, 16), shard)
+
+        if self.direct and 2 <= at <= 5:
+            self.column_step(at, band, cols, plane_shard, amount)
+        elif at == 0:
+            self.copy(0, part.at[:, self.other], self.from_core, self.across)
         elif at == 1:
             self.settle(self.got.at[0], self.from_core)
             part[:, self.mine] += self.from_core[...]
             for hop in range(1, self.chips):
-                chip = lax.rem(self.chip + hop, self.chips)
+                chip, device = chips(hop)
                 there, cut = self.patch(chip)
                 src = part.at[pl.ds(there, self.band), cut]
-                dst = self.from_chip.at[hop - 1]
-                self.copy(1, src, dst, self.device(self.z, chip, self.core)).start()
+                self.copy(1, src, self.from_chip.at[hop - 1], device)
         elif at == 2:
             self.settle(self.got.at[1], self.from_chip)
             held = part[band, cols]
             for hop in range(1, self.chips):
                 held = held + self.from_chip[hop - 1]
             part[band, cols] = held
-            for hop in range(1, PLANES):
-                z = lax.rem(self.z + hop, PLANES)
-                there = pl.multiple_of(row + z * self.shard, 8)
-                src = part.at[pl.ds(there, self.shard), cols]
-                dst = self.from_plane.at[hop - 1]
-                self.copy(2, src, dst, self.device(z, self.chip, self.core)).start()
+            self.copy(2, part.at[pairs(1 - self.low), cols], self.from_pair, self.pair)
         elif at == 3:
-            self.settle(self.got.at[2], self.from_plane)
-            held = part[rows, cols]
-            for hop in range(1, PLANES):
-                held = held + self.from_plane[hop - 1]
-            total[rows, cols] = held
-            for hop in range(1, PLANES):
-                z = lax.rem(self.z + hop, PLANES)
-                held = total.at[rows, cols]
-                self.copy(3, held, held, self.device(z, self.chip, self.core)).start()
+            self.settle(self.got.at[2], self.from_pair)
+            part[pairs(self.low), cols] += self.from_pair[...]
+            self.copy(3, part.at[shards(1 - self.high), cols], self.from_far, self.far)
         elif at == 4:
-            self.settle(self.got.at[3], self.from_plane)
+            self.settle(self.got.at[3], self.from_far)
+            held = part[shards(self.high), cols] + self.from_far[...]
+            if self.split_row is not None:
+                held = self.split(held, row + (self.low * 2 + self.high) * shard)
+            total[shards(self.high), cols] = held.astype(total.dtype)
+            held = total.at[shards(self.high), cols]
+            self.copy(4, held, held, self.far)
+        elif at == 5:
+            self.settle(self.got.at[4], amount(shard, self.cut))
+            held = total.at[pairs(self.low), cols]
+            self.copy(5, held, held, self.pair)
+        elif at == 6:
+            if self.direct:
+                self.settle(self.got.at[4], amount((PLANES - 1) * shard, self.cut))
+            else:
+                self.settle(self.got.at[5], amount(2 * shard, self.cut))
+            held = total.at[band, cols]
             for hop in range(1, self.chips):
-                chip = lax.rem(self.chip + hop, self.chips)
-                held = total.at[band, cols]
-                self.copy(4, held, held, self.device(self.z, chip, self.core)).start()
-        elif at == 5:
-            self.settle(self.got.at[4], self.from_chip)
+                self.copy(6, held, held, chips(hop)[1])
+        elif at == 7:
+            self.settle(self.got.at[6], every_chip)
             held = total.at[:, self.mine]
-            self.copy(5, held, held, across).start()
+            self.copy(7, held, held, self.across)
         else:
-            self.settle(self.got.at[5], self.from_core)
+            self.settle(self.got.at[7], amount(self.rows, self.half))
             self.settle(self.sent.at[0], self.from_core)
             self.settle(self.sent.at[1], self.from_chip)
-            self.settle(self.sent.at[2], self.from_plane)
-            self.settle(self.sent.at[3], self.from_plane)
-            self.settle(self.sent.at[4], self.from_chip)
-            self.settle(self.sent.at[5], self.from_core)
-
-
-def finish_kernel(n, tile, rows, grads, total, part, *refs):
-    summer = Summer(n, part.shape)
+            self.settle(self.sent.at[3], self.from_far)
+            if self.direct:
+                self.settle(self.sent.at[4], amount((PLANES - 1) * shard, self.cut))
+            else:
+                self.settle(self.sent.at[2], self.from_pair)
+                self.settle(self.sent.at[4], amount(shard, self.cut))
+                self.settle(self.sent.at[5], amount(2 * shard, self.cut))
+            self.settle(self.sent.at[6], every_chip)
+            self.settle(self.sent.at[7], amount(self.rows, self.half))
+
+
+def finish_kernel(n, tile, rows_there, grads, loss, total, part, rows, held, sem, *refs):
+    fetches = [
+        pltpu.make_async_copy(grads, held, sem.at[0]),
+        pltpu.make_async_copy(rows_there, rows, sem.at[1]),
+    ]
+    for fetch in fetches:
+        fetch.start()
+    below = -(-rows.shape[0] // 8) * 8
+    summer = Summer(n, part.shape, below, direct=True)
     summer.bind(part, total, refs)
     barrier = pltpu.get_barrier_semaphore()
-    peers = summer.plane_peers() + summer.column_peers()
+    peers = summer.peers()
     for peer in peers:
         pl.semaphore_signal(barrier, inc=1, device_id=(peer,), device_id_type=MESH)
     count, depth = rows.shape
@@ -213,11 +288,14 @@
 
         def add(at, carry):
             window = pl.ds(pl.multiple_of(at * tile, tile), tile)
-            part[:count, cols] += mat_product(rows[:, window], grads[window, cols])
+            part[:count, cols] += mat_product(rows[:, window], held[window, cols])
             return carry
 
         lax.fori_loop(0, depth // tile, add, 0)
-
+        part[pl.ds(below, 8), cols] = jnp.broadcast_to(loss[...], (8, summer.half))
+
+    for fetch in fetches:
+        fetch.wait()
     multiply(summer.other)
     pl.semaphore_wait(barrier, len(peers))
     summer.step(0)
@@ -226,25 +304,38 @@
         summer.step(at)
 
 
-def finish(n, rows, grads, collective):
-    shape = (Summer.padded(n, rows.shape[0], grads.shape[1]), grads.shape[1])
+def finish(n, rows, grads, loss, collective):
+    count = -(-rows.shape[0] // 8) * 8
+    shape = (Summer.padded(n, count + 8, grads.shape[1]), grads.shape[1])
     vmem = pl.BlockSpec(memory_space=pltpu.VMEM)
-    return pl.pallas_call(
+    total = pl.pallas_call(
         functools.partial(finish_kernel, n, 1024),
-        out_shape=jax.ShapeDtypeStruct(shape, jnp.float32),
-        in_specs=[vmem, vmem],
+        out_shape=jax.ShapeDtypeStruct(shape, jnp.bfloat16),
+        in_specs=[
+            pl.BlockSpec(memory_space=pltpu.HBM),
+            pl.BlockSpec(memory_space=pltpu.HBM),
+            vmem,
+        ],
         out_specs=vmem,
-        scratch_shapes=[pltpu.VMEM(shape, jnp.float32)] + Summer(n, shape).scratch(),
+        scratch_shapes=[
+            pltpu.VMEM(shape, jnp.float32),
+            pltpu.VMEM(rows.shape, rows.dtype),
+            pltpu.VMEM(grads.shape, grads.dtype),
+            pltpu.SemaphoreType.DMA((2,)),
+        ]
+        + Summer(n, shape, direct=True).scratch(),
         compiler_params=pltpu.CompilerParams(
-            collective_id=collective, has_side_effects=True, vmem_limit_bytes=40 * 2**20
+            collective_id=collective, has_side_effects=True, vmem_limit_bytes=VMEM_MOST
         ),
         name="finish",
-    )(rows, grads)
+    )(rows, grads, loss)
+    total = total.astype(jnp.float32)
+    return total[: rows.shape[0]], jnp.sum(total[count : count + 3, 0])
 
 
 class Exchange:
-    def __init__(self, n, slots, far_cap, near_cap, shape, kind):
-        self.n, self.slots = n, slots
+    def __init__(self, n, slots, way, far_cap, near_cap, shape, kind):
+        self.n, self.slots, self.way = n, slots, way
         self.far_cap, self.near_cap = far_cap, near_cap
         self.size = n // PLANES
         self.blocks, self.depth, self.width = shape
@@ -276,7 +367,7 @@
         )
 
     def bind(self, plan, table, out, refs):
-        self.plan, self.table, self.out = plan, table, out
+        self.plan, self.table, self.out = plan.at[self.way], table, out
         rest = list(refs)
         steps = self.steps
 
@@ -317,12 +408,16 @@
             return carry
 
         lax.fori_loop(1, self.size, in_plane, 0)
+        hello(self.near_dev)
         if column:
-            for hop in range(1, PLANES):
-                hello(lax.rem(self.z + hop, PLANES) * self.size + self.spot)
-            pl.semaphore_wait(barrier, self.size - 1 + PLANES - 1)
+            hello(((1 - self.z // 2) * 2 + self.z % 2) * self.size + self.spot)
+
+            @pl.when(self.inner == 1)
+            def _():
+                hello(self.relay_dev)
+
+            pl.semaphore_wait(barrier, self.size + 1 + self.inner)
             return
-        hello(self.near_dev)
 
         @pl.when(self.inner == 1)
         def _():
@@ -350,17 +445,12 @@
     def settle(sem, held):
         pltpu.make_async_copy(held, held, sem).wait()
 
-    def launch(self, step):
+    def launch_far(self, step):
         rows, cols = self.window(step)
-        plan, table = self.plan, self.table
-        far_stage, near_stage = self.far_stage[step], self.near_stage[step]
+        plan, table, far_stage = self.plan, self.table, self.far_stage[step]
 
         def fill_far(at, carry):
             far_stage[at] = table[plan[ROW_FAR, at], rows, cols]
-            return carry
-
-        def fill_near(at, carry):
-            near_stage[at] = table[plan[ROW_NEAR, at], rows, cols]
             return carry
 
         lax.fori_loop(0, self.far_cap, fill_far, 0, unroll=UNROLL)
@@ -375,6 +465,14 @@
                     self.far_recv.at[lane, step],
                     self.relay_dev,
                 ).start()
+
+    def launch_near(self, step):
+        rows, cols = self.window(step)
+        plan, table, near_stage = self.plan, self.table, self.near_stage[step]
+
+        def fill_near(at, carry):
+            near_stage[at] = table[plan[ROW_NEAR, at], rows, cols]
+            return carry
 
         lax.fori_loop(0, self.near_cap, fill_near, 0, unroll=UNROLL)
         self.remote(
@@ -461,18 +559,41 @@
     def run(self, side=None):
         steps = self.steps
         for step in range(min(AHEAD, steps)):
-            self.launch(step)
+            self.launch_far(step)
+            self.launch_near(step)
+
+        @pl.when(self.inner == 1)
+        def _():
+            for step in range(AHEAD, min(NEAR_AHEAD, steps)):
+                self.launch_near(step)
+
         for step in range(min(LEAD, steps)):
             self.serve(step, 0)
         for step in range(steps):
             if step + AHEAD < steps:
-                self.launch(step + AHEAD)
+                self.launch_far(step + AHEAD)
+                if NEAR_AHEAD == AHEAD:
+                    self.launch_near(step + AHEAD)
+                else:
+
+                    @pl.when(self.inner == 0)
+                    def _():
+                        self.launch_near(step + AHEAD)
+
+            if NEAR_AHEAD > AHEAD and step + NEAR_AHEAD < steps:
+
+                @pl.when(self.inner == 1)
+                def _():
+                    self.launch_near(step + NEAR_AHEAD)
+
             self.relay(step)
             self.serve(step, 1)
             if step + LEAD < steps:
                 self.serve(step + LEAD, 0)
             if side is not None:
                 side(step)
+        if side is not None:
+            side(steps)
         for chunk in range(CHUNKS):
             self.settle(self.serve_recv.at[chunk], self.out.at[chunk])
         for step in range(max(0, steps - self.ring), steps):
@@ -489,36 +610,44 @@
                     self.settle(self.pass_sent.at[lane, step], self.pass_stage[lane][step])
 
 
-def exchange_kernel(moves, plan, table, out, *refs):
-    moves.bind(plan, table, out, refs)
+def exchange_kernel(moves, plan, table, out, held_table, table_sem, *refs):
+    moves.bind(plan, held_table, out, refs)
+    fetch = pltpu.make_async_copy(table, held_table, table_sem)
+    fetch.start()
     moves.greet()
+    fetch.wait()
     moves.run()
 
 
-def exchange_sum_kernel(moves, summer, plan, table, part, out, total, held, sem, *refs):
-    moves.bind(plan, table, out, refs[5:])
-    summer.bind(held, total, refs[:5])
+def exchange_sum_kernel(
+    moves, summer, plan, table, part, out, total, held_table, table_sem, held, sem, *refs
+):
+    moves.bind(plan, held_table, out, refs[6:])
+    fetch_table = pltpu.make_async_copy(table, held_table, table_sem)
+    fetch_table.start()
+    summer.bind(held, total, refs[:6])
     fetch = pltpu.make_async_copy(part, held, sem)
     fetch.start()
     moves.greet(column=True)
+    fetch_table.wait()
 
     def side(step):
         if step == 0:
             fetch.wait()
-        at = step // PARTS
-        if step % PARTS == 0 and at < Summer.STEPS:
-            summer.step(at)
+        if step in SUM_AT:
+            summer.step(SUM_AT.index(step))
 
     moves.run(side)
 
 
-def exchange(n, slots, far_cap, near_cap, collective, plan, table, part=None):
-    moves = Exchange(n, slots, far_cap, near_cap, table.shape, table.dtype)
+def exchange(n, slots, way, far_cap, near_cap, collective, plan, table, part=None):
+    moves = Exchange(n, slots, way, far_cap, near_cap, table.shape, table.dtype)
     hbm = pl.BlockSpec(memory_space=pl.ANY)
     vmem = pl.BlockSpec(memory_space=pltpu.VMEM)
-    in_specs = [pl.BlockSpec(memory_space=pltpu.SMEM), vmem]
+    in_specs = [pl.BlockSpec(memory_space=pltpu.SMEM), hbm]
+    table_held = [pltpu.VMEM(table.shape, table.dtype), pltpu.SemaphoreType.DMA]
     params = pltpu.CompilerParams(
-        collective_id=collective, has_side_effects=True, vmem_limit_bytes=60 * 2**20
+        collective_id=collective, has_side_effects=True, vmem_limit_bytes=VMEM_MOST
     )
     if part is None:
         return pl.pallas_call(
@@ -526,17 +655,18 @@
             out_shape=moves.out_shape(),
             in_specs=in_specs,
             out_specs=hbm,
-            scratch_shapes=moves.scratch(),
+            scratch_shapes=table_held + moves.scratch(),
             compiler_params=params,
             name="exchange",
         )(plan, table)
     summer = Summer(n, part.shape)
     return pl.pallas_call(
         functools.partial(exchange_sum_kernel, moves, summer),
-        out_shape=(moves.out_shape(), jax.ShapeDtypeStruct(part.shape, jnp.float32)),
+        out_shape=(moves.out_shape(), jax.ShapeDtypeStruct(part.shape, jnp.bfloat16)),
         in_specs=in_specs + [hbm],
         out_specs=(hbm, vmem),
-        scratch_shapes=[pltpu.VMEM(part.shape, jnp.float32), pltpu.SemaphoreType.DMA]
+        scratch_shapes=table_held
+        + [pltpu.VMEM(part.shape, jnp.float32), pltpu.SemaphoreType.DMA]
         + summer.scratch()
         + moves.scratch(),
         compiler_params=params,
@@ -544,71 +674,107 @@
     )(plan, table, part)
 
 
-def gather_sum_kernel(flip, slots, first_row, sinks, weights, got, *refs):
-    out, total = refs[-2:]
+def add_products(flip, slots, first_row, sinks, weights, got, total, at, size):
+    z, _, _, near, far_in, far_out = place(lax.axis_index("nodes"), size)
+    depth, width = total.shape[1:]
+    dims = (((0,), (0,)), ((), ())) if flip else (((1,), (0,)), ((), ()))
+    for kind, owner_z in enumerate((z, near, far_in, far_out)):
+        for slot in range(slots):
+            sink = sinks[first_row + slot, owner_z * size + at]
+            rows = got[:, 0, kind, slot].reshape(depth, width)
+            total[sink] += lax.dot_general(
+                weights[owner_z, 0, slot], rows, dims, preferred_element_type=jnp.float32
+            )
+
+
+def return_sum_kernel(slots, first_row, *refs):
+    sinks, weights, got, own, mixer = refs[:5]
+    states, head_state, out = refs[5:13], refs[13:17], refs[17]
+    updates, head_update, total = refs[18:24], refs[24:27], refs[27]
     at = pl.program_id(0)
-    size = pl.num_programs(0)
-    z, _, _, near, far_in, far_out = place(lax.axis_index("nodes"), size)
+    blocks, depth, width = out.shape
 
     @pl.when(at == 0)
     def _():
         total[...] = jnp.zeros_like(total)
-
-    blocks, depth, width = total.shape
-    if flip:
-        own, mixer = refs[:2]
-        span = own.shape[0] // depth
-        base = right_product(own[...], mixer[...]).reshape(span, depth, width)
-        total[pl.ds(at * span, span)] += base
-    for kind, owner_z in enumerate((z, near, far_in, far_out)):
-        for slot in range(slots):
-            sink = sinks[first_row + slot, owner_z * size + at]
-
-            @pl.when(sink < blocks)
-            def _():
-                edge = weights[owner_z, 0, slot]
-                rows = got[:, 0, kind, slot].reshape(depth, width)
-                dims = (((0,), (0,)), ((), ())) if flip else (((1,), (0,)), ((), ()))
-                total[sink] += lax.dot_general(
-                    edge, rows, dims, preferred_element_type=jnp.float32
-                )
+        label_width = head_state[0].shape[1]
+        head_grad = head_state[1][...].astype(jnp.float32).T[:, :label_width]
+        fresh = adam_update(head_state[0][...], head_grad, head_state[2][...], head_state[3][...])
+        for to, values in zip(head_update, fresh):
+            to[...] = values
+
+    span = own.shape[0] // depth
+    base = right_product(own[...], mixer[...]).reshape(span, depth, width)
+    total[pl.ds(at * span, span)] += base
+    for state, update in ((states[:4], updates[:3]), (states[4:], updates[3:])):
+        grad = state[1][...].astype(jnp.float32)
+        fresh = adam_update(state[0][...], grad, state[2][...], state[3][...])
+        for to, values in zip(update, fresh):
+            to[...] = values
+    size = pl.num_programs(0)
+    add_products(True, slots, first_row, sinks, weights, got, total, at, size)
 
     @pl.when(at == pl.num_programs(0) - 1)
     def _():
-        out[...] = total[...].astype(out.dtype)
-
-
-def gather_sum(flip, first_row, sinks, weights, got, blocks, *base):
+        out[...] = to_half(total[:blocks])
+
+
+def block_specs(weights, got):
+    chunks, size, kinds, slots, rows, width = got.shape
+    depth = chunks * rows
+    edges = weights.reshape(PLANES, size, slots, depth, depth)
+
+    def clip(at):
+        return jnp.minimum(at, size - 1)
+
+    specs = [
+        pl.BlockSpec((PLANES, 1, slots, depth, depth), lambda at, *_: (0, clip(at), 0, 0, 0)),
+        pl.BlockSpec(
+            (chunks, 1, kinds, slots, rows, width), lambda at, *_: (0, clip(at), 0, 0, 0, 0)
+        ),
+    ]
+    return edges, specs
+
+
+def return_sum(first_row, sinks, weights, got, blocks, own, mixer, grads, groups, head):
     chunks, size, _, slots, rows, width = got.shape
     depth = chunks * rows
-    edges = weights.reshape(PLANES, size, slots, depth, depth)
+    edges, specs = block_specs(weights, got)
     tile = blocks * depth // size
-    base_specs = [
+    specs = specs + [
         pl.BlockSpec((tile, width), lambda at, sinks: (at, 0)),
         pl.BlockSpec((width, width), lambda at, sinks: (0, 0)),
     ]
-    return pl.pallas_call(
-        functools.partial(gather_sum_kernel, flip, slots, first_row),
-        out_shape=jax.ShapeDtypeStruct((blocks, depth, width), jnp.bfloat16),
+    states, shapes, out_specs = [], [], []
+    for place_at, (weight, first, second) in enumerate(groups):
+        part = weight.shape[0] // size
+        spec = pl.BlockSpec((part, width), lambda at, sinks: (at, 0))
+        moved = pl.BlockSpec((part, width), lambda at, sinks, p=place_at: (at + p * size, 0))
+        states += [weight, grads, first, second]
+        specs = specs + [spec, moved, spec, spec]
+        shapes += [jax.ShapeDtypeStruct(weight.shape, jnp.float32)] * 3
+        out_specs += [spec] * 3
+    head_at = 2 * groups[0][0].shape[0] // LANES
+    still = pl.BlockSpec(head[0].shape, lambda at, sinks: (0, 0))
+    states += [head[0], grads, head[1], head[2]]
+    specs = specs + [still, pl.BlockSpec((LANES, width), lambda at, sinks: (head_at, 0)), still, still]
+    shapes += [jax.ShapeDtypeStruct(head[0].shape, jnp.float32)] * 3
+    out_specs += [still] * 3
+    found = pl.pallas_call(
+        functools.partial(return_sum_kernel, slots, first_row),
+        out_shape=[jax.ShapeDtypeStruct((blocks, depth, width), jnp.bfloat16)] + shapes,
         grid_spec=pltpu.PrefetchScalarGridSpec(
             num_scalar_prefetch=1,
             grid=(size,),
-            in_specs=[
-                pl.BlockSpec(
-                    (PLANES, 1, slots, depth, depth), lambda at, sinks: (0, at, 0, 0, 0)
-                ),
-                pl.BlockSpec(
-                    (chunks, 1, KINDS, slots, rows, width),
-                    lambda at, sinks: (0, at, 0, 0, 0, 0),
-                ),
-            ]
-            + base_specs[: len(base)],
-            out_specs=pl.BlockSpec((blocks, depth, width), lambda at, sinks: (0, 0, 0)),
-            scratch_shapes=[pltpu.VMEM((blocks, depth, width), jnp.float32)],
+            in_specs=specs,
+            out_specs=[pl.BlockSpec((blocks, depth, width), lambda at, sinks: (0, 0, 0))]
+            + out_specs,
+            scratch_shapes=[pltpu.VMEM((blocks + 1, depth, width), jnp.float32)],
         ),
-        compiler_params=pltpu.CompilerParams(vmem_limit_bytes=40 * 2**20),
-        name="gather_sum",
-    )(sinks, edges, got, *base)
+        compiler_params=pltpu.CompilerParams(vmem_limit_bytes=48 * 2**20),
+        name="return_sum",
+    )(sinks, edges, got, own, mixer, *states)
+    return found[0], found[1:4], found[4:7], found[7:10]
 
 
 ROW_FAR, ROW_NEAR, ROW_PASS, ROW_SERVE = 0, 1, 2, 4
@@ -616,7 +782,7 @@
 
 def plan_rows(slots):
     wishes = ROW_SERVE + KINDS * slots
-    return wishes, wishes + slots, -(-(wishes + slots + 1) // 8) * 8
+    return wishes, -(-(wishes + slots) // 8) * 8
 
 
 def column(values, lane):
@@ -624,12 +790,12 @@
     return jnp.sum(jnp.where(lanes == lane, values, 0.0), axis=1, keepdims=True)
 
 
-def lay_plan(n, slots, blocks, rungs, way, wishes_of, plan, present):
+def lay_plan(n, slots, blocks, rungs, way, wishes_of, plan, chosen, present):
     size = n // PLANES
     me = lax.axis_index("nodes")
     z, spot, inner, near, far_in, far_out = place(me, size)
     half = z // 2
-    row_wish, row_rung, _ = plan_rows(slots)
+    row_wish, _ = plan_rows(slots)
 
     taker = lax.broadcasted_iota(jnp.int32, (LANES, LANES), 0)
     group = lax.broadcasted_iota(jnp.int32, (LANES, LANES), 1)
@@ -659,7 +825,7 @@
     def put(row, values):
         plan[way, pl.ds(row, 1), :] = values.astype(jnp.int32)
 
-    put(row_rung, jnp.broadcast_to(rung, (1, LANES)))
+    chosen[...] = rung.astype(jnp.int32)
     block_id = lax.broadcasted_iota(jnp.int32, (blocks, LANES), 0)
     block_lane = lax.broadcasted_iota(jnp.int32, (blocks, LANES), 1)
     ids = block_id.astype(jnp.float32)
@@ -699,9 +865,23 @@
 
 
 def prelude_kernel(n, slots, blocks, rungs, tile, *refs):
-    mine, rows, weight, hidden, plan, taken = refs[:6]
-    wishes = refs[6 : 6 + 2 * slots]
-    present, send_sem, recv_sem = refs[6 + 2 * slots :]
+    mine, rows, weight, hidden, plan = refs[:5]
+    chosen, taken = refs[5:7], refs[7]
+    wishes = refs[8 : 8 + 2 * slots]
+    present, held, held_weight, row_sem, weight_sem, send_sem, recv_sem = refs[8 + 2 * slots :]
+    tiles = rows.shape[1] // tile
+
+    def window(at):
+        return pl.ds(pl.multiple_of(at * tile, tile), tile)
+
+    def fetch(at):
+        part = window(at)
+        return pltpu.make_async_copy(rows.at[:, part], held.at[:, part], row_sem.at[at])
+
+    fetch_weight = pltpu.make_async_copy(weight, held_weight, weight_sem)
+    fetch_weight.start()
+    for at in range(tiles):
+        fetch(at).start()
     me = lax.axis_index("nodes")
     barrier = pltpu.get_barrier_semaphore()
 
@@ -713,6 +893,15 @@
 
     lax.fori_loop(1, n, greet, 0)
     taken[me] = mine[...]
+    fetch_weight.wait()
+    half_weight = to_half(held_weight[...])
+
+    def project(at):
+        fetch(at).wait()
+        hidden[window(at), :] = to_half(left_product(held[:, window(at)], half_weight))
+
+    for at in range(tiles // 2):
+        project(at)
     pl.semaphore_wait(barrier, n - 1)
 
     def send(step, carry):
@@ -727,14 +916,8 @@
         return carry
 
     lax.fori_loop(1, n, send, 0)
-    half_weight = to_half(weight[...])
-
-    def project(at, carry):
-        window = pl.ds(pl.multiple_of(at * tile, tile), tile)
-        hidden[window, :] = to_half(left_product(rows[:, window], half_weight))
-        return carry
-
-    lax.fori_loop(0, rows.shape[1] // tile, project, 0)
+    for at in range(tiles // 2, tiles):
+        project(at)
     others = taken.at[pl.ds(0, n - 1)]
     pltpu.make_async_copy(others, others, recv_sem).wait()
     pltpu.make_async_copy(others, others, send_sem).wait()
@@ -758,6 +941,7 @@
             way,
             wishes[way * slots : (way + 1) * slots],
             plan,
+            chosen[way],
             present,
         )
 
@@ -765,27 +949,156 @@
 def prelude(n, slots, blocks, rungs, mine, rows, weight):
     count, width = rows.shape[1], weight.shape[1]
     vmem = pl.BlockSpec(memory_space=pltpu.VMEM)
-    plan_shape = (2, plan_rows(slots)[2], LANES)
+    plan_shape = (2, plan_rows(slots)[1], LANES)
     return pl.pallas_call(
         functools.partial(prelude_kernel, n, slots, blocks, rungs, 512),
         out_shape=(
             jax.ShapeDtypeStruct((count, width), jnp.bfloat16),
             jax.ShapeDtypeStruct(plan_shape, jnp.int32),
+            jax.ShapeDtypeStruct((1, 1), jnp.int32),
+            jax.ShapeDtypeStruct((1, 1), jnp.int32),
         ),
-        in_specs=[vmem, vmem, vmem],
-        out_specs=(vmem, vmem),
+        in_specs=[vmem, pl.BlockSpec(memory_space=pltpu.HBM), pl.BlockSpec(memory_space=pltpu.HBM)],
+        out_specs=(vmem, vmem, vmem, vmem),
         scratch_shapes=[pltpu.VMEM((n,) + mine.shape, jnp.int32)]
         + [pltpu.VMEM((n, LANES), jnp.int32) for _ in range(2 * slots)]
         + [
             pltpu.VMEM((n * blocks, LANES), jnp.float32),
+            pltpu.VMEM(rows.shape, rows.dtype),
+            pltpu.VMEM(weight.shape, weight.dtype),
+            pltpu.SemaphoreType.DMA((count // 512,)),
+            pltpu.SemaphoreType.DMA,
             pltpu.SemaphoreType.DMA,
             pltpu.SemaphoreType.DMA,
         ],
         compiler_params=pltpu.CompilerParams(
-            collective_id=0, has_side_effects=True, vmem_limit_bytes=40 * 2**20
+            collective_id=0, has_side_effects=True, vmem_limit_bytes=VMEM_MOST
         ),
         name="prelude",
     )(mine, rows, weight)
+
+
+def sigmoid(values):
+    return 1.0 / (1.0 + jnp.exp(-values))
+
+
+def dense_kernel(label_width, pieces, slots, first_row, count, sinks, edges, got, *refs):
+    marks, truth, own, pair, merge, head = refs[:6]
+    grad_own, grad_taken, part, loss, total = refs[6:]
+    at = pl.program_id(0)
+    gathers = pl.num_programs(0) - total.shape[0] * total.shape[1] // own.shape[0]
+
+    @pl.when(at == 0)
+    def _():
+        total[...] = jnp.zeros_like(total)
+        part[...] = jnp.zeros_like(part)
+        loss[...] = jnp.zeros_like(loss)
+
+    @pl.when(at < gathers)
+    def _():
+        add_products(False, slots, first_row, sinks, edges, got, total, at, gathers)
+
+    @pl.when(at >= gathers)
+    def _():
+        span = own.shape[0] // total.shape[1]
+        taken = total.at[pl.ds((at - gathers) * span, span)]
+        dense_tile(
+            label_width,
+            pieces,
+            (count, marks, truth, own, taken, pair, merge, head),
+            (grad_own, grad_taken, part, loss),
+        )
+
+
+def dense_tile(label_width, pieces, given, made):
+    count, marks, truth, own, taken, pair, merge, head = given
+    grad_own, grad_taken, part, loss = made
+    width = own.shape[1]
+    tile = own.shape[0] // pieces
+    span = taken.shape[0] // pieces
+    denom = count[0].astype(jnp.float32) * float(label_width)
+    for piece in range(pieces):
+        rows = pl.ds(piece * tile, tile)
+        hidden = own[rows, :]
+        gathered = to_half(taken[pl.ds(piece * span, span)]).reshape(tile, width)
+        self_part = to_half(mat_product(hidden, pair[0]))
+        neigh_part = to_half(mat_product(gathered, pair[1]))
+        linear = mat_product(self_part, merge[:width]) + mat_product(neigh_part, merge[width:])
+        sig = sigmoid(linear)
+        active = linear * sig
+        scale = lax.rsqrt(jnp.sum(active * active, axis=1, keepdims=True) + norm_eps)
+        output = active * scale
+        final = to_half(output)
+        logits = mat_product(final, head[...])
+        labels = truth[rows, :].astype(jnp.float32)
+        labels = jnp.pad(labels, ((0, 0), (0, LANES - label_width)))
+        marked = marks[0, :, rows].astype(jnp.float32)
+        marked = jnp.broadcast_to(marked, (LANES, tile)).T
+        column_id = lax.broadcasted_iota(jnp.int32, (tile, LANES), 1)
+        marked = jnp.where(column_id < label_width, marked, 0.0)
+        decay = jnp.exp(-jnp.abs(logits))
+        entry = jnp.maximum(logits, 0.0) - logits * labels + jnp.log1p(decay)
+        loss[...] += jnp.sum(entry * marked, axis=(0, 1), keepdims=True) / denom
+        grad_logits = to_half((sigmoid(logits) - labels) * marked / denom)
+        part[pl.ds(4 * width, LANES), :] += left_product(grad_logits, final)
+        grad_out = right_product(grad_logits, head[...])
+        along = jnp.sum(grad_out * output, axis=1, keepdims=True)
+        grad_active = scale * (grad_out - output * along)
+        grad_linear = to_half(grad_active * sig * (1.0 + linear * (1.0 - sig)))
+        part[pl.ds(2 * width, width), :] += left_product(self_part, grad_linear)
+        part[pl.ds(3 * width, width), :] += left_product(neigh_part, grad_linear)
+        grad_self = to_half(right_product(grad_linear, merge[:width]))
+        grad_neigh = to_half(right_product(grad_linear, merge[width:]))
+        grad_own[rows, :] = grad_self
+        part[pl.ds(0, width), :] += left_product(hidden, grad_self)
+        part[pl.ds(width, width), :] += left_product(gathered, grad_neigh)
+        grad_taken[rows, :] = to_half(right_product(grad_neigh, pair[1]))
+
+
+def dense(tile, pieces, part_rows, first_row, scalars, edges, got, marks, truth, own, weights):
+    rows, width = own.shape
+    label_width = truth.shape[1]
+    size, slots = got.shape[1], got.shape[3]
+    edges, specs = block_specs(edges, got)
+    depth = edges.shape[-1]
+
+    def later(at):
+        return jnp.maximum(at - size, 0)
+
+    by_rows = pl.BlockSpec((tile, width), lambda at, *_: (later(at), 0))
+
+    def whole(values):
+        return pl.BlockSpec(values.shape, lambda at, *_: (0,) * values.ndim)
+
+    return pl.pallas_call(
+        functools.partial(dense_kernel, label_width, pieces, slots, first_row),
+        out_shape=(
+            jax.ShapeDtypeStruct((rows, width), jnp.bfloat16),
+            jax.ShapeDtypeStruct((rows, width), jnp.bfloat16),
+            jax.ShapeDtypeStruct((part_rows, width), jnp.float32),
+            jax.ShapeDtypeStruct((1, 1), jnp.float32),
+        ),
+        grid_spec=pltpu.PrefetchScalarGridSpec(
+            num_scalar_prefetch=2,
+            grid=(size + rows // tile,),
+            in_specs=specs
+            + [
+                pl.BlockSpec((1, 1, tile), lambda at, *_: (later(at), 0, 0)),
+                pl.BlockSpec((tile, label_width), lambda at, *_: (later(at), 0)),
+                by_rows,
+            ]
+            + [whole(values) for values in weights],
+            out_specs=(
+                by_rows,
+                by_rows,
+                pl.BlockSpec((part_rows, width), lambda at, *_: (0, 0)),
+                pl.BlockSpec((1, 1), lambda at, *_: (0, 0)),
+            ),
+            scratch_shapes=[pltpu.VMEM((rows // depth + 1, depth, width), jnp.float32)],
+        ),
+        compiler_params=pltpu.CompilerParams(vmem_limit_bytes=VMEM_MOST),
+        name="dense",
+    )(*scalars, edges, got, marks.reshape(rows // tile, 1, tile), truth, own, *weights)
 
 
 def shards(
@@ -822,85 +1135,71 @@
     raw = jnp.where(alive, raw, block_count).transpose(0, 2, 1).reshape(2 * slots, n)
     raw = jnp.pad(raw, ((0, 0), (0, LANES - n)), constant_values=block_count)
     near_full = min(block_count, size * slots)
-    rungs = [(min(23, block_count), min(15, near_full)), (block_count, near_full)]
-    if near_full > 16:
-        rungs = rungs[1:]
-    hidden_half, plan = prelude(
+    rungs = [(21, 14), (23, 15), (block_count, near_full)]
+    if near_full > 16 or block_count < 24:
+        rungs = rungs[-1:]
+    hidden_half, plan, *rung_of = prelude(
         n, slots, block_count, rungs, raw.reshape(1, 2 * slots * LANES), features.T, embed_weight
     )
-    row_wish, row_rung, _ = plan_rows(slots)
+    row_wish, _ = plan_rows(slots)
 
     def swap(way, *held):
         def at(rung):
             far_cap, near_cap = rungs[rung]
             return lambda *held: exchange(
-                n, slots, far_cap, near_cap, 2 + way * len(rungs) + rung, *held
+                n, slots, way, far_cap, near_cap, 2 + way * len(rungs) + rung, *held
             )
 
         if len(rungs) == 1:
-            return at(0)(plan[way], *held)
+            return at(0)(plan, *held)
         branches = [at(rung) for rung in range(len(rungs))]
-        return lax.switch(plan[way, row_rung, 0], branches, plan[way], *held)
+        return lax.switch(rung_of[way].reshape(()), branches, plan, *held)
 
     pair_half = to_half(pair_weight)
     merge_half = to_half(merge_weight)
     head_half = to_half(head_weight)
     got = swap(0, hidden_half.reshape(block_count, block_rows, hidden_width))
-    gathered = gather_sum(
-        False, slots, raw, adjacency, got, block_count
-    ).reshape(row_count, hidden_width)
-    adjacency_later, gathered = lax.optimization_barrier((adjacency, gathered))
-    edges_back = lax.all_to_all(adjacency_later, "nodes", split_axis=0, concat_axis=0, tiled=True)
-
-    self_part = mat_product(hidden_half, pair_half[0, 0])
-    neigh_part = mat_product(gathered, pair_half[0, 1])
-    joined = to_half(jnp.concatenate([self_part, neigh_part], axis=1))
-    linear = mat_product(joined, merge_half[0])
-    active = linear * jax.nn.sigmoid(linear)
-    scale = lax.rsqrt(jnp.sum(active * active, axis=1, keepdims=True) + norm_eps)
-    output = active * scale
-    final_half = to_half(output)
-    logits = mat_product(final_half, head_half)
-    truth = labels.astype(jnp.float32)
-    row_mask = labelled.astype(jnp.float32)[:, None]
-    denom = label_count[0].astype(jnp.float32) * logits.shape[1]
-    per_entry = jnp.maximum(logits, 0.0) - logits * truth + jnp.log1p(jnp.exp(-jnp.abs(logits)))
-    loss_part = jnp.sum(per_entry * row_mask) / denom
-    grad_logits = to_half((jax.nn.sigmoid(logits) - truth) * row_mask / denom)
-    head_grad = left_product(final_half, grad_logits)
-    grad_out = right_product(grad_logits, head_half)
-    grad_active = scale * (grad_out - output * jnp.sum(grad_out * output, axis=1, keepdims=True))
-    sig_value = jax.nn.sigmoid(linear)
-    grad_linear = to_half(grad_active * sig_value * (1.0 + linear * (1.0 - sig_value)))
-    merge_grad = left_product(joined, grad_linear)
-    grad_joined = to_half(right_product(grad_linear, merge_half[0]))
-    grad_self_out = grad_joined[:, :hidden_width]
-    grad_neigh_out = grad_joined[:, hidden_width:]
-    grad_self = left_product(hidden_half, grad_self_out)
-    grad_neigh = left_product(gathered, grad_neigh_out)
-    grad_gathered = to_half(right_product(grad_neigh_out, pair_half[0, 1]))
-    label_width = head_grad.shape[1]
-    spread = jnp.zeros((hidden_width, LANES - label_width), jnp.float32)
-    spread = spread.at[0, 0].set(loss_part)
-    head_wide = jnp.concatenate([head_grad, spread], axis=1).reshape(-1, hidden_width)
-    part = jnp.concatenate([grad_self, grad_neigh, merge_grad, head_wide], axis=0)
-    part_rows = Summer.padded(n, part.shape[0], hidden_width)
-    part = jnp.pad(part, ((0, part_rows - part.shape[0]), (0, 0)))
+    later, got = lax.optimization_barrier((adjacency, got))
+    edges_back = lax.all_to_all(later, "nodes", split_axis=0, concat_axis=0, tiled=True)
+    label_width = labels.shape[1]
+    head_wide = jnp.pad(head_half, ((0, 0), (0, LANES - label_width)))
+    part_rows = Summer.padded(n, 4 * hidden_width + LANES, hidden_width)
+    grad_self, grad_gathered, part, loss_part = dense(
+        min(TILE, row_count),
+        PIECES,
+        part_rows,
+        slots,
+        (label_count, raw),
+        adjacency,
+        got,
+        labelled,
+        labels,
+        hidden_half,
+        (pair_half[0], merge_half[0], head_wide),
+    )
     back, total = swap(1, grad_gathered.reshape(block_count, block_rows, hidden_width), part)
-    pair_grad = total[: 2 * hidden_width].reshape(pair_weight.shape)
-    merge_grad = total[2 * hidden_width : 4 * hidden_width].reshape(merge_weight.shape)
-    head_wide = total[4 * hidden_width : 4 * hidden_width + head_wide.shape[0]]
-    head_wide = head_wide.reshape(hidden_width, LANES)
-    head_grad = head_wide[:, :label_width]
-    loss_total = head_wide[0, label_width]
-
-    grad_hidden = gather_sum(
-        True, row_wish, plan[0], edges_back, back, block_count, grad_joined, pair_half[0, 0]
-    ).reshape(row_count, hidden_width)
-    embed_grad = finish(n, features.T, grad_hidden, 1)[: features.shape[1]]
-    pair_next = adam_update(pair_weight, pair_grad, pair_moment, pair_variance)
-    merge_next = adam_update(merge_weight, merge_grad, merge_moment, merge_variance)
-    head_next = adam_update(head_weight, head_grad, head_moment, head_variance)
+    def flat(values):
+        return values.reshape(-1, hidden_width)
+
+    grad_hidden, pair_next, merge_next, head_next = return_sum(
+        row_wish,
+        plan.reshape(-1, LANES),
+        edges_back,
+        back,
+        block_count,
+        grad_self,
+        pair_half[0, 0],
+        total,
+        (
+            (flat(pair_weight), flat(pair_moment), flat(pair_variance)),
+            (flat(merge_weight), flat(merge_moment), flat(merge_variance)),
+        ),
+        (head_weight, head_moment, head_variance),
+    )
+    pair_next = [values.reshape(pair_weight.shape) for values in pair_next]
+    merge_next = [values.reshape(merge_weight.shape) for values in merge_next]
+    grad_hidden = grad_hidden.reshape(row_count, hidden_width)
+    embed_grad, loss_total = finish(n, features.T, grad_hidden, loss_part, 1)
     embed_next = adam_update(embed_weight, embed_grad, embed_moment, embed_variance)
     return (
         loss_total.reshape(1),

time: 541 us -> 465 us (0.86)
  matrix products: 65.5 us -> 0 us
  other arithmetic: 25.7 us -> 10.5 us
  local copies, waits for them, and re-layouts: 15.1 us -> 3.25 us
  loops' own time: 0.44 us -> 10.3 us
  Pallas kernels: 419 us -> 427 us
    dot_general x11 -> x0, matrix products: 65.5 us -> none  [the longest x4 25.1 us: left_product(): lax.dot_general(former, latter, (((0,), (0,)), ((), ())), preferred_eleme...]
    pallas_call x2, Pallas kernels: 30.3 us -> 71 us  [the longest x1 48.8 us: dense(): pl.pallas_call(functools.partial(dense_kernel, label_width, pieces, slots...]
    pallas_call x1, Pallas kernels: 192 us -> 166 us  [exchange(): pl.pallas_call(functools.partial(exchange_sum_kernel, moves, summer), out...]
    sub x4 -> x1, other arithmetic: 16.4 us -> 3.83 us  [adam_update(): weight - learn_rate * (first_hat / (jnp.sqrt(second_hat) + adam_eps) + de...]
    pallas_call x1, Pallas kernels: 149 us -> 138 us  [exchange(): pl.pallas_call(functools.partial(exchange_kernel, moves), out_shape=moves...]
    another operation x2, loops' own time: 0.44 us -> 10.3 us  [swap(): return lax.switch(rung_of[way].reshape(()), branches, plan, *held)]
  transfers between devices with their start and end apart: 1 -> 1, of which waited for: 0 -> 0; matrix products, arithmetic and copies ran while one was open for 18% -> 1% of each run, Pallas kernels for 36% -> 47%
where the time goes in v3:
time: 465 us; the launch traced here: 457 us
  Pallas kernels  427 us (92%)
  other arithmetic  10.5 us (2%)
  loops' own time  10.3 us (2%)
    pallas_call x1, Pallas kernels, exchange(): pl.pallas_call(functools.partial(exchange_sum_kernel, moves, summer), out...  166 us
    pallas_call x1, Pallas kernels, exchange(): pl.pallas_call(functools.partial(exchange_kernel, moves), out_shape=moves...  138 us
    pallas_call x1, Pallas kernels, dense(): pl.pallas_call(functools.partial(dense_kernel, label_width, pieces, slots...  48.8 us
    pallas_call x1, Pallas kernels, finish(): pl.pallas_call(functools.partial(finish_kernel, n, 1024), out_shape=jax.S...  33.5 us
    pallas_call x1, Pallas kernels, return_sum(): pl.pallas_call(functools.partial(return_sum_kernel, slots, first_row), ou...  22.3 us
    pallas_call x1, Pallas kernels, prelude(): pl.pallas_call(functools.partial(prelude_kernel, n, slots, blocks, rungs,...  17.3 us
    another operation x2, loops' own time, swap(): return lax.switch(rung_of[way].reshape(()), branches, plan, *held)  10.3 us
  transfers between devices with their start and end apart: 1, of which 0 were waited for; matrix products, arithmetic and copies ran while one was open for 1% of the time, Pallas kernels for 47%

profile of v3, /device:TPU:0, one launch (start us, length us, event | category | flops | bytes accessed | tf_op | source)
XLA Modules:
  0.0 457.3 jit_solution(8295921483607869403)
XLA Ops:
  0.6 0.7 iota_compare_fusion
  1.3 0.7 add_select_fusion
  2.0 0.6 pad.8.sinks
  2.6 17.3 %prelude.1 = (bf16[4096,512]{1,0:T(8,128)(2,1)}, s32[2,16,128]{2,1,0:T(8,128)S(1)}, s32[1,1]{1,0:T(1,128)}, s32[1,1]{1,0:T(1,128)}) custom-call(s32[1,512]{1,0:T(1,128)} %bitcast.51, bf16[602,4096]{1,0:T(8,128)(2,1)} %bitcast.41, f32[602,512]{1,0:T(8,128)} %refs_2_.1), custom_call_target="tpu_custom_call" | custom-call | tf_op jit(solution)/shard_map/prelude/pallas_call | solution.py:953
  20.6 148.3 %conditional.2 = (bf16[8,8,4,2,16,512]{5,4,3,2,1,0:T(8,128)(2,1)}) conditional(s32[]{:T(128)} %bitcast.6, (s32[2,16,128]{2,1,0:T(8,128)S(1)}, bf16[32,128,512]{2,1,0:T(8,128)(2,1)}) %tuple.42, (s32[2,16,128]{2,1,0:T(8,128)S(1)}, bf16[32,128,512]{2,1,0:T(8,128)(2,1)}) %tuple.43, (s32[2,16,128]{2,1,0:T(8,128)S(1)}, ...), branch_computations={%region_0.1_spmd, %region_1.2_spmd, %region_2.3_spmd} | conditional | bytes 8 | solution.py:1156
  20.6 138.5 %exchange.3 = bf16[8,8,4,2,16,512]{5,4,3,2,1,0:T(8,128)(2,1)} custom-call(s32[2,16,128]{2,1,0:T(8,128)S(1)} %get-tuple-element.31.plan, bf16[32,128,512]{2,1,0:T(8,128)(2,1)} %get-tuple-element.32.table), custom_call_target="tpu_custom_call" | custom-call | tf_op jit(solution)/shard_map/cond/branch_0_fun/exchange/pallas_call | solution.py:653
  168.9 0.0 copy-start.1
  168.9 0.0 copy-start
  168.9 3.6 all-to-all-start
  173.9 1.1 convert_element_type.14
  175.0 0.7 pad.9.refs_5_
  175.7 1.1 convert_bitcast_fusion.1.refs_3_
  176.8 0.9 copy-done.4
  177.7 1.1 convert_bitcast_fusion.refs_4_
  178.8 48.8 %dense.1 = (bf16[4096,512]{1,0:T(8,128)(2,1)}, bf16[4096,512]{1,0:T(8,128)(2,1)}, f32[2176,512]{1,0:T(8,128)}, f32[1,1]{1,0:T(1,128)}) custom-call(s32[1]{0:T(128)S(6)} %copy.42.count, s32[4,128]{1,0:T(4,128)} %pad.8.sinks, bf16[4,8,2,128,128]{4,3,2,1,0:T(8,128)(2,1)} %bitcast.43, bf16[8,8,4,2,16,512]{5,4,3,2,1,0:T(8,128)(2,1)} %get-tuple-element.115.got, ...), custom_call_target="tpu_custom_call" | custom-call | tf_op jit(solution)/shard_map/dense/pallas_call | solution.py:1073
  227.5 0.0 copy-start.3
  227.6 166.8 %conditional.3 = ((bf16[8,8,4,2,16,512]{5,4,3,2,1,0:T(8,128)(2,1)}, bf16[2176,512]{1,0:T(8,128)(2,1)})) conditional(s32[]{:T(128)} %bitcast.9, (s32[2,16,128]{2,1,0:T(8,128)S(1)}, bf16[32,128,512]{2,1,0:T(8,128)(2,1)}, f32[2176,512]{1,0:T(8,128)}) %tuple.45, (s32[2,16,128]{2,1,0:T(8,128)S(1)}, bf16[32,128,512]{2,1,0:T(8,128)(2,1)}, ...), branch_computations={%region_3.4_spmd, %region_4.5_spmd, %region_5.6_spmd} | conditional | bytes 8 | solution.py:1156
  227.8 166.4 %exchange_sum.4 = (bf16[8,8,4,2,16,512]{5,4,3,2,1,0:T(8,128)(2,1)}, bf16[2176,512]{1,0:T(8,128)(2,1)}) custom-call(s32[2,16,128]{2,1,0:T(8,128)S(1)} %get-tuple-element.43.plan, bf16[32,128,512]{2,1,0:T(8,128)(2,1)} %get-tuple-element.44.table, f32[2176,512]{1,0:T(8,128)} %get-tuple-element.45.part), custom_call_target="tpu_custom_call" | custom-call | tf_op jit(solution)/shard_map/cond/branch_1_fun/exchange_sum/pallas_call | solution.py:663
  394.4 1.1 slice_bitcast_fusion.refs_4_
  395.5 22.3 %return_sum.1 = (bf16[32,128,512]{2,1,0:T(8,128)(2,1)}, f32[1024,512]{1,0:T(8,128)}, f32[1024,512]{1,0:T(8,128)}, f32[1024,512]{1,0:T(8,128)}, f32[1024,512]{1,0...) custom-call(s32[32,128]{1,0:T(8,128)S(1)} %bitcast.50, ...), custom_call_target="tpu_custom_call" | custom-call | tf_op jit(solution)/shard_map/return_sum/pallas_call | solution.py:763
  417.8 33.5 %finish.1 = bf16[640,512]{1,0:T(8,128)(2,1)} custom-call(bf16[602,4096]{1,0:T(8,128)(2,1)} %bitcast.42, bf16[4096,512]{1,0:T(8,128)(2,1)} %bitcast.45, f32[1,1]{1,0:T(1,128)} %get-tuple-element.96.loss), custom_call_target="tpu_custom_call" | custom-call | tf_op jit(solution)/shard_map/finish/pallas_call | solution.py:311
  451.3 1.3 convert_element_type.17
  452.6 0.6 slice_reduce_fusion
  453.3 3.8 multiply_subtract_fusion
  (12 shorter events, 0.0 us)
Async XLA Ops:
  168.9 3.7 copy-start.1
  168.9 5.0 %copy-start = (f32[1,2,512,512]{3,2,1,0:T(8,128)S(1)}, f32[1,2,512,512]{3,2,1,0:T(8,128)}, u32[]{:S(2)}) copy-start(f32[1,2,512,512]{3,2,1,0:T(8,128)} %param.35) | copy-start | bytes 6291460
  168.9 226.5 %all-to-all-start = ((bf16[64,128,128]{2,1,0:T(8,128)(2,1)}), bf16[64,128,128]{2,1,0:T(8,128)(2,1)}, u32[]{:S(2)}, u32[]{:S(2)}) async-start(bf16[64,128,128]{2,1,0:T(8,128)(2,1)} %param.33), calls=%async_computation | async-start | bytes 4194304 | tf_op jit(solution)/shard_map/all_to_all | solution.py:1163
  175.7 2.0 copy-start.4
  227.5 168.0 %copy-start.2 = (f32[512,121]{1,0:T(8,128)S(1)}, f32[512,121]{1,0:T(8,128)}, u32[]{:S(2)}) copy-start(f32[512,121]{1,0:T(8,128)} %refs_15_.1) | copy-start | bytes 743428
  227.5 168.0 %copy-start.3 = (f32[512,121]{1,0:T(8,128)S(1)}, f32[512,121]{1,0:T(8,128)}, u32[]{:S(2)}) copy-start(f32[512,121]{1,0:T(8,128)} %refs_16_.1) | copy-start | bytes 743428
  417.8 35.5 %copy-start.6 = (f32[602,512]{1,0:T(8,128)S(1)}, f32[602,512]{1,0:T(8,128)}, u32[]{:S(2)}) copy-start(f32[602,512]{1,0:T(8,128)} %param.38) | copy-start | bytes 3698692
  451.3 2.0 copy-start.5

commit v4 on v3

--- a/solution.py
+++ b/solution.py
@@ -22,11 +22,12 @@
 AHEAD = 3
 NEAR_AHEAD = 3
 LEAD = 2
-UNROLL = False
 LANES = 128
 VMEM_MOST = 60 * 2**20
 TILE = 1024
 PIECES = 2
+STAGES = 9
+SKEW = 2
 SUM_AT = (0, 2, 9, 13, 17, 20, 24, 30, 32)
 MESH = pl.DeviceIdType.MESH
 
@@ -329,8 +330,8 @@
         ),
         name="finish",
     )(rows, grads, loss)
-    total = total.astype(jnp.float32)
-    return total[: rows.shape[0]], jnp.sum(total[count : count + 3, 0])
+    loss = jnp.sum(total[count : count + 3, 0].astype(jnp.float32))
+    return total[: rows.shape[0]].astype(jnp.float32), loss
 
 
 class Exchange:
@@ -357,40 +358,33 @@
         steps, ring = self.steps, self.ring
         dma = pltpu.SemaphoreType.DMA
         return (
-            [piece(self.far_cap) for _ in range(steps)]
-            + [piece(self.near_cap) for _ in range(2 * steps)]
-            + [piece(self.far_cap) for _ in range(2 * steps)]
-            + [piece(self.near_cap) for _ in range(2 * steps)]
-            + [piece(self.size, 2, self.slots) for _ in range(2 * ring)]
-            + [dma((steps,)), dma((steps,)), dma((steps,)), dma((2, steps)), dma((2, steps))]
-            + [dma((2, ring)), dma((CHUNKS,))]
+            [piece(self.near_cap) for _ in range(steps)]
+            + [piece(2, self.far_cap) for _ in range(steps)]
+            + [piece(steps, self.far_cap), piece(steps, self.near_cap)]
+            + [piece(steps, 2, self.near_cap)]
+            + [piece(ring, self.size, 2, self.slots) for _ in range(2)]
+            + [dma, dma, dma, dma((steps,)), dma((steps,)), dma((2, ring)), dma((CHUNKS,))]
         )
 
     def bind(self, plan, table, out, refs):
         self.plan, self.table, self.out = plan.at[self.way], table, out
-        rest = list(refs)
         steps = self.steps
-
-        def take(count):
-            found = rest[:count]
-            del rest[:count]
-            return found
-
-        self.far_stage = take(steps)
-        self.near_stage = take(steps)
-        self.near_got = take(steps)
-        self.far_got = [take(steps), take(steps)]
-        self.pass_stage = [take(steps), take(steps)]
-        self.serve_stage = [take(self.ring), take(self.ring)]
+        self.near_got, self.far_got = refs[:steps], refs[steps : 2 * steps]
         (
+            self.far_stage,
+            self.near_stage,
+            self.pass_stage,
+            first_stage,
+            second_stage,
             self.far_sent,
             self.near_sent,
+            self.pass_sent,
             self.near_recv,
             self.far_recv,
-            self.pass_sent,
             self.serve_sent,
             self.serve_recv,
-        ) = rest
+        ) = refs[2 * steps :]
+        self.serve_stage = (first_stage, second_stage)
         me = lax.axis_index("nodes")
         self.z, self.spot, self.inner, near, far_in, far_out = place(me, self.size)
         self.near_dev = near * self.size + self.spot
@@ -447,69 +441,55 @@
 
     def launch_far(self, step):
         rows, cols = self.window(step)
-        plan, table, far_stage = self.plan, self.table, self.far_stage[step]
-
-        def fill_far(at, carry):
-            far_stage[at] = table[plan[ROW_FAR, at], rows, cols]
+        plan, table, stage = self.plan, self.table, self.far_stage.at[step]
+
+        def fill(at, carry):
+            stage[at] = table[plan[ROW_FAR, at], rows, cols]
             return carry
 
-        lax.fori_loop(0, self.far_cap, fill_far, 0, unroll=UNROLL)
-        for lane in range(2):
-
-            @pl.when(self.inner == 1 - lane)
-            def _():
-                self.remote(
-                    far_stage,
-                    self.far_got[lane][step],
-                    self.far_sent.at[step],
-                    self.far_recv.at[lane, step],
-                    self.relay_dev,
-                ).start()
+        lax.fori_loop(0, self.far_cap, fill, 0)
+        self.remote(
+            stage,
+            self.far_got[step].at[1 - self.inner],
+            self.far_sent,
+            self.far_recv.at[step],
+            self.relay_dev,
+        ).start()
 
     def launch_near(self, step):
         rows, cols = self.window(step)
-        plan, table, near_stage = self.plan, self.table, self.near_stage[step]
-
-        def fill_near(at, carry):
-            near_stage[at] = table[plan[ROW_NEAR, at], rows, cols]
+        plan, table, stage = self.plan, self.table, self.near_stage.at[step]
+
+        def fill(at, carry):
+            stage[at] = table[plan[ROW_NEAR, at], rows, cols]
             return carry
 
-        lax.fori_loop(0, self.near_cap, fill_near, 0, unroll=UNROLL)
+        lax.fori_loop(0, self.near_cap, fill, 0)
         self.remote(
-            near_stage,
-            self.near_got[step],
-            self.near_sent.at[step],
-            self.near_recv.at[step],
-            self.near_dev,
+            stage, self.near_got[step], self.near_sent, self.near_recv.at[step], self.near_dev
         ).start()
 
     def relay(self, step):
-        plan = self.plan
+        plan, got, stage = self.plan, self.far_got[step], self.pass_stage.at[step]
+        part = got.at[:, pl.ds(0, self.near_cap)]
 
         @pl.when(self.inner == 1)
         def _():
-            for lane in range(2):
-                got, stage = self.far_got[lane][step], self.pass_stage[lane][step]
-                self.settle(self.far_recv.at[lane, step], got)
-
-                def fill(at, carry):
-                    stage[at] = got[plan[ROW_PASS + lane, at]]
-                    return carry
-
-                lax.fori_loop(0, self.near_cap, fill, 0, unroll=UNROLL)
-                self.remote(
-                    stage,
-                    got.at[pl.ds(0, self.near_cap)],
-                    self.pass_sent.at[lane, step],
-                    self.far_recv.at[lane, step],
-                    self.near_dev,
-                ).start()
+            self.settle(self.far_recv.at[step], got)
+
+            def fill(at, carry):
+                for lane in range(2):
+                    stage[lane, at] = got[lane, plan[ROW_PASS + lane, at]]
+                return carry
+
+            lax.fori_loop(0, self.near_cap, fill, 0)
+            self.remote(
+                stage, part, self.pass_sent, self.far_recv.at[step], self.near_dev
+            ).start()
 
         @pl.when(self.inner == 0)
         def _():
-            for lane in range(2):
-                got = self.far_got[lane][step].at[pl.ds(0, self.near_cap)]
-                self.settle(self.far_recv.at[lane, step], got)
+            self.settle(self.far_recv.at[step], part)
 
     def serve(self, step, pair):
         rows, cols = self.window(step)
@@ -519,7 +499,7 @@
             self.settle(self.near_recv.at[step], self.near_got[step])
         if step >= self.ring:
             self.drain(step - self.ring, pair)
-        stage = self.serve_stage[pair][slot_at]
+        stage = self.serve_stage[pair].at[slot_at]
 
         def fill(peer, carry):
             taker = self.z * size + peer
@@ -530,8 +510,8 @@
                     stage[peer, 0, slot] = table[first, rows, cols]
                     stage[peer, 1, slot] = self.near_got[step][second]
                 else:
-                    stage[peer, 0, slot] = self.far_got[0][step][first]
-                    stage[peer, 1, slot] = self.far_got[1][step][second]
+                    stage[peer, 0, slot] = self.far_got[step][0, first]
+                    stage[peer, 1, slot] = self.far_got[step][1, second]
             return carry
 
         lax.fori_loop(0, size, fill, 0)
@@ -553,7 +533,7 @@
 
     def drain(self, step, pair):
         slot_at = step % self.ring
-        held = self.serve_stage[pair][slot_at].at[pl.ds(0, self.size - 1)]
+        held = self.serve_stage[pair].at[slot_at, pl.ds(0, self.size - 1)]
         self.settle(self.serve_sent.at[pair, slot_at], held)
 
     def run(self, side=None):
@@ -596,18 +576,18 @@
             side(steps)
         for chunk in range(CHUNKS):
             self.settle(self.serve_recv.at[chunk], self.out.at[chunk])
-        for step in range(max(0, steps - self.ring), steps):
-            self.drain(step, 0)
-            self.drain(step, 1)
-        for step in range(steps):
-            self.settle(self.far_sent.at[step], self.far_stage[step])
-            self.settle(self.near_sent.at[step], self.near_stage[step])
+        def drain(at, carry):
+            for pair in range(2):
+                self.drain(at, pair)
+            return carry
+
+        lax.fori_loop(0, self.ring, drain, 0)
+        self.settle(self.far_sent, self.far_stage)
+        self.settle(self.near_sent, self.near_stage)
 
         @pl.when(self.inner == 1)
         def _():
-            for step in range(steps):
-                for lane in range(2):
-                    self.settle(self.pass_sent.at[lane, step], self.pass_stage[lane][step])
+            self.settle(self.pass_sent, self.pass_stage)
 
 
 def exchange_kernel(moves, plan, table, out, held_table, table_sem, *refs):
@@ -690,13 +670,14 @@
 def return_sum_kernel(slots, first_row, *refs):
     sinks, weights, got, own, mixer = refs[:5]
     states, head_state, out = refs[5:13], refs[13:17], refs[17]
-    updates, head_update, total = refs[18:24], refs[24:27], refs[27]
+    updates, head_update, total, mixer_half = refs[18:24], refs[24:27], refs[27], refs[28]
     at = pl.program_id(0)
     blocks, depth, width = out.shape
 
     @pl.when(at == 0)
     def _():
         total[...] = jnp.zeros_like(total)
+        mixer_half[...] = to_half(mixer[0])
         label_width = head_state[0].shape[1]
         head_grad = head_state[1][...].astype(jnp.float32).T[:, :label_width]
         fresh = adam_update(head_state[0][...], head_grad, head_state[2][...], head_state[3][...])
@@ -704,7 +685,7 @@
             to[...] = values
 
     span = own.shape[0] // depth
-    base = right_product(own[...], mixer[...]).reshape(span, depth, width)
+    base = right_product(own[...], mixer_half[...]).reshape(span, depth, width)
     total[pl.ds(at * span, span)] += base
     for state, update in ((states[:4], updates[:3]), (states[4:], updates[3:])):
         grad = state[1][...].astype(jnp.float32)
@@ -743,7 +724,7 @@
     tile = blocks * depth // size
     specs = specs + [
         pl.BlockSpec((tile, width), lambda at, sinks: (at, 0)),
-        pl.BlockSpec((width, width), lambda at, sinks: (0, 0)),
+        pl.BlockSpec((1, width, width), lambda at, sinks: (0, 0, 0)),
     ]
     states, shapes, out_specs = [], [], []
     for place_at, (weight, first, second) in enumerate(groups):
@@ -769,7 +750,10 @@
             in_specs=specs,
             out_specs=[pl.BlockSpec((blocks, depth, width), lambda at, sinks: (0, 0, 0))]
             + out_specs,
-            scratch_shapes=[pltpu.VMEM((blocks + 1, depth, width), jnp.float32)],
+            scratch_shapes=[
+                pltpu.VMEM((blocks + 1, depth, width), jnp.float32),
+                pltpu.VMEM((width, width), jnp.bfloat16),
+            ],
         ),
         compiler_params=pltpu.CompilerParams(vmem_limit_bytes=48 * 2**20),
         name="return_sum",
@@ -825,7 +809,7 @@
     def put(row, values):
         plan[way, pl.ds(row, 1), :] = values.astype(jnp.int32)
 
-    chosen[...] = rung.astype(jnp.int32)
+    chosen[...] = len(rungs) - 1 - rung.astype(jnp.int32)
     block_id = lax.broadcasted_iota(jnp.int32, (blocks, LANES), 0)
     block_lane = lax.broadcasted_iota(jnp.int32, (blocks, LANES), 1)
     ids = block_id.astype(jnp.float32)
@@ -865,10 +849,10 @@
 
 
 def prelude_kernel(n, slots, blocks, rungs, tile, *refs):
-    mine, rows, weight, hidden, plan = refs[:5]
-    chosen, taken = refs[5:7], refs[7]
-    wishes = refs[8 : 8 + 2 * slots]
-    present, held, held_weight, row_sem, weight_sem, send_sem, recv_sem = refs[8 + 2 * slots :]
+    need, target, alive, rows, weight, hidden, plan = refs[:7]
+    chosen, sunk, mine, taken = refs[7:9], refs[9], refs[10], refs[11]
+    wishes = refs[12 : 12 + 2 * slots]
+    present, held, held_weight, row_sem, weight_sem, send_sem, recv_sem = refs[12 + 2 * slots :]
     tiles = rows.shape[1] // tile
 
     def window(at):
@@ -892,6 +876,14 @@
         return carry
 
     lax.fori_loop(1, n, greet, 0)
+    mine[...] = jnp.full(mine.shape, blocks, jnp.int32)
+    sunk[...] = jnp.full(sunk.shape, blocks, jnp.int32)
+    for slot in range(slots):
+        live = slot < alive[...]
+        sunk_row = jnp.where(live, target[pl.ds(slot, 1), :], blocks)
+        mine[:, pl.ds(slot * LANES, n)] = jnp.where(live, need[pl.ds(slot, 1), :], blocks)
+        mine[:, pl.ds((slots + slot) * LANES, n)] = sunk_row
+        sunk[pl.ds(slot, 1), pl.ds(0, n)] = sunk_row
     taken[me] = mine[...]
     fetch_weight.wait()
     half_weight = to_half(held_weight[...])
@@ -946,7 +938,7 @@
         )
 
 
-def prelude(n, slots, blocks, rungs, mine, rows, weight):
+def prelude(n, slots, blocks, rungs, need, target, alive, rows, weight):
     count, width = rows.shape[1], weight.shape[1]
     vmem = pl.BlockSpec(memory_space=pltpu.VMEM)
     plan_shape = (2, plan_rows(slots)[1], LANES)
@@ -957,10 +949,14 @@
             jax.ShapeDtypeStruct(plan_shape, jnp.int32),
             jax.ShapeDtypeStruct((1, 1), jnp.int32),
             jax.ShapeDtypeStruct((1, 1), jnp.int32),
+            jax.ShapeDtypeStruct((8, LANES), jnp.int32),
         ),
-        in_specs=[vmem, pl.BlockSpec(memory_space=pltpu.HBM), pl.BlockSpec(memory_space=pltpu.HBM)],
-        out_specs=(vmem, vmem, vmem, vmem),
-        scratch_shapes=[pltpu.VMEM((n,) + mine.shape, jnp.int32)]
+        in_specs=[vmem, vmem, vmem] + [pl.BlockSpec(memory_space=pltpu.HBM)] * 2,
+        out_specs=(vmem,) * 5,
+        scratch_shapes=[
+            pltpu.VMEM((1, 2 * slots * LANES), jnp.int32),
+            pltpu.VMEM((n, 1, 2 * slots * LANES), jnp.int32),
+        ]
         + [pltpu.VMEM((n, LANES), jnp.int32) for _ in range(2 * slots)]
         + [
             pltpu.VMEM((n * blocks, LANES), jnp.float32),
@@ -975,7 +971,7 @@
             collective_id=0, has_side_effects=True, vmem_limit_bytes=VMEM_MOST
         ),
         name="prelude",
-    )(mine, rows, weight)
+    )(need, target, alive, rows, weight)
 
 
 def sigmoid(values):
@@ -983,8 +979,9 @@
 
 
 def dense_kernel(label_width, pieces, slots, first_row, count, sinks, edges, got, *refs):
-    marks, truth, own, pair, merge, head = refs[:6]
-    grad_own, grad_taken, part, loss, total = refs[6:]
+    marks, truth, own = refs[:3]
+    grad_own, grad_taken, part, loss, total = refs[6:11]
+    pair, merge, head = refs[11:]
     at = pl.program_id(0)
     gathers = pl.num_programs(0) - total.shape[0] * total.shape[1] // own.shape[0]
 
@@ -993,6 +990,9 @@
         total[...] = jnp.zeros_like(total)
         part[...] = jnp.zeros_like(part)
         loss[...] = jnp.zeros_like(loss)
+        for to, weight in zip((pair, merge), refs[3:5]):
+            to[...] = to_half(weight[...])
+        head[...] = to_half(jnp.pad(refs[5][...], ((0, 0), (0, LANES - label_width))))
 
     @pl.when(at < gathers)
     def _():
@@ -1017,19 +1017,24 @@
     tile = own.shape[0] // pieces
     span = taken.shape[0] // pieces
     denom = count[0].astype(jnp.float32) * float(label_width)
-    for piece in range(pieces):
+
+    def stages(piece):
         rows = pl.ds(piece * tile, tile)
         hidden = own[rows, :]
         gathered = to_half(taken[pl.ds(piece * span, span)]).reshape(tile, width)
         self_part = to_half(mat_product(hidden, pair[0]))
         neigh_part = to_half(mat_product(gathered, pair[1]))
+        yield
         linear = mat_product(self_part, merge[:width]) + mat_product(neigh_part, merge[width:])
+        yield
         sig = sigmoid(linear)
         active = linear * sig
         scale = lax.rsqrt(jnp.sum(active * active, axis=1, keepdims=True) + norm_eps)
         output = active * scale
         final = to_half(output)
+        yield
         logits = mat_product(final, head[...])
+        yield
         labels = truth[rows, :].astype(jnp.float32)
         labels = jnp.pad(labels, ((0, 0), (0, LANES - label_width)))
         marked = marks[0, :, rows].astype(jnp.float32)
@@ -1040,19 +1045,30 @@
         entry = jnp.maximum(logits, 0.0) - logits * labels + jnp.log1p(decay)
         loss[...] += jnp.sum(entry * marked, axis=(0, 1), keepdims=True) / denom
         grad_logits = to_half((sigmoid(logits) - labels) * marked / denom)
+        yield
         part[pl.ds(4 * width, LANES), :] += left_product(grad_logits, final)
         grad_out = right_product(grad_logits, head[...])
+        yield
         along = jnp.sum(grad_out * output, axis=1, keepdims=True)
         grad_active = scale * (grad_out - output * along)
         grad_linear = to_half(grad_active * sig * (1.0 + linear * (1.0 - sig)))
+        yield
         part[pl.ds(2 * width, width), :] += left_product(self_part, grad_linear)
         part[pl.ds(3 * width, width), :] += left_product(neigh_part, grad_linear)
         grad_self = to_half(right_product(grad_linear, merge[:width]))
         grad_neigh = to_half(right_product(grad_linear, merge[width:]))
+        yield
         grad_own[rows, :] = grad_self
         part[pl.ds(0, width), :] += left_product(hidden, grad_self)
         part[pl.ds(width, width), :] += left_product(gathered, grad_neigh)
         grad_taken[rows, :] = to_half(right_product(grad_neigh, pair[1]))
+        yield
+
+    running = [stages(piece) for piece in range(pieces)]
+    for turn in range(STAGES + SKEW * (pieces - 1)):
+        for piece in range(pieces):
+            if 0 <= turn - SKEW * piece < STAGES:
+                next(running[piece])
 
 
 def dense(tile, pieces, part_rows, first_row, scalars, edges, got, marks, truth, own, weights):
@@ -1068,7 +1084,9 @@
     by_rows = pl.BlockSpec((tile, width), lambda at, *_: (later(at), 0))
 
     def whole(values):
-        return pl.BlockSpec(values.shape, lambda at, *_: (0,) * values.ndim)
+        return pl.BlockSpec(
+            values.shape, lambda at, *_: (0,) * values.ndim, pipeline_mode=pl.Buffered(1)
+        )
 
     return pl.pallas_call(
         functools.partial(dense_kernel, label_width, pieces, slots, first_row),
@@ -1094,7 +1112,9 @@
                 pl.BlockSpec((part_rows, width), lambda at, *_: (0, 0)),
                 pl.BlockSpec((1, 1), lambda at, *_: (0, 0)),
             ),
-            scratch_shapes=[pltpu.VMEM((rows // depth + 1, depth, width), jnp.float32)],
+            scratch_shapes=[pltpu.VMEM((rows // depth + 1, depth, width), jnp.float32)]
+            + [pltpu.VMEM(values.shape, jnp.bfloat16) for values in weights[:2]]
+            + [pltpu.VMEM((width, LANES), jnp.bfloat16)],
         ),
         compiler_params=pltpu.CompilerParams(vmem_limit_bytes=VMEM_MOST),
         name="dense",
@@ -1130,16 +1150,20 @@
     n = lax.axis_size("nodes")
     size = n // PLANES
     block_count = row_count // block_rows
-    alive = lax.broadcasted_iota(jnp.int32, need_blocks.shape[1:], 1) < need_count[0][:, None]
-    raw = jnp.stack([need_blocks[0], target_block[0]])
-    raw = jnp.where(alive, raw, block_count).transpose(0, 2, 1).reshape(2 * slots, n)
-    raw = jnp.pad(raw, ((0, 0), (0, LANES - n)), constant_values=block_count)
     near_full = min(block_count, size * slots)
-    rungs = [(21, 14), (23, 15), (block_count, near_full)]
+    rungs = [(22, 15), (24, 16), (block_count, near_full)]
     if near_full > 16 or block_count < 24:
         rungs = rungs[-1:]
-    hidden_half, plan, *rung_of = prelude(
-        n, slots, block_count, rungs, raw.reshape(1, 2 * slots * LANES), features.T, embed_weight
+    hidden_half, plan, *rung_of, sunk = prelude(
+        n,
+        slots,
+        block_count,
+        rungs,
+        need_blocks[0].T,
+        target_block[0].T,
+        need_count,
+        features.T,
+        embed_weight,
     )
     row_wish, _ = plan_rows(slots)
 
@@ -1152,30 +1176,26 @@
 
         if len(rungs) == 1:
             return at(0)(plan, *held)
-        branches = [at(rung) for rung in range(len(rungs))]
+        branches = [at(rung) for rung in reversed(range(len(rungs)))]
         return lax.switch(rung_of[way].reshape(()), branches, plan, *held)
 
-    pair_half = to_half(pair_weight)
-    merge_half = to_half(merge_weight)
-    head_half = to_half(head_weight)
     got = swap(0, hidden_half.reshape(block_count, block_rows, hidden_width))
     later, got = lax.optimization_barrier((adjacency, got))
     edges_back = lax.all_to_all(later, "nodes", split_axis=0, concat_axis=0, tiled=True)
     label_width = labels.shape[1]
-    head_wide = jnp.pad(head_half, ((0, 0), (0, LANES - label_width)))
     part_rows = Summer.padded(n, 4 * hidden_width + LANES, hidden_width)
     grad_self, grad_gathered, part, loss_part = dense(
         min(TILE, row_count),
         PIECES,
         part_rows,
-        slots,
-        (label_count, raw),
+        0,
+        (label_count, sunk),
         adjacency,
         got,
         labelled,
         labels,
         hidden_half,
-        (pair_half[0], merge_half[0], head_wide),
+        (pair_weight[0], merge_weight[0], head_weight),
     )
     back, total = swap(1, grad_gathered.reshape(block_count, block_rows, hidden_width), part)
     def flat(values):
@@ -1188,7 +1208,7 @@
         back,
         block_count,
         grad_self,
-        pair_half[0, 0],
+        pair_weight[0],
         total,
         (
             (flat(pair_weight), flat(pair_moment), flat(pair_variance)),

time: 465 us -> 449 us (0.966)
  other arithmetic: 10.5 us -> 4.85 us
  transfers between devices with their start and end apart: 1 -> 1, of which waited for: 0 -> 0; matrix products, arithmetic and copies ran while one was open for 1% -> 0% of each run, Pallas kernels for 47% -> 47%
where the time goes in v4:
time: 449 us; the launch traced here: 444 us
  Pallas kernels  423 us (94%)
  loops' own time  9.32 us (2%)
  other arithmetic  4.85 us (1%)
    pallas_call x1, Pallas kernels, exchange(): pl.pallas_call(functools.partial(exchange_sum_kernel, moves, summer), out...  163 us
    pallas_call x1, Pallas kernels, exchange(): pl.pallas_call(functools.partial(exchange_kernel, moves), out_shape=moves...  140 us
    pallas_call x1, Pallas kernels, dense(): pl.pallas_call(functools.partial(dense_kernel, label_width, pieces, slots...  45.3 us
    pallas_call x1, Pallas kernels, finish(): pl.pallas_call(functools.partial(finish_kernel, n, 1024), out_shape=jax.S...  34.2 us
    pallas_call x1, Pallas kernels, return_sum(): pl.pallas_call(functools.partial(return_sum_kernel, slots, first_row), ou...  22.3 us
    pallas_call x1, Pallas kernels, prelude(): pl.pallas_call(functools.partial(prelude_kernel, n, slots, blocks, rungs,...  17.3 us
    another operation x2, loops' own time, swap(): return lax.switch(rung_of[way].reshape(()), branches, plan, *held)  9.32 us
  transfers between devices with their start and end apart: 1, of which 0 were waited for; matrix products, arithmetic and copies ran while one was open for 0% of the time, Pallas kernels for 47%

profile of v4, /device:TPU:0, one launch (start us, length us, event | category | flops | bytes accessed | tf_op | source)
XLA Modules:
  0.0 444.2 jit_solution(2348242425719421575)
XLA Ops:
  0.6 17.3 %prelude.1 = (bf16[4096,512]{1,0:T(8,128)(2,1)}, s32[2,16,128]{2,1,0:T(8,128)S(1)}, s32[1,1]{1,0:T(1,128)}, s32[1,1]{1,0:T(1,128)}, s32[8,128]{1,0:T(8,128)}) custom-call(s32[2,32]{1,0:T(2,128)} %bitcast.50, s32[2,32]{1,0:T(2,128)} %bitcast.51, s32[1,32]{1,0:T(1,128)} %refs_2_.1, bf16[602,4096]{1,0:T(8,128)(2,1)} %bitcast.39, f32[602,512]{1,0:T(8,128)} %refs_4_.1), custom_call_target="tpu_custom_call" | custom-call | tf_op jit(solution)/shard_map/prelude/pallas_call | solution.py:945
  18.5 149.3 %conditional.2 = (bf16[8,8,4,2,16,512]{5,4,3,2,1,0:T(8,128)(2,1)}) conditional(s32[]{:T(128)} %bitcast.6, (s32[2,16,128]{2,1,0:T(8,128)S(1)}, bf16[32,128,512]{2,1,0:T(8,128)(2,1)}) %tuple.42, (s32[2,16,128]{2,1,0:T(8,128)S(1)}, bf16[32,128,512]{2,1,0:T(8,128)(2,1)}) %tuple.43, (s32[2,16,128]{2,1,0:T(8,128)S(1)}, ...), branch_computations={%region_0.0_spmd, %region_1.0_spmd, %region_2.0_spmd} | conditional | bytes 8 | solution.py:1180
  18.5 140.4 %exchange.5 = bf16[8,8,4,2,16,512]{5,4,3,2,1,0:T(8,128)(2,1)} custom-call(s32[2,16,128]{2,1,0:T(8,128)S(1)} %get-tuple-element.38.plan, bf16[32,128,512]{2,1,0:T(8,128)(2,1)} %get-tuple-element.39.table), custom_call_target="tpu_custom_call" | custom-call | tf_op jit(solution)/shard_map/cond/branch_2_fun/exchange/pallas_call | solution.py:633
  167.8 4.1 all-to-all-start
  173.2 45.3 %dense.1 = (bf16[4096,512]{1,0:T(8,128)(2,1)}, bf16[4096,512]{1,0:T(8,128)(2,1)}, f32[2176,512]{1,0:T(8,128)}, f32[1,1]{1,0:T(1,128)}) custom-call(s32[1]{0:T(128)S(6)} %copy.42.count, s32[8,128]{1,0:T(8,128)} %get-tuple-element.90.sinks, bf16[4,8,2,128,128]{4,3,2,1,0:T(8,128)(2,1)} %bitcast.10.edges, ...), custom_call_target="tpu_custom_call" | custom-call | tf_op jit(solution)/shard_map/dense/pallas_call | solution.py:1091
  218.5 0.0 copy-start
  218.5 0.0 copy-start.1
  218.5 0.0 copy-start.2
  218.5 0.0 copy-start.3
  218.5 163.8 %conditional.3 = ((bf16[8,8,4,2,16,512]{5,4,3,2,1,0:T(8,128)(2,1)}, bf16[2176,512]{1,0:T(8,128)(2,1)})) conditional(s32[]{:T(128)} %bitcast.9, (s32[2,16,128]{2,1,0:T(8,128)S(1)}, bf16[32,128,512]{2,1,0:T(8,128)(2,1)}, f32[2176,512]{1,0:T(8,128)}) %tuple.45, (s32[2,16,128]{2,1,0:T(8,128)S(1)}, bf16[32,128,512]{2,1,0:T(8,128)(2,1)}, ...), branch_computations={%region_3.0_spmd, %region_4.0_spmd, %region_5.0_spmd} | conditional | bytes 8 | solution.py:1180
  218.8 163.3 %exchange_sum.5 = (bf16[8,8,4,2,16,512]{5,4,3,2,1,0:T(8,128)(2,1)}, bf16[2176,512]{1,0:T(8,128)(2,1)}) custom-call(s32[2,16,128]{2,1,0:T(8,128)S(1)} %get-tuple-element.46.plan, bf16[32,128,512]{2,1,0:T(8,128)(2,1)} %get-tuple-element.47.table, f32[2176,512]{1,0:T(8,128)} %get-tuple-element.48.part), custom_call_target="tpu_custom_call" | custom-call | tf_op jit(solution)/shard_map/cond/branch_2_fun/exchange_sum/pallas_call | solution.py:643
  382.3 0.0 all-to-all-done
  382.3 0.0 copy-done
  382.3 0.0 copy-done.1
  382.3 0.0 copy-done.2
  382.4 0.0 copy-done.3
  382.4 22.3 %return_sum.1 = (bf16[32,128,512]{2,1,0:T(8,128)(2,1)}, f32[1024,512]{1,0:T(8,128)}, f32[1024,512]{1,0:T(8,128)}, f32[1024,512]{1,0:T(8,128)}, f32[1024,512]{1,0...) custom-call(s32[32,128]{1,0:T(8,128)S(1)} %bitcast.48, ...), custom_call_target="tpu_custom_call" | custom-call | tf_op jit(solution)/shard_map/return_sum/pallas_call | solution.py:744
  404.7 0.0 copy-start.4
  404.7 0.0 copy-start.5
  404.7 0.0 copy-start.6
  404.7 34.2 %finish.1 = bf16[640,512]{1,0:T(8,128)(2,1)} custom-call(bf16[602,4096]{1,0:T(8,128)(2,1)} %bitcast.40, bf16[4096,512]{1,0:T(8,128)(2,1)} %bitcast.43, f32[1,1]{1,0:T(1,128)} %get-tuple-element.98.loss), custom_call_target="tpu_custom_call" | custom-call | tf_op jit(solution)/shard_map/finish/pallas_call | solution.py:312
  438.9 1.3 convert_reduce_fusion
  440.1 0.0 copy-done.4
  440.2 3.6 multiply_subtract_fusion
  (2 shorter events, 0.0 us)
Async XLA Ops:
  167.8 214.5 %all-to-all-start = ((bf16[64,128,128]{2,1,0:T(8,128)(2,1)}), bf16[64,128,128]{2,1,0:T(8,128)(2,1)}, u32[]{:S(2)}, u32[]{:S(2)}) async-start(bf16[64,128,128]{2,1,0:T(8,128)(2,1)} %param.33), calls=%async_computation | async-start | bytes 4194304 | tf_op jit(solution)/shard_map/all_to_all | solution.py:1184
  218.5 163.8 %copy-start = (f32[1,2,512,512]{3,2,1,0:T(8,128)S(1)}, f32[1,2,512,512]{3,2,1,0:T(8,128)}, u32[]{:S(2)}) copy-start(f32[1,2,512,512]{3,2,1,0:T(8,128)} %param.35) | copy-start | bytes 6291460
  218.5 163.8 %copy-start.1 = (f32[512,121]{1,0:T(8,128)S(1)}, f32[512,121]{1,0:T(8,128)}, u32[]{:S(2)}) copy-start(f32[512,121]{1,0:T(8,128)} %refs_13_.1) | copy-start | bytes 743428
  218.5 163.8 %copy-start.2 = (f32[512,121]{1,0:T(8,128)S(1)}, f32[512,121]{1,0:T(8,128)}, u32[]{:S(2)}) copy-start(f32[512,121]{1,0:T(8,128)} %refs_15_.1) | copy-start | bytes 743428
  218.5 163.8 %copy-start.3 = (f32[512,121]{1,0:T(8,128)S(1)}, f32[512,121]{1,0:T(8,128)}, u32[]{:S(2)}) copy-start(f32[512,121]{1,0:T(8,128)} %refs_16_.1) | copy-start | bytes 743428
  404.7 35.5 %copy-start.4 = (f32[602,512]{1,0:T(8,128)S(1)}, f32[602,512]{1,0:T(8,128)}, u32[]{:S(2)}) copy-start(f32[602,512]{1,0:T(8,128)} %refs_4_.1) | copy-start | bytes 3698692
  404.7 35.5 %copy-start.5 = (f32[602,512]{1,0:T(8,128)S(1)}, f32[602,512]{1,0:T(8,128)}, u32[]{:S(2)}) copy-start(f32[602,512]{1,0:T(8,128)} %param.38) | copy-start | bytes 3698692
  404.7 35.5 %copy-start.6 = (f32[602,512]{1,0:T(8,128)S(1)}, f32[602,512]{1,0:T(8,128)}, u32[]{:S(2)}) copy-start(f32[602,512]{1,0:T(8,128)} %param.42) | copy-start | bytes 3698692

commit v5 on v4

--- a/solution.py
+++ b/solution.py
@@ -19,8 +19,8 @@
 KINDS = 4
 CHUNKS = 8
 PARTS = 4
-AHEAD = 3
-NEAR_AHEAD = 3
+AHEAD = 4
+NEAR_AHEAD = 4
 LEAD = 2
 LANES = 128
 VMEM_MOST = 60 * 2**20
@@ -28,7 +28,7 @@
 PIECES = 2
 STAGES = 9
 SKEW = 2
-SUM_AT = (0, 2, 9, 13, 17, 20, 24, 30, 32)
+SUM_AT = (0, 2, 8, 11, 14, 17, 20, 26, 32)
 MESH = pl.DeviceIdType.MESH
 
 

time: 449 us -> 444 us (0.989)
  Pallas kernels: 423 us -> 418 us
where the time goes in v5:
time: 444 us; the launch traced here: 439 us
  Pallas kernels  418 us (94%)
  loops' own time  9.32 us (2%)
  other arithmetic  4.85 us (1%)
    pallas_call x1, Pallas kernels, exchange(): pl.pallas_call(functools.partial(exchange_sum_kernel, moves, summer), out...  159 us
    pallas_call x1, Pallas kernels, exchange(): pl.pallas_call(functools.partial(exchange_kernel, moves), out_shape=moves...  140 us
    pallas_call x1, Pallas kernels, dense(): pl.pallas_call(functools.partial(dense_kernel, label_width, pieces, slots...  45.3 us
    pallas_call x1, Pallas kernels, finish(): pl.pallas_call(functools.partial(finish_kernel, n, 1024), out_shape=jax.S...  34 us
    pallas_call x1, Pallas kernels, return_sum(): pl.pallas_call(functools.partial(return_sum_kernel, slots, first_row), ou...  22.3 us
    pallas_call x1, Pallas kernels, prelude(): pl.pallas_call(functools.partial(prelude_kernel, n, slots, blocks, rungs,...  17.3 us
    another operation x2, loops' own time, swap(): return lax.switch(rung_of[way].reshape(()), branches, plan, *held)  9.32 us
  transfers between devices with their start and end apart: 1, of which 0 were waited for; matrix products, arithmetic and copies ran while one was open for 0% of the time, Pallas kernels for 47%

profile of v5, /device:TPU:0, one launch (start us, length us, event | category | flops | bytes accessed | tf_op | source)
XLA Modules:
  0.0 438.8 jit_solution(9531295819603998714)
XLA Ops:
  0.6 17.3 %prelude.1 = (bf16[4096,512]{1,0:T(8,128)(2,1)}, s32[2,16,128]{2,1,0:T(8,128)S(1)}, s32[1,1]{1,0:T(1,128)}, s32[1,1]{1,0:T(1,128)}, s32[8,128]{1,0:T(8,128)}) custom-call(s32[2,32]{1,0:T(2,128)} %bitcast.50, s32[2,32]{1,0:T(2,128)} %bitcast.51, s32[1,32]{1,0:T(1,128)} %refs_2_.1, bf16[602,4096]{1,0:T(8,128)(2,1)} %bitcast.39, f32[602,512]{1,0:T(8,128)} %refs_4_.1), custom_call_target="tpu_custom_call" | custom-call | tf_op jit(solution)/shard_map/prelude/pallas_call | solution.py:945
  18.5 148.9 %conditional.2 = (bf16[8,8,4,2,16,512]{5,4,3,2,1,0:T(8,128)(2,1)}) conditional(s32[]{:T(128)} %bitcast.6, (s32[2,16,128]{2,1,0:T(8,128)S(1)}, bf16[32,128,512]{2,1,0:T(8,128)(2,1)}) %tuple.42, (s32[2,16,128]{2,1,0:T(8,128)S(1)}, bf16[32,128,512]{2,1,0:T(8,128)(2,1)}) %tuple.43, (s32[2,16,128]{2,1,0:T(8,128)S(1)}, ...), branch_computations={%region_0.0_spmd, %region_1.0_spmd, %region_2.0_spmd} | conditional | bytes 8 | solution.py:1180
  18.5 140.0 %exchange.5 = bf16[8,8,4,2,16,512]{5,4,3,2,1,0:T(8,128)(2,1)} custom-call(s32[2,16,128]{2,1,0:T(8,128)S(1)} %get-tuple-element.38.plan, bf16[32,128,512]{2,1,0:T(8,128)(2,1)} %get-tuple-element.39.table), custom_call_target="tpu_custom_call" | custom-call | tf_op jit(solution)/shard_map/cond/branch_2_fun/exchange/pallas_call | solution.py:633
  167.4 3.5 all-to-all-start
  172.2 45.3 %dense.1 = (bf16[4096,512]{1,0:T(8,128)(2,1)}, bf16[4096,512]{1,0:T(8,128)(2,1)}, f32[2176,512]{1,0:T(8,128)}, f32[1,1]{1,0:T(1,128)}) custom-call(s32[1]{0:T(128)S(6)} %copy.42.count, s32[8,128]{1,0:T(8,128)} %get-tuple-element.90.sinks, bf16[4,8,2,128,128]{4,3,2,1,0:T(8,128)(2,1)} %bitcast.10.edges, ...), custom_call_target="tpu_custom_call" | custom-call | tf_op jit(solution)/shard_map/dense/pallas_call | solution.py:1091
  217.5 0.0 copy-start
  217.6 0.0 copy-start.1
  217.6 0.0 copy-start.2
  217.6 0.0 copy-start.3
  217.6 159.5 %conditional.3 = ((bf16[8,8,4,2,16,512]{5,4,3,2,1,0:T(8,128)(2,1)}, bf16[2176,512]{1,0:T(8,128)(2,1)})) conditional(s32[]{:T(128)} %bitcast.9, (s32[2,16,128]{2,1,0:T(8,128)S(1)}, bf16[32,128,512]{2,1,0:T(8,128)(2,1)}, f32[2176,512]{1,0:T(8,128)}) %tuple.45, (s32[2,16,128]{2,1,0:T(8,128)S(1)}, bf16[32,128,512]{2,1,0:T(8,128)(2,1)}, ...), branch_computations={%region_3.0_spmd, %region_4.0_spmd, %region_5.0_spmd} | conditional | bytes 8 | solution.py:1180
  217.8 159.0 %exchange_sum.5 = (bf16[8,8,4,2,16,512]{5,4,3,2,1,0:T(8,128)(2,1)}, bf16[2176,512]{1,0:T(8,128)(2,1)}) custom-call(s32[2,16,128]{2,1,0:T(8,128)S(1)} %get-tuple-element.46.plan, bf16[32,128,512]{2,1,0:T(8,128)(2,1)} %get-tuple-element.47.table, f32[2176,512]{1,0:T(8,128)} %get-tuple-element.48.part), custom_call_target="tpu_custom_call" | custom-call | tf_op jit(solution)/shard_map/cond/branch_2_fun/exchange_sum/pallas_call | solution.py:643
  377.1 0.0 all-to-all-done
  377.1 0.0 copy-done
  377.1 0.0 copy-done.1
  377.1 0.0 copy-done.2
  377.1 0.0 copy-done.3
  377.1 22.3 %return_sum.1 = (bf16[32,128,512]{2,1,0:T(8,128)(2,1)}, f32[1024,512]{1,0:T(8,128)}, f32[1024,512]{1,0:T(8,128)}, f32[1024,512]{1,0:T(8,128)}, f32[1024,512]{1,0...) custom-call(s32[32,128]{1,0:T(8,128)S(1)} %bitcast.48, ...), custom_call_target="tpu_custom_call" | custom-call | tf_op jit(solution)/shard_map/return_sum/pallas_call | solution.py:744
  399.4 0.0 copy-start.4
  399.5 0.0 copy-start.5
  399.5 0.0 copy-start.6
  399.5 34.0 %finish.1 = bf16[640,512]{1,0:T(8,128)(2,1)} custom-call(bf16[602,4096]{1,0:T(8,128)(2,1)} %bitcast.40, bf16[4096,512]{1,0:T(8,128)(2,1)} %bitcast.43, f32[1,1]{1,0:T(1,128)} %get-tuple-element.98.loss), custom_call_target="tpu_custom_call" | custom-call | tf_op jit(solution)/shard_map/finish/pallas_call | solution.py:312
  433.5 1.3 convert_reduce_fusion
  434.8 0.0 copy-done.4
  434.8 3.6 multiply_subtract_fusion
  (2 shorter events, 0.0 us)
Async XLA Ops:
  167.4 209.7 %all-to-all-start = ((bf16[64,128,128]{2,1,0:T(8,128)(2,1)}), bf16[64,128,128]{2,1,0:T(8,128)(2,1)}, u32[]{:S(2)}, u32[]{:S(2)}) async-start(bf16[64,128,128]{2,1,0:T(8,128)(2,1)} %param.33), calls=%async_computation | async-start | bytes 4194304 | tf_op jit(solution)/shard_map/all_to_all | solution.py:1184
  217.5 159.6 %copy-start = (f32[1,2,512,512]{3,2,1,0:T(8,128)S(1)}, f32[1,2,512,512]{3,2,1,0:T(8,128)}, u32[]{:S(2)}) copy-start(f32[1,2,512,512]{3,2,1,0:T(8,128)} %param.35) | copy-start | bytes 6291460
  217.6 159.5 %copy-start.1 = (f32[512,121]{1,0:T(8,128)S(1)}, f32[512,121]{1,0:T(8,128)}, u32[]{:S(2)}) copy-start(f32[512,121]{1,0:T(8,128)} %refs_13_.1) | copy-start | bytes 743428
  217.6 159.5 %copy-start.2 = (f32[512,121]{1,0:T(8,128)S(1)}, f32[512,121]{1,0:T(8,128)}, u32[]{:S(2)}) copy-start(f32[512,121]{1,0:T(8,128)} %refs_15_.1) | copy-start | bytes 743428
  217.6 159.5 %copy-start.3 = (f32[512,121]{1,0:T(8,128)S(1)}, f32[512,121]{1,0:T(8,128)}, u32[]{:S(2)}) copy-start(f32[512,121]{1,0:T(8,128)} %refs_16_.1) | copy-start | bytes 743428
  399.4 35.4 %copy-start.4 = (f32[602,512]{1,0:T(8,128)S(1)}, f32[602,512]{1,0:T(8,128)}, u32[]{:S(2)}) copy-start(f32[602,512]{1,0:T(8,128)} %refs_4_.1) | copy-start | bytes 3698692
  399.5 35.4 %copy-start.5 = (f32[602,512]{1,0:T(8,128)S(1)}, f32[602,512]{1,0:T(8,128)}, u32[]{:S(2)}) copy-start(f32[602,512]{1,0:T(8,128)} %param.38) | copy-start | bytes 3698692
  399.5 35.4 %copy-start.6 = (f32[602,512]{1,0:T(8,128)S(1)}, f32[602,512]{1,0:T(8,128)}, u32[]{:S(2)}) copy-start(f32[602,512]{1,0:T(8,128)} %param.42) | copy-start | bytes 3698692

commit v6 on v5

--- a/solution.py
+++ b/solution.py
@@ -18,17 +18,16 @@
 PLANES = 4
 KINDS = 4
 CHUNKS = 8
-PARTS = 4
-AHEAD = 4
-NEAR_AHEAD = 4
-LEAD = 2
 LANES = 128
 VMEM_MOST = 60 * 2**20
 TILE = 1024
 PIECES = 2
 STAGES = 9
 SKEW = 2
-SUM_AT = (0, 2, 8, 11, 14, 17, 20, 26, 32)
+PACE = {
+    4: (4, 2, (0, 2, 8, 11, 14, 17, 20, 26, 32)),
+    2: (3, 1, (0, 1, 4, 6, 8, 9, 11, 14, 16)),
+}
 MESH = pl.DeviceIdType.MESH
 
 
@@ -335,15 +334,16 @@
 
 
 class Exchange:
-    def __init__(self, n, slots, way, far_cap, near_cap, shape, kind):
-        self.n, self.slots, self.way = n, slots, way
+    def __init__(self, n, slots, way, parts, far_cap, near_cap, shape, kind):
+        self.n, self.slots, self.way, self.parts = n, slots, way, parts
+        self.ahead, self.lead, self.sum_at = PACE[parts]
         self.far_cap, self.near_cap = far_cap, near_cap
         self.size = n // PLANES
         self.blocks, self.depth, self.width = shape
         self.kind = kind
         self.rows = self.depth // CHUNKS
-        self.cols = self.width // PARTS
-        self.steps = CHUNKS * PARTS
+        self.cols = self.width // self.parts
+        self.steps = CHUNKS * self.parts
         self.ring = self.steps if self.size <= 8 else 2
 
     def out_shape(self):
@@ -421,8 +421,8 @@
         pl.semaphore_wait(barrier, self.size + 1)
 
     def window(self, step):
-        return pl.ds((step // PARTS) * self.rows, self.rows), pl.ds(
-            (step % PARTS) * self.cols, self.cols
+        return pl.ds((step // self.parts) * self.rows, self.rows), pl.ds(
+            (step % self.parts) * self.cols, self.cols
         )
 
     def remote(self, src, dst, sent, got, device):
@@ -494,7 +494,7 @@
     def serve(self, step, pair):
         rows, cols = self.window(step)
         plan, table, slots, size = self.plan, self.table, self.slots, self.size
-        chunk, slot_at = step // PARTS, step % self.ring
+        chunk, slot_at = step // self.parts, step % self.ring
         if pair == 0:
             self.settle(self.near_recv.at[step], self.near_got[step])
         if step >= self.ring:
@@ -538,38 +538,19 @@
 
     def run(self, side=None):
         steps = self.steps
-        for step in range(min(AHEAD, steps)):
+        for step in range(min(self.ahead, steps)):
             self.launch_far(step)
             self.launch_near(step)
-
-        @pl.when(self.inner == 1)
-        def _():
-            for step in range(AHEAD, min(NEAR_AHEAD, steps)):
-                self.launch_near(step)
-
-        for step in range(min(LEAD, steps)):
+        for step in range(min(self.lead, steps)):
             self.serve(step, 0)
         for step in range(steps):
-            if step + AHEAD < steps:
-                self.launch_far(step + AHEAD)
-                if NEAR_AHEAD == AHEAD:
-                    self.launch_near(step + AHEAD)
-                else:
-
-                    @pl.when(self.inner == 0)
-                    def _():
-                        self.launch_near(step + AHEAD)
-
-            if NEAR_AHEAD > AHEAD and step + NEAR_AHEAD < steps:
-
-                @pl.when(self.inner == 1)
-                def _():
-                    self.launch_near(step + NEAR_AHEAD)
-
+            if step + self.ahead < steps:
+                self.launch_far(step + self.ahead)
+                self.launch_near(step + self.ahead)
             self.relay(step)
             self.serve(step, 1)
-            if step + LEAD < steps:
-                self.serve(step + LEAD, 0)
+            if step + self.lead < steps:
+                self.serve(step + self.lead, 0)
             if side is not None:
                 side(step)
         if side is not None:
@@ -614,14 +595,14 @@
     def side(step):
         if step == 0:
             fetch.wait()
-        if step in SUM_AT:
-            summer.step(SUM_AT.index(step))
+        if step in moves.sum_at:
+            summer.step(moves.sum_at.index(step))
 
     moves.run(side)
 
 
-def exchange(n, slots, way, far_cap, near_cap, collective, plan, table, part=None):
-    moves = Exchange(n, slots, way, far_cap, near_cap, table.shape, table.dtype)
+def exchange(n, slots, way, parts, far_cap, near_cap, collective, plan, table, part=None):
+    moves = Exchange(n, slots, way, parts, far_cap, near_cap, table.shape, table.dtype)
     hbm = pl.BlockSpec(memory_space=pl.ANY)
     vmem = pl.BlockSpec(memory_space=pltpu.VMEM)
     in_specs = [pl.BlockSpec(memory_space=pltpu.SMEM), hbm]
@@ -1170,8 +1151,9 @@
     def swap(way, *held):
         def at(rung):
             far_cap, near_cap = rungs[rung]
+            parts = 4 if rung == 0 else 2
             return lambda *held: exchange(
-                n, slots, way, far_cap, near_cap, 2 + way * len(rungs) + rung, *held
+                n, slots, way, parts, far_cap, near_cap, 2 + way * len(rungs) + rung, *held
             )
 
         if len(rungs) == 1:

time: 444 us -> 430 us (0.968); the launches traced: 439 us -> 430 us
  loops' own time: 9.32 us -> 0.29 us
    another operation x2, loops' own time: 9.32 us -> 0.29 us  [swap(): return lax.switch(rung_of[way].reshape(()), branches, plan, *held)]
  transfers between devices with their start and end apart: 1 -> 1, of which waited for: 0 -> 0; matrix products, arithmetic and copies ran while one was open for 0% -> 0% of each run, Pallas kernels for 47% -> 48%
where the time goes in v6:
time: 430 us
  Pallas kernels  418 us (97%)
  other arithmetic  4.85 us (1%)
    pallas_call x1, Pallas kernels, exchange(): pl.pallas_call(functools.partial(exchange_sum_kernel, moves, summer), out...  159 us
    pallas_call x1, Pallas kernels, exchange(): pl.pallas_call(functools.partial(exchange_kernel, moves), out_shape=moves...  140 us
    pallas_call x1, Pallas kernels, dense(): pl.pallas_call(functools.partial(dense_kernel, label_width, pieces, slots...  45.4 us
    pallas_call x1, Pallas kernels, finish(): pl.pallas_call(functools.partial(finish_kernel, n, 1024), out_shape=jax.S...  34.2 us
    pallas_call x1, Pallas kernels, return_sum(): pl.pallas_call(functools.partial(return_sum_kernel, slots, first_row), ou...  22.3 us
    pallas_call x1, Pallas kernels, prelude(): pl.pallas_call(functools.partial(prelude_kernel, n, slots, blocks, rungs,...  17.3 us
  transfers between devices with their start and end apart: 1, of which 0 were waited for; matrix products, arithmetic and copies ran while one was open for 0% of the time, Pallas kernels for 48%

profile of v6, /device:TPU:0, one launch (start us, length us, event | category | flops | bytes accessed | tf_op | source)
XLA Modules:
  0.0 429.5 jit_solution(14754048693473442423)
XLA Ops:
  0.6 17.3 %prelude.1 = (bf16[4096,512]{1,0:T(8,128)(2,1)}, s32[2,16,128]{2,1,0:T(8,128)S(1)}, s32[1,1]{1,0:T(1,128)}, s32[1,1]{1,0:T(1,128)}, s32[8,128]{1,0:T(8,128)}) custom-call(s32[2,32]{1,0:T(2,128)} %bitcast.50, s32[2,32]{1,0:T(2,128)} %bitcast.51, s32[1,32]{1,0:T(1,128)} %refs_2_.1, bf16[602,4096]{1,0:T(8,128)(2,1)} %bitcast.39, f32[602,512]{1,0:T(8,128)} %refs_4_.1), custom_call_target="tpu_custom_call" | custom-call | tf_op jit(solution)/shard_map/prelude/pallas_call | solution.py:926
  18.5 140.1 %conditional.2 = (bf16[8,8,4,2,16,512]{5,4,3,2,1,0:T(8,128)(2,1)}) conditional(s32[]{:T(128)} %bitcast.6, (s32[2,16,128]{2,1,0:T(8,128)S(1)}, bf16[32,128,512]{2,1,0:T(8,128)(2,1)}) %tuple.42, (s32[2,16,128]{2,1,0:T(8,128)S(1)}, bf16[32,128,512]{2,1,0:T(8,128)(2,1)}) %tuple.43, (s32[2,16,128]{2,1,0:T(8,128)S(1)}, ...), branch_computations={%region_0.0_spmd, %region_1.0_spmd, %region_2.0_spmd} | conditional | bytes 8 | solution.py:1162
  18.5 140.0 %exchange.5 = bf16[8,8,4,2,16,512]{5,4,3,2,1,0:T(8,128)(2,1)} custom-call(s32[2,16,128]{2,1,0:T(8,128)S(1)} %get-tuple-element.38.plan, bf16[32,128,512]{2,1,0:T(8,128)(2,1)} %get-tuple-element.39.table), custom_call_target="tpu_custom_call" | custom-call | tf_op jit(solution)/shard_map/cond/branch_2_fun/exchange/pallas_call | solution.py:614
  158.6 3.7 all-to-all-start
  163.5 45.4 %dense.1 = (bf16[4096,512]{1,0:T(8,128)(2,1)}, bf16[4096,512]{1,0:T(8,128)(2,1)}, f32[2176,512]{1,0:T(8,128)}, f32[1,1]{1,0:T(1,128)}) custom-call(s32[1]{0:T(128)S(6)} %copy.42.count, s32[8,128]{1,0:T(8,128)} %get-tuple-element.90.sinks, bf16[4,8,2,128,128]{4,3,2,1,0:T(8,128)(2,1)} %bitcast.10.edges, ...), custom_call_target="tpu_custom_call" | custom-call | tf_op jit(solution)/shard_map/dense/pallas_call | solution.py:1072
  208.9 0.0 copy-start
  208.9 0.0 copy-start.1
  208.9 0.0 copy-start.2
  208.9 0.0 copy-start.3
  209.0 159.1 %conditional.3 = ((bf16[8,8,4,2,16,512]{5,4,3,2,1,0:T(8,128)(2,1)}, bf16[2176,512]{1,0:T(8,128)(2,1)})) conditional(s32[]{:T(128)} %bitcast.9, (s32[2,16,128]{2,1,0:T(8,128)S(1)}, bf16[32,128,512]{2,1,0:T(8,128)(2,1)}, f32[2176,512]{1,0:T(8,128)}) %tuple.45, (s32[2,16,128]{2,1,0:T(8,128)S(1)}, bf16[32,128,512]{2,1,0:T(8,128)(2,1)}, ...), branch_computations={%region_3.0_spmd, %region_4.0_spmd, %region_5.0_spmd} | conditional | bytes 8 | solution.py:1162
  209.0 158.8 %exchange_sum.5 = (bf16[8,8,4,2,16,512]{5,4,3,2,1,0:T(8,128)(2,1)}, bf16[2176,512]{1,0:T(8,128)(2,1)}) custom-call(s32[2,16,128]{2,1,0:T(8,128)S(1)} %get-tuple-element.46.plan, bf16[32,128,512]{2,1,0:T(8,128)(2,1)} %get-tuple-element.47.table, f32[2176,512]{1,0:T(8,128)} %get-tuple-element.48.part), custom_call_target="tpu_custom_call" | custom-call | tf_op jit(solution)/shard_map/cond/branch_2_fun/exchange_sum/pallas_call | solution.py:624
  368.0 0.0 all-to-all-done
  368.0 0.0 copy-done
  368.0 0.0 copy-done.1
  368.0 0.0 copy-done.2
  368.1 0.0 copy-done.3
  368.1 22.3 %return_sum.1 = (bf16[32,128,512]{2,1,0:T(8,128)(2,1)}, f32[1024,512]{1,0:T(8,128)}, f32[1024,512]{1,0:T(8,128)}, f32[1024,512]{1,0:T(8,128)}, f32[1024,512]{1,0...) custom-call(s32[32,128]{1,0:T(8,128)S(1)} %bitcast.48, ...), custom_call_target="tpu_custom_call" | custom-call | tf_op jit(solution)/shard_map/return_sum/pallas_call | solution.py:725
  390.4 0.0 copy-start.4
  390.4 0.0 copy-start.5
  390.4 0.0 copy-start.6
  390.4 34.2 %finish.1 = bf16[640,512]{1,0:T(8,128)(2,1)} custom-call(bf16[602,4096]{1,0:T(8,128)(2,1)} %bitcast.40, bf16[4096,512]{1,0:T(8,128)(2,1)} %bitcast.43, f32[1,1]{1,0:T(1,128)} %get-tuple-element.98.loss), custom_call_target="tpu_custom_call" | custom-call | tf_op jit(solution)/shard_map/finish/pallas_call | solution.py:311
  424.7 1.3 convert_reduce_fusion
  425.9 0.0 copy-done.4
  425.9 3.6 multiply_subtract_fusion
  (2 shorter events, 0.0 us)
Async XLA Ops:
  158.6 209.4 %all-to-all-start = ((bf16[64,128,128]{2,1,0:T(8,128)(2,1)}), bf16[64,128,128]{2,1,0:T(8,128)(2,1)}, u32[]{:S(2)}, u32[]{:S(2)}) async-start(bf16[64,128,128]{2,1,0:T(8,128)(2,1)} %param.33), calls=%async_computation | async-start | bytes 4194304 | tf_op jit(solution)/shard_map/all_to_all | solution.py:1166
  208.9 159.1 %copy-start = (f32[1,2,512,512]{3,2,1,0:T(8,128)S(1)}, f32[1,2,512,512]{3,2,1,0:T(8,128)}, u32[]{:S(2)}) copy-start(f32[1,2,512,512]{3,2,1,0:T(8,128)} %param.35) | copy-start | bytes 6291460
  208.9 159.1 %copy-start.1 = (f32[512,121]{1,0:T(8,128)S(1)}, f32[512,121]{1,0:T(8,128)}, u32[]{:S(2)}) copy-start(f32[512,121]{1,0:T(8,128)} %refs_13_.1) | copy-start | bytes 743428
  208.9 159.1 %copy-start.2 = (f32[512,121]{1,0:T(8,128)S(1)}, f32[512,121]{1,0:T(8,128)}, u32[]{:S(2)}) copy-start(f32[512,121]{1,0:T(8,128)} %refs_15_.1) | copy-start | bytes 743428
  208.9 159.1 %copy-start.3 = (f32[512,121]{1,0:T(8,128)S(1)}, f32[512,121]{1,0:T(8,128)}, u32[]{:S(2)}) copy-start(f32[512,121]{1,0:T(8,128)} %refs_16_.1) | copy-start | bytes 743428
  390.4 35.6 %copy-start.4 = (f32[602,512]{1,0:T(8,128)S(1)}, f32[602,512]{1,0:T(8,128)}, u32[]{:S(2)}) copy-start(f32[602,512]{1,0:T(8,128)} %refs_4_.1) | copy-start | bytes 3698692
  390.4 35.5 %copy-start.5 = (f32[602,512]{1,0:T(8,128)S(1)}, f32[602,512]{1,0:T(8,128)}, u32[]{:S(2)}) copy-start(f32[602,512]{1,0:T(8,128)} %param.38) | copy-start | bytes 3698692
  390.4 35.5 %copy-start.6 = (f32[602,512]{1,0:T(8,128)S(1)}, f32[602,512]{1,0:T(8,128)}, u32[]{:S(2)}) copy-start(f32[602,512]{1,0:T(8,128)} %param.42) | copy-start | bytes 3698692
